TPU v7x, 32 devices: a whole 2x2x4 slice. The times are simulated.
32 devices in a mesh: light: 4 (over x, core), strip: 8 (over z, y).
Axes of the slice: x: 2, y: 2, z: 4, core: 2. Of those that a mesh axis runs over, the one named last changes fastest.
Arguments:
- depth_start: float32 [128, 4096], P(None, 'strip'), may hold values from -0.3 to 0.3
- albedo_start: float32 [128, 4096], P(None, 'strip'), may hold values from 0.5 to 2
- observations: bfloat16 [32, 128, 4096], P('light', None, 'strip'), may hold values from 0 to 26
- light_table: int32 [32, 4], P('light'), may hold values from 0 to 999
- valid_mask: int32 [128, 4096], P(None, 'strip'), may hold values 0 or 1
Outputs:
- depth_final: float32 [128, 4096], P(None, 'strip')
- albedo_final: float32 [128, 4096], P(None, 'strip')
All inputs are finite; a program needn't handle non-finite values. No bound on the sum of `valid_mask` on one device may be relied on, other than what follows from the above.
Results may differ from a plain program's by a relative error of at most 0.0003.
Values may be sent and summed in bfloat16 or wider, within the bound.
No kernel may reach another device: no remote copies, remote signals or barrier semaphores. Data moves between devices by JAX's collectives and lax.ppermute only.
A program may use at most 64 MiB of HBM per device.

v0:
```python
import jax
import jax.numpy as jnp
from jax import lax
from jax.sharding import PartitionSpec as P

ITERS = 2


temper = 0.5
step_depth = 0.1
step_albedo = 0.2
epsilon = 1e-06


def extended(block, sides, width):
    for axis, dim in sides:
        count = lax.axis_size(axis)
        forward = [(i, i + 1) for i in range(count - 1)]
        backward = [(target, source) for source, target in forward]
        low = lax.ppermute(
            lax.slice_in_dim(block, block.shape[dim] - width, None, axis=dim), axis, forward
        )
        high = lax.ppermute(lax.slice_in_dim(block, 0, width, axis=dim), axis, backward)
        block = jnp.concatenate([low, block, high], axis=dim)
    return block


def decode_lights(table):
    values = table.astype(jnp.float32)
    light_x = (values[:, 0] / 500.0 - 1.0)[:, None, None]
    light_y = (values[:, 1] / 500.0 - 1.0)[:, None, None]
    light_z = (1.0 + values[:, 2] / 1000.0)[:, None, None]
    intensity = (0.5 + values[:, 3] / 1000.0)[:, None, None]
    return (light_x, light_y, light_z, intensity)


def shade_terms(surface, col_pad, row_pad, albedo, observed, table, valid, coord_x, coord_y):
    slope_x = 0.5 * (col_pad[:, 2:] - col_pad[:, :-2])
    slope_y = 0.5 * (row_pad[2:] - row_pad[:-2])
    light_x, light_y, light_z, intensity = decode_lights(table)
    delta_x = light_x - coord_x
    delta_y = light_y - coord_y
    delta_z = light_z - surface
    distance_sq = delta_x * delta_x + delta_y * delta_y + delta_z * delta_z
    norm_sq = 1.0 + slope_x * slope_x + slope_y * slope_y
    facing = -slope_x * delta_x - slope_y * delta_y + delta_z
    falloff = intensity / (distance_sq * jnp.sqrt(distance_sq) * jnp.sqrt(norm_sq))
    radiance = albedo * falloff * facing
    residual = valid * (radiance - observed.astype(jnp.float32))
    scores = -temper * residual * residual
    return (
        scores,
        residual,
        falloff,
        facing,
        delta_x,
        delta_y,
        delta_z,
        distance_sq,
        norm_sq,
        slope_x,
        slope_y,
    )


def light_gradients(weights, terms, albedo):
    (
        scores,
        residual,
        falloff,
        facing,
        delta_x,
        delta_y,
        delta_z,
        distance_sq,
        norm_sq,
        slope_x,
        slope_y,
    ) = terms
    lit = weights * residual * falloff
    grad_albedo = jnp.sum(lit * facing, axis=0)
    scaled = lit * albedo
    grad_direct = jnp.sum(scaled * (-1.0 + 3.0 * facing * delta_z / distance_sq), axis=0)
    grad_x = jnp.sum(scaled * (-delta_x - facing * slope_x / norm_sq), axis=0)
    grad_y = jnp.sum(scaled * (-delta_y - facing * slope_y / norm_sq), axis=0)
    return (grad_x, grad_y, grad_direct, grad_albedo)


def depth_stencil(grad_x_pad, grad_y_pad, grad_direct):
    return (
        grad_direct
        + 0.5 * (grad_x_pad[:, :-2] - grad_x_pad[:, 2:])
        + 0.5 * (grad_y_pad[:-2] - grad_y_pad[2:])
    )


def coordinates(nrows, total_rows, strip_cols):
    total_cols = strip_cols * lax.axis_size("strip")
    col_start = lax.axis_index("strip") * strip_cols
    columns = (jnp.arange(strip_cols) + col_start).astype(jnp.float32)
    coord_x = ((columns + 0.5) / total_cols - 0.5)[None, :]
    row_index = jnp.arange(nrows).astype(jnp.float32)
    coord_y = ((row_index + 0.5 - total_rows / 2.0) / total_cols)[:, None]
    return (coord_x, coord_y)


def update(surface, albedo, full_depth, full_albedo, mean_depth, mean_albedo):
    surface = surface - step_depth * jnp.tanh(full_depth / jnp.sqrt(mean_depth + epsilon))
    albedo = albedo - step_albedo * jnp.tanh(full_albedo / jnp.sqrt(mean_albedo + epsilon))
    return (surface, albedo)


def shards(depth_start, albedo_start, observations, light_table, valid_mask):
    strip_cols = depth_start.shape[1]
    total_rows = depth_start.shape[0]
    surface = depth_start
    albedo = albedo_start
    valid = valid_mask.astype(jnp.float32)
    coord_x, coord_y = coordinates(total_rows, total_rows, strip_cols)
    for iteration in range(ITERS):
        col_pad = extended(surface, (("strip", 1),), 1)
        row_pad = jnp.pad(surface, ((1, 1), (0, 0)))
        terms = shade_terms(
            surface, col_pad, row_pad, albedo, observations, light_table, valid, coord_x, coord_y
        )
        scores = terms[0]
        local_high = jnp.max(scores, axis=0)
        highest = lax.pmax(local_high, "light")
        raised = jnp.exp(scores - highest)
        summed = lax.psum(jnp.sum(raised, axis=0), "light")
        weights = raised / summed
        grad_x, grad_y, grad_direct, grad_albedo = light_gradients(weights, terms, albedo)
        grad_x, grad_y, grad_direct, full_albedo = lax.psum(
            (grad_x, grad_y, grad_direct, grad_albedo), "light"
        )
        slope_pad = extended(grad_x, (("strip", 1),), 1)
        full_depth = depth_stencil(slope_pad, jnp.pad(grad_y, ((1, 1), (0, 0))), grad_direct)
        square_depth, square_albedo = lax.psum(
            (jnp.sum(full_depth * full_depth), jnp.sum(full_albedo * full_albedo)), "strip"
        )
        pixel_count = full_depth.size * lax.axis_size("strip")
        surface, albedo = update(
            surface,
            albedo,
            full_depth,
            full_albedo,
            square_depth / pixel_count,
            square_albedo / pixel_count,
        )
    return (surface, albedo)


def solution(mesh):
    in_specs = (
        P(None, "strip"),
        P(None, "strip"),
        P("light", None, "strip"),
        P("light", None),
        P(None, "strip"),
    )
    out_specs = (P(None, "strip"), P(None, "strip"))
    return jax.shard_map(shards, mesh=mesh, in_specs=in_specs, out_specs=out_specs, check_vma=False)
```

profile of v0, /device:TPU:0, one launch (start us, length us, event | category | flops | bytes accessed | tf_op | source)
XLA Modules:
  0.0 334.7 jit_solution(5058168484332134036)
XLA Ops:
  9.6 5.5 %collective-permute-start.1 = (f32[128,1]{1,0:T(8,128)S(1)}, f32[128,1]{1,0:T(8,128)S(1)}, u32[]{:S(2)}, u32[]{:S(2)}) collective-permute-start(f32[128,1]{1,0:T(8,128)S(1)} %get-tuple-element.45), channel_id=1, source_target_pairs={{0,1},{1,2},{2,3},{3,4},{4,5},{5,6},{6,7},{8,9},{9,10},{10,11},{11... | collective-permute-start | bytes 1544 | tf_op jit(solution)/shard_map/ppermute | solution.py:20
  17.1 2.3 fusion.45
  20.2 2.7 fusion.15
  23.0 35.8 %all-reduce.15.cloned.1.call-done = f32[128,512]{1,0:T(8,128)} async-done(((f32[128,512]{1,0:T(8,128)}), f32[128,512]{1,0:T(8,128)}) %all-reduce.15.cloned.1.call-update) | async-done | bytes 262160 | tf_op jit(solution)/shard_map/pmax | solution.py:128
  58.9 2.1 fusion.14
  61.0 32.5 %all-reduce.17.cloned.1.call-done = f32[128,512]{1,0:T(8,128)} async-done(((f32[128,512]{1,0:T(8,128)}), f32[128,512]{1,0:T(8,128)}) %all-reduce.17.cloned.1.call-update) | async-done | bytes 262160 | tf_op jit(solution)/shard_map/psum | solution.py:130
  93.5 5.8 %multiply_reduce_fusion.5 = (f32[128,512]{1,0:T(8,128)}, f32[128,512]{1,0:T(8,128)}, f32[128,512]{1,0:T(8,128)}, f32[128,512]{1,0:T(8,128)}) fusion(f32[128,512]{1,0:T(8,128)} %get-tuple-element.35, f32[128,512]{1,0:T(8,128)} %copy-done.15, f32[8,512]{1,0:T(8,128)S(1)} %get-tuple-element.46, f32[8,128]{1,0:T(8,128)S(1)} %get-tuple-element.55, ...), kind=kLoop, calls=%fused_computation.33 | loop fusion | flops 18612224 | bytes 5566528 | tf_op jit(solution)/shard_map/reduce_sum | solution.py:84
  99.4 36.6 %all-reduce.25.cloned.1.call-done = (f32[128,512]{1,0:T(8,128)}, f32[128,512]{1,0:T(8,128)}, f32[128,512]{1,0:T(8,128)}, f32[128,512]{1,0:T(8,128)}) async-done(((f32[128,512]{1,0:T(8,128)}, f32[128,512]{1,0:T(8,128)}, f32[128,512]{1,0:T(8,128)}, f32[128,512]{1,0:T(8,128)}), (f32[128,512]{1,0:T(8,128)}, f32[128,512]{1,0:T(8,128)}, f32[128,512]{1,0:T(8,128)}, ...) | async-done | bytes 1048592 | tf_op jit(solution)/shard_map/psum | solution.py:133
  136.9 3.4 %collective-permute-start.2 = (f32[128,1]{1,0:T(8,128)S(1)}, f32[128,1]{1,0:T(8,128)S(1)}, u32[]{:S(2)}, u32[]{:S(2)}) collective-permute-start(f32[128,1]{1,0:T(8,128)S(1)} %get-tuple-element.42), channel_id=1, source_target_pairs={{0,1},{1,2},{2,3},{3,4},{4,5},{5,6},{6,7},{8,9},{9,10},{10,11},{11... | collective-permute-start | bytes 1544 | tf_op jit(solution)/shard_map/ppermute | solution.py:20
  143.2 3.2 collective-permute-done.3
  146.5 2.1 multiply_reduce_fusion.9
  148.6 20.2 %all-reduce.5 = (f32[]{:T(128)}, f32[]{:T(128)}) all-reduce(f32[]{:T(128)} %get-tuple-element.30, f32[]{:T(128)} %multiply_reduce_fusion.8), channel_id=1, replica_groups=mesh['light'=4,'strip'=8] {'strip'}, use_global_device_ids=true, to_apply=%region_11.12 | all-reduce | flops 2 | bytes 16 | tf_op jit(solution)/shard_map/psum | solution.py:138
  171.6 4.5 %collective-permute-start.5 = (f32[128,1]{1,0:T(8,128)S(1)}, f32[128,1]{1,0:T(8,128)S(1)}, u32[]{:S(2)}, u32[]{:S(2)}) collective-permute-start(f32[128,1]{1,0:T(8,128)S(1)} %get-tuple-element.41), channel_id=1, source_target_pairs={{0,1},{1,2},{2,3},{3,4},{4,5},{5,6},{6,7},{8,9},{9,10},{10,11},{11... | collective-permute-start | bytes 1544 | tf_op jit(solution)/shard_map/ppermute | solution.py:20
  179.7 4.0 %fusion.17 = (f32[128,512]{1,0:T(8,128)}, f32[8,128,512]{2,1,0:T(8,128)S(1)}) fusion(bf16[8,128,512]{2,1,0:T(8,128)(2,1)} %param.7, f32[8,128]{1,0:T(8,128)S(1)} %get-tuple-element.55, f32[128,512]{1,0:T(8,128)S(1)} %get-tuple-element.29, f32[8,512]{1,0:T(8,128)S(1)} %get-tuple-element.48, f32[128,512]{1,0:T(8,128)S(1)} %neg.27, ...), kind=kLoop, calls=%fused_computation.41 | loop fusion | flops 9895936 | bytes 5021760 | tf_op jit(solution)/shard_map/reduce_max | solution.py:127
  183.7 31.2 %all-reduce.19.cloned.1.call-done = f32[128,512]{1,0:T(8,128)} async-done(((f32[128,512]{1,0:T(8,128)}), f32[128,512]{1,0:T(8,128)}) %all-reduce.19.cloned.1.call-update) | async-done | bytes 262160 | tf_op jit(solution)/shard_map/pmax | solution.py:128
  214.9 2.1 fusion.16
  217.1 32.4 %all-reduce.21.cloned.1.call-done = f32[128,512]{1,0:T(8,128)} async-done(((f32[128,512]{1,0:T(8,128)}), f32[128,512]{1,0:T(8,128)}) %all-reduce.21.cloned.1.call-update) | async-done | bytes 262160 | tf_op jit(solution)/shard_map/psum | solution.py:130
  249.5 5.7 %multiply_reduce_fusion.2 = (f32[128,512]{1,0:T(8,128)}, f32[128,512]{1,0:T(8,128)}, f32[128,512]{1,0:T(8,128)}, f32[128,512]{1,0:T(8,128)}) fusion(f32[128,512]{1,0:T(8,128)} %get-tuple-element.27, f32[128,512]{1,0:T(8,128)} %copy-done.14, f32[128,512]{1,0:T(8,128)S(1)} %copy-done.9, f32[128,512]{1,0:T(8,128)S(1)} %neg.27, ...), kind=kLoop, calls=%fused_computation.28 | loop fusion | flops 18612224 | bytes 5566528 | tf_op jit(solution)/shard_map/reduce_sum | solution.py:84
  255.2 36.6 %all-reduce.23.cloned.1.call-done = (f32[128,512]{1,0:T(8,128)}, f32[128,512]{1,0:T(8,128)}, f32[128,512]{1,0:T(8,128)}, f32[128,512]{1,0:T(8,128)}) async-done(((f32[128,512]{1,0:T(8,128)}, f32[128,512]{1,0:T(8,128)}, f32[128,512]{1,0:T(8,128)}, f32[128,512]{1,0:T(8,128)}), (f32[128,512]{1,0:T(8,128)}, f32[128,512]{1,0:T(8,128)}, f32[128,512]{1,0:T(8,128)}, ...) | async-done | bytes 1048592 | tf_op jit(solution)/shard_map/psum | solution.py:133
  292.8 3.4 %collective-permute-start.6 = (f32[128,1]{1,0:T(8,128)S(1)}, f32[128,1]{1,0:T(8,128)S(1)}, u32[]{:S(2)}, u32[]{:S(2)}) collective-permute-start(f32[128,1]{1,0:T(8,128)S(1)} %get-tuple-element.38), channel_id=1, source_target_pairs={{0,1},{1,2},{2,3},{3,4},{4,5},{5,6},{6,7},{8,9},{9,10},{10,11},{11... | collective-permute-start | bytes 1544 | tf_op jit(solution)/shard_map/ppermute | solution.py:20
  299.1 3.2 collective-permute-done.7
  302.3 2.1 multiply_reduce_fusion.7
  304.4 20.2 %all-reduce.4 = (f32[]{:T(128)}, f32[]{:T(128)}) all-reduce(f32[]{:T(128)} %get-tuple-element.22, f32[]{:T(128)} %multiply_reduce_fusion.6), channel_id=1, replica_groups=mesh['light'=4,'strip'=8] {'strip'}, use_global_device_ids=true, to_apply=%region_27.28 | all-reduce | flops 2 | bytes 16 | tf_op jit(solution)/shard_map/psum | solution.py:138
  326.0 1.8 multiply_subtract_fusion
  (74 shorter events, 18.1 us)
Async XLA Ops:
  7.2 13.0 %copy-start = (f32[128,512]{1,0:T(8,128)S(1)}, f32[128,512]{1,0:T(8,128)}, u32[]{:S(2)}) copy-start(f32[128,512]{1,0:T(8,128)} %param.5) | copy-start | bytes 786436
  7.2 13.0 %copy-start.1 = (bf16[8,128,512]{2,1,0:T(8,128)(2,1)S(1)}, bf16[8,128,512]{2,1,0:T(8,128)(2,1)}, u32[]{:S(2)}) copy-start(bf16[8,128,512]{2,1,0:T(8,128)(2,1)} %param.7) | copy-start | bytes 3145732
  7.2 51.7 %all-reduce.15.cloned.1.call-start = ((), (), s32[]{:S(2)}) async-start(), calls=%async_computation | async-start | bytes 524288 | tf_op jit(solution)/shard_map/pmax | solution.py:128
  8.3 8.7 %collective-permute-start = (f32[128,1]{1,0:T(8,128)S(1)}, f32[128,1]{1,0:T(8,128)S(1)}, u32[]{:S(2)}, u32[]{:S(2)}) collective-permute-start(f32[128,1]{1,0:T(8,128)S(1)} %get-tuple-element.44), channel_id=1, source_target_pairs={{1,0},{2,1},{3,2},{4,3},{5,4},{6,5},{7,6},{9,8},{10,9},{11,10},{12... | collective-permute-start | bytes 1544 | tf_op jit(solution)/shard_map/ppermute | solution.py:23
  9.6 7.6 %collective-permute-start.1 = (f32[128,1]{1,0:T(8,128)S(1)}, f32[128,1]{1,0:T(8,128)S(1)}, u32[]{:S(2)}, u32[]{:S(2)}) collective-permute-start(f32[128,1]{1,0:T(8,128)S(1)} %get-tuple-element.45), channel_id=1, source_target_pairs={{0,1},{1,2},{2,3},{3,4},{4,5},{5,6},{6,7},{8,9},{9,10},{10,11},{11... | collective-permute-start | bytes 1544 | tf_op jit(solution)/shard_map/ppermute | solution.py:20
  17.0 5.9 %copy-start.2 = (f32[128,512]{1,0:T(8,128)}, f32[128,512]{1,0:T(8,128)S(1)}, u32[]{:S(2)}) copy-start(f32[128,512]{1,0:T(8,128)S(1)} %convert_element_type.30) | copy-start | bytes 786436
  22.9 70.6 %copy-start.7 = (f32[128,512]{1,0:T(8,128)S(1)}, f32[128,512]{1,0:T(8,128)}, u32[]{:S(2)}) copy-start(f32[128,512]{1,0:T(8,128)} %param.6) | copy-start | bytes 786436
  22.9 70.6 %copy-start.5 = (f32[128,512]{1,0:T(8,128)S(1)}, f32[128,512]{1,0:T(8,128)}, u32[]{:S(2)}) copy-start(f32[128,512]{1,0:T(8,128)} %copy-done.4) | copy-start | bytes 786436
  22.9 70.6 %copy-start.11 = (f32[128,512]{1,0:T(8,128)S(1)}, f32[128,512]{1,0:T(8,128)}, u32[]{:S(2)}) copy-start(f32[128,512]{1,0:T(8,128)} %copy-done.10) | copy-start | bytes 786436
  23.0 70.5 %copy-start.13 = (f32[128,512]{1,0:T(8,128)S(1)}, f32[128,512]{1,0:T(8,128)}, u32[]{:S(2)}) copy-start(f32[128,512]{1,0:T(8,128)} %copy-done.12) | copy-start | bytes 786436
  23.0 70.5 %all-reduce.17.cloned.1.call-start = ((), (), s32[]{:S(2)}) async-start(), calls=%async_computation.1 | async-start | bytes 524288 | tf_op jit(solution)/shard_map/psum | solution.py:130
  61.0 75.0 %all-reduce.25.cloned.1.call-start = ((), (), s32[]{:S(2)}) async-start(), calls=%async_computation.5 | async-start | bytes 2097152 | tf_op jit(solution)/shard_map/psum | solution.py:133
  99.3 115.6 %all-reduce.19.cloned.1.call-start = ((), (), s32[]{:S(2)}) async-start(), calls=%async_computation.2 | async-start | bytes 524288 | tf_op jit(solution)/shard_map/pmax | solution.py:128
  135.9 40.2 %copy-start.16 = (f32[128,512]{1,0:T(8,128)S(1)}, f32[128,512]{1,0:T(8,128)}, u32[]{:S(2)}) copy-start(f32[128,512]{1,0:T(8,128)} %get-tuple-element.21) | copy-start | bytes 786436
  136.9 6.3 %collective-permute-start.2 = (f32[128,1]{1,0:T(8,128)S(1)}, f32[128,1]{1,0:T(8,128)S(1)}, u32[]{:S(2)}, u32[]{:S(2)}) collective-permute-start(f32[128,1]{1,0:T(8,128)S(1)} %get-tuple-element.42), channel_id=1, source_target_pairs={{0,1},{1,2},{2,3},{3,4},{4,5},{5,6},{6,7},{8,9},{9,10},{10,11},{11... | collective-permute-start | bytes 1544 | tf_op jit(solution)/shard_map/ppermute | solution.py:20
  140.3 6.2 %collective-permute-start.3 = (f32[128,1]{1,0:T(8,128)S(1)}, f32[128,1]{1,0:T(8,128)S(1)}, u32[]{:S(2)}, u32[]{:S(2)}) collective-permute-start(f32[128,1]{1,0:T(8,128)S(1)} %get-tuple-element.43), channel_id=1, source_target_pairs={{1,0},{2,1},{3,2},{4,3},{5,4},{6,5},{7,6},{9,8},{10,9},{11,10},{12... | collective-permute-start | bytes 1544 | tf_op jit(solution)/shard_map/ppermute | solution.py:23
  148.6 31.1 %copy-start.3 = (f32[128,512]{1,0:T(8,128)S(1)}, f32[128,512]{1,0:T(8,128)}, u32[]{:S(2)}) copy-start(f32[128,512]{1,0:T(8,128)} %copy-done.2) | copy-start | bytes 786436
  170.3 6.2 %collective-permute-start.4 = (f32[128,1]{1,0:T(8,128)S(1)}, f32[128,1]{1,0:T(8,128)S(1)}, u32[]{:S(2)}, u32[]{:S(2)}) collective-permute-start(f32[128,1]{1,0:T(8,128)S(1)} %get-tuple-element.40), channel_id=1, source_target_pairs={{1,0},{2,1},{3,2},{4,3},{5,4},{6,5},{7,6},{9,8},{10,9},{11,10},{12... | collective-permute-start | bytes 1544 | tf_op jit(solution)/shard_map/ppermute | solution.py:23
  171.6 6.4 %collective-permute-start.5 = (f32[128,1]{1,0:T(8,128)S(1)}, f32[128,1]{1,0:T(8,128)S(1)}, u32[]{:S(2)}, u32[]{:S(2)}) collective-permute-start(f32[128,1]{1,0:T(8,128)S(1)} %get-tuple-element.41), channel_id=1, source_target_pairs={{0,1},{1,2},{2,3},{3,4},{4,5},{5,6},{6,7},{8,9},{9,10},{10,11},{11... | collective-permute-start | bytes 1544 | tf_op jit(solution)/shard_map/ppermute | solution.py:20
  183.7 65.8 %copy-start.9 = (f32[128,512]{1,0:T(8,128)S(1)}, f32[128,512]{1,0:T(8,128)}, u32[]{:S(2)}) copy-start(f32[128,512]{1,0:T(8,128)} %copy-done.8) | copy-start | bytes 786436
  183.7 65.8 %all-reduce.21.cloned.1.call-start = ((), (), s32[]{:S(2)}) async-start(), calls=%async_computation.3 | async-start | bytes 524288 | tf_op jit(solution)/shard_map/psum | solution.py:130
  217.0 74.8 %all-reduce.23.cloned.1.call-start = ((), (), s32[]{:S(2)}) async-start(), calls=%async_computation.4 | async-start | bytes 2097152 | tf_op jit(solution)/shard_map/psum | solution.py:133
  292.8 6.3 %collective-permute-start.6 = (f32[128,1]{1,0:T(8,128)S(1)}, f32[128,1]{1,0:T(8,128)S(1)}, u32[]{:S(2)}, u32[]{:S(2)}) collective-permute-start(f32[128,1]{1,0:T(8,128)S(1)} %get-tuple-element.38), channel_id=1, source_target_pairs={{0,1},{1,2},{2,3},{3,4},{4,5},{5,6},{6,7},{8,9},{9,10},{10,11},{11... | collective-permute-start | bytes 1544 | tf_op jit(solution)/shard_map/ppermute | solution.py:20
  296.2 6.2 %collective-permute-start.7 = (f32[128,1]{1,0:T(8,128)S(1)}, f32[128,1]{1,0:T(8,128)S(1)}, u32[]{:S(2)}, u32[]{:S(2)}) collective-permute-start(f32[128,1]{1,0:T(8,128)S(1)} %get-tuple-element.39), channel_id=1, source_target_pairs={{1,0},{2,1},{3,2},{4,3},{5,4},{6,5},{7,6},{9,8},{10,9},{11,10},{12... | collective-permute-start | bytes 1544 | tf_op jit(solution)/shard_map/ppermute | solution.py:23
  (7 other events, 21.4 us)
Sparse Core Ops, SparseCore 0:
  23.1 35.6 all-reduce.14
  61.2 32.2 all-reduce.16
  99.4 36.4 all-reduce.24
  183.8 31.0 all-reduce.18
  217.1 32.2 all-reduce.20
  255.3 36.4 all-reduce.22
where the time goes:
time: 336 us; the launch traced here: 335 us
  waiting for transfers between devices  214 us (64%)
  blocking collectives  40.4 us (12%)
  other arithmetic  37 us (11%)
  starting transfers between devices  22.2 us (7%)
  between operations  17.1 us (5%)
  local copies, waits for them, and re-layouts  4.48 us (1%)
    psum x2, waiting for transfers between devices, shards(): lax.psum((grad_x, grad_y, grad_direct, grad_albedo), 'light')  73.2 us
    pmax x2, waiting for transfers between devices, shards(): highest = lax.pmax(local_high, 'light')  67 us
    psum x2, waiting for transfers between devices, shards(): summed = lax.psum(jnp.sum(raised, axis=0), 'light')  64.9 us
    psum x2, blocking collectives, shards(): lax.psum((jnp.sum(full_depth * full_depth), jnp.sum(full_albedo * full_al...  40.4 us
    ppermute x4, starting transfers between devices, extended(): lax.ppermute(lax.slice_in_dim(block, block.shape[dim] - width, None, axis...  16.8 us
    reduce_sum x2, other arithmetic, light_gradients(): grad_x = jnp.sum(scaled * (-delta_x - facing * slope_x / norm_sq), axis=0)  11.5 us
  transfers between devices with their start and end apart: 14, of which 11 were waited for; matrix products, arithmetic and copies ran while one was open for 2% of the time, Pallas kernels for 0%

commit v1 on v0

v1 whole, which is shorter than its diff:
```python
import functools
import math

import jax
import jax.numpy as jnp
from jax import lax
from jax.experimental import pallas as pl
from jax.experimental.pallas import tpu as pltpu
from jax.sharding import PartitionSpec as P

AXES = ("light", "strip")
STEP_DEPTH = 0.1
STEP_ALBEDO = 0.2
EPS = 1e-06
HALF_LOG2E = 0.5 * math.log2(math.e)
F32 = jnp.float32
VM = pl.BlockSpec(memory_space=pltpu.VMEM)
TR = 16


def iota(shape, dim):
    return lax.broadcasted_iota(jnp.int32, shape, dim)


def position():
    nl, ns = lax.axis_size("light"), lax.axis_size("strip")
    li, si = lax.axis_index("light"), lax.axis_index("strip")
    return li, si, si * nl + li, nl * ns


def exchange_index(place):
    nl, ns = lax.axis_size("light"), lax.axis_size("strip")
    return lax.rem(place, nl) * ns + lax.div(place, nl)


def call(body, out, scratch=(), name=None, aliases=None, cost=None):
    return pl.pallas_call(
        body,
        out_shape=out,
        scratch_shapes=list(scratch),
        name=name,
        input_output_aliases=aliases or {},
        compiler_params=pltpu.CompilerParams(vmem_limit_bytes=40 << 20),
        cost_estimate=cost,
    )


def edges_body(nl, obs_ref, depth_ref, albedo_ref, valid_ref, fwd_ref, bwd_ref, eh_ref, sr_ref):
    lights, rows, cols = obs_ref.shape
    w = cols // nl

    def picks(columns):
        pad = -len(columns) % 8
        row = iota((len(columns) + pad, cols), 0)
        col = iota((len(columns) + pad, cols), 1)
        hit = jnp.zeros(row.shape, jnp.bool_)
        for index, column in enumerate(columns):
            hit = hit | ((row == index) & (col == column))
        return hit.astype(F32)

    ends = []
    for q in range(nl):
        ends += [q * w, q * w + w - 1]
    pairs = []
    for q in range(nl):
        pairs += [q * w, q * w + 1, q * w + w - 2, q * w + w - 1]
    contract = (((1,), (1,)), ((), ()))
    pick_ends = picks(ends)
    pick_pairs = picks(pairs)
    exact = lax.Precision.HIGHEST
    depth = lax.dot_general(pick_pairs, depth_ref[...], contract, precision=exact, preferred_element_type=F32)
    albedo = lax.dot_general(pick_ends, albedo_ref[...], contract, precision=exact, preferred_element_type=F32)
    valid = lax.dot_general(
        pick_ends, valid_ref[...].astype(F32), contract, precision=exact, preferred_element_type=F32
    )
    zero = jnp.zeros((1, rows), F32)
    fwd_ref[...] = jnp.zeros_like(fwd_ref)
    bwd_ref[...] = jnp.zeros_like(bwd_ref)
    eh_ref[...] = jnp.zeros_like(eh_ref)
    sr_ref[...] = jnp.zeros_like(sr_ref)
    pick16 = pick_ends.astype(jnp.bfloat16)
    for l in range(lights):
        e = lax.dot_general(pick16, obs_ref[l], contract, preferred_element_type=F32)
        bwd_ref[l : l + 1, :] = e[0:1]
        fwd_ref[l : l + 1, :] = e[2 * nl - 1 : 2 * nl]
        for q in range(nl):
            if q > 0:
                eh_ref[q, l : l + 1, :] = e[2 * q - 1 : 2 * q]
            if q < nl - 1:
                eh_ref[q, lights + l : lights + l + 1, :] = e[2 * q + 2 : 2 * q + 3]
    n = lights
    last = 4 * (nl - 1)
    fwd_ref[n : n + 2, :] = depth[last + 2 : last + 4]
    fwd_ref[n + 2 : n + 3, :] = albedo[2 * nl - 1 : 2 * nl]
    fwd_ref[n + 3 : n + 4, :] = valid[2 * nl - 1 : 2 * nl]
    bwd_ref[n : n + 2, :] = depth[0:2]
    bwd_ref[n + 2 : n + 3, :] = albedo[0:1]
    bwd_ref[n + 3 : n + 4, :] = valid[0:1]
    for q in range(nl):
        sr_ref[q, 2:3, :] = depth[4 * q : 4 * q + 1]
        sr_ref[q, 3:4, :] = depth[4 * q + 3 : 4 * q + 4]
        if q > 0:
            sr_ref[q, 0:2, :] = depth[4 * q - 2 : 4 * q]
            sr_ref[q, 6:7, :] = albedo[2 * q - 1 : 2 * q]
            sr_ref[q, 8:9, :] = valid[2 * q - 1 : 2 * q]
        if q < nl - 1:
            sr_ref[q, 4:6, :] = depth[4 * q + 4 : 4 * q + 6]
            sr_ref[q, 7:8, :] = albedo[2 * q + 2 : 2 * q + 3]
            sr_ref[q, 9:10, :] = valid[2 * q + 2 : 2 * q + 3]


def halos_body(nl, eh_ref, sr_ref, low_ref, high_ref, table_ref, *outs):
    small_refs, own_ref = outs[:nl], outs[nl]
    li = lax.axis_index("light")
    n = table_ref.shape[0]
    table = table_ref[...].astype(F32)
    for k in range(nl):
        q = li ^ k
        ref = small_refs[k]
        ref[0 : 2 * n, :] = eh_ref[q]
        ref[2 * n :, :] = jnp.zeros((ref.shape[0] - 2 * n, ref.shape[1]), F32)
        ref[2 * n : 3 * n, 0:4] = table

        @pl.when(q == 0)
        def _():
            ref[0:n, :] = low_ref[0:n, :]

        @pl.when(q == nl - 1)
        def _():
            ref[n : 2 * n, :] = high_ref[0:n, :]

    own_ref[...] = sr_ref[li]

    @pl.when(li == 0)
    def _():
        own_ref[0:2, :] = low_ref[n : n + 2, :]
        own_ref[6:7, :] = low_ref[n + 2 : n + 3, :]
        own_ref[8:9, :] = low_ref[n + 3 : n + 4, :]

    @pl.when(li == nl - 1)
    def _():
        own_ref[4:6, :] = high_ref[n : n + 2, :]
        own_ref[7:8, :] = high_ref[n + 2 : n + 3, :]
        own_ref[9:10, :] = high_ref[n + 3 : n + 4, :]


def decode(table):
    return (
        table[:, 0:1] / 500.0 - 1.0,
        table[:, 1:2] / 500.0 - 1.0,
        1.0 + table[:, 2:3] / 1000.0,
        0.5 + table[:, 3:4] / 1000.0,
    )


def columns_from(left, right, shape):
    rows, w = shape
    at = iota((w, rows), 0)
    return jnp.transpose(jnp.where(at == 0, left, jnp.where(at == w - 1, right, 0.0)))


def shifts_rows(x):
    r = iota(x.shape, 0)
    n = x.shape[0]
    above = jnp.where(r == 0, 0.0, pltpu.roll(x, 1, 0))
    below = jnp.where(r == n - 1, 0.0, pltpu.roll(x, n - 1, 0))
    return above, below


def shifts_cols(x, ends):
    c = iota(x.shape, 1)
    n = x.shape[1]
    before = jnp.where(c == 0, ends, pltpu.roll(x, 1, 1))
    after = jnp.where(c == n - 1, ends, pltpu.roll(x, n - 1, 1))
    return before, after


def fill_context(ctx_ref, surface, albedo, left, right):
    ends = columns_from(left, right, surface.shape)
    before, after = shifts_cols(surface, ends)
    above, below = shifts_rows(surface)
    sx = 0.5 * (after - before)
    sy = 0.5 * (below - above)
    ctx_ref[0] = surface
    ctx_ref[1] = sx
    ctx_ref[2] = sy
    ctx_ref[3] = albedo * lax.rsqrt(1.0 + sx * sx + sy * sy)


def fill_params(pb_ref, base, small_ref, w, place, total):
    n = small_ref.shape[0] // 3
    lx, ly, lz, le = decode(small_ref[2 * n : 3 * n, :])
    col = iota((8, w), 1) + place * w
    px = (col.astype(F32) + 0.5) / total - 0.5
    for j in range(n):
        dx = jnp.broadcast_to(lx[j : j + 1], (8, w)) - px
        pb_ref[base + j, 0] = dx
        pb_ref[base + j, 1] = dx * dx
        pb_ref[base + j, 2] = jnp.broadcast_to(ly[j : j + 1], (8, w))
        pb_ref[base + j, 3] = jnp.broadcast_to(lz[j : j + 1], (8, w))
        pb_ref[base + j, 4] = jnp.broadcast_to(le[j : j + 1], (8, w))


def accumulate(state, tile, py, obs, pb_ref, base):
    surface, sx, sy, scaled = tile
    kept = []
    least = None
    for j in range(len(obs)):
        dx, dx2 = pb_ref[base + j, 0], pb_ref[base + j, 1]
        dy = pb_ref[base + j, 2] - py
        dz = pb_ref[base + j, 3] - surface
        dist = (dx2 + dy * dy) + dz * dz
        facing = dz - (sx * dx + sy * dy)
        r = lax.rsqrt(dist)
        r2 = r * r
        g = (r2 * r) * pb_ref[base + j, 4]
        residual = scaled * (g * facing) - obs[j]
        square = residual * residual
        least = square if least is None else jnp.minimum(least, square)
        kept.append((square, residual * g, facing, dz * r2, dx, dy))
    if state is not None:
        before = state[0]
        least = jnp.minimum(least, before)
    sums = None
    for square, q, facing, drop, dx, dy in kept:
        w = jnp.exp2((least - square) * HALF_LOG2E)
        p = w * q
        pf = p * facing
        terms = (w, p, p * dx, p * dy, pf, pf * drop)
        sums = terms if sums is None else tuple(a + b for a, b in zip(sums, terms))
    if state is not None:
        fade = jnp.exp2((least - before) * HALF_LOG2E)
        sums = tuple(a * fade + b for a, b in zip(state[1:], sums))
    return (least,) + sums


def sweep(ctx_ref, pb_ref, obs_refs, bases, total, load, store):
    rows, w = ctx_ref.shape[1:]
    split = (TR // 8, 8, w)

    def step(i, carry):
        at = pl.ds(pl.multiple_of(i * TR, TR), TR)
        tile = tuple(ctx_ref[f, at, :].reshape(split) for f in range(4))
        row = iota(split, 0) * 8 + iota(split, 1) + i * TR
        py = (row.astype(F32) + (0.5 - rows / 2.0)) / total
        state = load(at)
        for obs_ref, base in zip(obs_refs, bases):
            obs = [obs_ref[j, at, :].astype(F32).reshape(split) for j in range(obs_ref.shape[0])]
            state = accumulate(state, tile, py, obs, pb_ref, base)
        store(at, state)
        return carry

    lax.fori_loop(0, rows // TR, step, 0)


def state_load(state_ref, w):
    return lambda at: tuple(state_ref[f, at, :].reshape(TR // 8, 8, w) for f in range(7))


def state_store(state_ref, w):
    def store(at, state):
        for f in range(7):
            state_ref[f, at, :] = state[f].reshape(TR, w)

    return store


def halo_slope(column, side, small_refs, srow_ref, rows, total):
    n = small_refs[0].shape[0] // 3
    obs = jnp.concatenate([ref[side * n : (side + 1) * n, :] for ref in small_refs], axis=0)
    table = jnp.concatenate([ref[2 * n : 3 * n, :] for ref in small_refs], axis=0)
    lx, ly, lz, le = decode(table)
    outer, inner = (0, 2) if side == 0 else (5, 3)
    here = 1 if side == 0 else 4
    surface = srow_ref[here : here + 1, :]
    toward = srow_ref[inner : inner + 1, :] - srow_ref[outer : outer + 1, :]
    sx = 0.5 * toward if side == 0 else -0.5 * toward
    lane = iota((8, rows), 1)
    wide = jnp.broadcast_to(surface, (8, rows))
    above = jnp.where(lane == 0, 0.0, pltpu.roll(wide, 1, 1))
    below = jnp.where(lane == rows - 1, 0.0, pltpu.roll(wide, rows - 1, 1))
    sy = (0.5 * (below - above))[0:1]
    albedo = srow_ref[6 + side : 7 + side, :]
    valid = srow_ref[8 + side : 9 + side, :]
    px = (column.astype(F32) + 0.5) / total - 0.5
    py = (iota((1, rows), 1).astype(F32) + (0.5 - rows / 2.0)) / total
    rn = lax.rsqrt(1.0 + sx * sx + sy * sy)
    dx = jnp.broadcast_to(lx - px, obs.shape)
    dy = ly - py
    dz = lz - surface
    dist = dx * dx + dy * dy + dz * dz
    facing = dz - (sx * dx + sy * dy)
    r = lax.rsqrt(dist)
    g = (r * r) * r * le
    residual = (albedo * rn) * (g * facing) - obs
    square = residual * residual
    least = jnp.min(square, axis=0, keepdims=True)
    w = jnp.exp2((least - square) * HALF_LOG2E)
    p = w * residual * g
    total_w = jnp.sum(w, axis=0, keepdims=True)
    px_sum = jnp.sum(p * dx, axis=0, keepdims=True)
    pf_sum = jnp.sum(p * facing, axis=0, keepdims=True)
    return -(valid * albedo * rn / total_w) * (px_sum + (sx * rn * rn) * pf_sum)


def gradients(state_ref, ctx_ref, albedo, valid, slope_low, slope_high):
    sx, sy = ctx_ref[1], ctx_ref[2]
    rn = lax.rsqrt(1.0 + sx * sx + sy * sy)
    inverse = valid * rn / state_ref[1]
    factor = inverse * albedo
    pf = state_ref[5]
    rn2pf = rn * rn * pf
    grad_albedo = inverse * pf
    direct = factor * (3.0 * state_ref[6] - state_ref[2])
    grad_x = -factor * (state_ref[3] + sx * rn2pf)
    grad_y = -factor * (state_ref[4] + sy * rn2pf)
    before, after = shifts_cols(grad_x, columns_from(slope_low, slope_high, grad_x.shape))
    above, below = shifts_rows(grad_y)
    return direct + 0.5 * (before - after) + 0.5 * (above - below), grad_albedo


def partial_sums(depth, albedo):
    n = depth.shape[1]
    d = jnp.sum(depth * depth, axis=0, keepdims=True)
    a = jnp.sum(albedo * albedo, axis=0, keepdims=True)
    d = jnp.broadcast_to(d, (8, n))
    a = jnp.broadcast_to(a, (8, n))
    d = d + pltpu.roll(d, n // 2, 1)
    a = a + pltpu.roll(a, n // 2, 1)
    return jnp.where(iota((8, n), 1) < n // 2, d, a)[0:1]


def inverse_scales(recv_ref, row, count):
    rows = recv_ref[:, row, :]
    n = rows.shape[1]
    lane = iota(rows.shape, 1)
    d = jnp.sum(jnp.where(lane < n // 2, rows, 0.0), keepdims=True)
    a = jnp.sum(jnp.where(lane < n // 2, 0.0, rows), keepdims=True)
    return lax.rsqrt(d / count + EPS), lax.rsqrt(a / count + EPS)


def first_body(nl, depth_ref, albedo_ref, valid_ref, srow_ref, small0, small1, obs0, obs1, ctx_ref, mask_ref, state_ref, pb_ref):
    li, si, place, count = position()
    rows, w = ctx_ref.shape[1:]
    at = pl.ds(pl.multiple_of(li * w, w), w)
    albedo = albedo_ref[:, at]
    mask_ref[0] = albedo
    mask_ref[1] = valid_ref[:, at].astype(F32)
    fill_context(ctx_ref, depth_ref[:, at], albedo, srow_ref[1:2, :], srow_ref[4:5, :])
    total = w * count
    n = obs0.shape[0]
    fill_params(pb_ref, 0, small0, w, place, total)
    fill_params(pb_ref, n, small1, w, place, total)
    sweep(ctx_ref, pb_ref, (obs0, obs1), (0, n), total, lambda at: None, state_store(state_ref, w))


def more_body(ctx_ref, in_ref, small, obs, state_ref, pb_ref):
    li, si, place, count = position()
    rows, w = ctx_ref.shape[1:]
    total = w * count
    fill_params(pb_ref, 0, small, w, place, total)
    sweep(ctx_ref, pb_ref, (obs,), (0,), total, state_load(in_ref, w), state_store(state_ref, w))


def finish(state_ref, ctx_ref, albedo, valid, small_refs, srow_ref, grad_ref, edge_ref, pay_ref):
    li, si, place, count = position()
    rows, w = ctx_ref.shape[1:]
    total = w * count
    low = halo_slope(place * w - 1, 0, small_refs, srow_ref, rows, total)
    high = halo_slope(place * w + w, 1, small_refs, srow_ref, rows, total)
    depth, grad_albedo = gradients(state_ref, ctx_ref, albedo, valid, low, high)
    sums = partial_sums(depth, grad_albedo)
    if edge_ref is None:
        pay_ref[...] = jnp.broadcast_to(sums[None], pay_ref.shape)
        return depth, grad_albedo
    grad_ref[0] = depth
    grad_ref[1] = grad_albedo
    dt = jnp.transpose(depth)
    at = jnp.transpose(grad_albedo)
    edge_ref[0:1, :] = dt[0:1]
    edge_ref[1:2, :] = dt[w - 1 : w]
    pay_ref[:, 0:2, :] = jnp.broadcast_to(dt[0:2][None], (count, 2, rows))
    pay_ref[:, 2:3, :] = jnp.broadcast_to(at[0:1][None], (count, 1, rows))
    pay_ref[:, 3:4, :] = jnp.broadcast_to(sums[None], (count, 1, w))

    @pl.when(place < count - 1)
    def _():
        to = exchange_index(place + 1)
        pay_ref[to, 0:2, :] = dt[w - 2 : w]
        pay_ref[to, 2:3, :] = at[w - 1 : w]

    return depth, grad_albedo


def last_body(nl, ctx_ref, mask_ref, in_ref, srow_ref, *rest):
    small_refs, (obs, grad_ref, edge_ref, pay_ref, pb_ref, state_ref) = rest[:nl], rest[nl:]
    li, si, place, count = position()
    rows, w = ctx_ref.shape[1:]
    total = w * count
    fill_params(pb_ref, 0, small_refs[nl - 1], w, place, total)
    sweep(ctx_ref, pb_ref, (obs,), (0,), total, state_load(in_ref, w), state_store(state_ref, w))
    edge_ref[...] = jnp.zeros_like(edge_ref)
    finish(state_ref, ctx_ref, mask_ref[0], mask_ref[1], small_refs, srow_ref, grad_ref, edge_ref, pay_ref)


def second_body(nl, recv_ref, grad_ref, edge_ref, ctx0_ref, mask_ref, srow0_ref, *rest):
    small_refs, obs_refs = rest[:nl], rest[nl : 2 * nl]
    out_ref, pay_ref, ctx_ref, state_ref, pb_ref, srow_ref = rest[2 * nl :]
    li, si, place, count = position()
    rows, w = ctx_ref.shape[1:]
    total = w * count
    inv_depth, inv_albedo = inverse_scales(recv_ref, 3, float(rows * total))
    surface = ctx0_ref[0] - STEP_DEPTH * jnp.tanh(grad_ref[0] * inv_depth)
    albedo = mask_ref[0] - STEP_ALBEDO * jnp.tanh(grad_ref[1] * inv_albedo)
    out_ref[0] = surface
    out_ref[1] = albedo
    srow_ref[...] = jnp.zeros_like(srow_ref)
    srow_ref[2:4, :] = edge_ref[0:2, :]

    @pl.when(place > 0)
    def _():
        frm = exchange_index(jnp.maximum(place - 1, 0))
        srow_ref[0:2, :] = recv_ref[frm, 0:2, :]
        srow_ref[6:7, :] = recv_ref[frm, 2:3, :]

    @pl.when(place < count - 1)
    def _():
        frm = exchange_index(jnp.minimum(place + 1, count - 1))
        srow_ref[4:6, :] = recv_ref[frm, 0:2, :]
        srow_ref[7:8, :] = recv_ref[frm, 2:3, :]

    changes = srow_ref[0:8, :]
    kind = iota(changes.shape, 0) < 6
    changes = jnp.where(
        kind, STEP_DEPTH * jnp.tanh(changes * inv_depth), STEP_ALBEDO * jnp.tanh(changes * inv_albedo)
    )
    srow_ref[0:8, :] = srow0_ref[0:8, :] - changes
    srow_ref[8:16, :] = srow0_ref[8:16, :]
    fill_context(ctx_ref, surface, albedo, srow_ref[1:2, :], srow_ref[4:5, :])
    n = obs_refs[0].shape[0]
    bases = tuple(k * n for k in range(nl))
    for k in range(nl):
        fill_params(pb_ref, bases[k], small_refs[k], w, place, total)
    sweep(ctx_ref, pb_ref, obs_refs, bases, total, lambda at: None, state_store(state_ref, w))
    depth, grad_albedo = finish(
        state_ref, ctx_ref, albedo, mask_ref[1], small_refs, srow_ref, None, None, pay_ref
    )
    out_ref[2] = depth
    out_ref[3] = grad_albedo


def final_body(nl, recv_ref, *rest):
    parts, (depth_ref, albedo_ref) = rest[:nl], rest[nl:]
    li, si, place, count = position()
    rows, w = parts[0].shape[1:]
    inv_depth, inv_albedo = inverse_scales(recv_ref, 0, float(rows * w * count))
    for k in range(nl):
        at = pl.ds(pl.multiple_of((li ^ k) * w, w), w)
        depth_ref[:, at] = parts[k][0] - STEP_DEPTH * jnp.tanh(parts[k][2] * inv_depth)
        albedo_ref[:, at] = parts[k][1] - STEP_ALBEDO * jnp.tanh(parts[k][3] * inv_albedo)


def shape(*dims, dtype=F32):
    return jax.ShapeDtypeStruct(dims, dtype)


def shards(depth_start, albedo_start, observations, light_table, valid_mask):
    nl, ns = lax.axis_size("light"), lax.axis_size("strip")
    nd = nl * ns
    lights, rows, cols = observations.shape
    w = cols // nl
    li = lax.axis_index("light")

    def over(k):
        return [(i, i ^ k) for i in range(nl)]

    def block(x, k):
        return lax.dynamic_slice_in_dim(x, (li ^ k) * w, w, axis=2)

    obs2 = lax.ppermute(block(observations, 2), "light", over(2))
    obs1 = lax.ppermute(block(observations, 1), "light", over(1))
    obs0 = block(observations, 0)
    up = 2 * lights
    fwd, bwd, eh, sr = call(
        functools.partial(edges_body, nl),
        (shape(up, rows), shape(up, rows), shape(nl, up, rows), shape(nl, 16, rows)),
        name="edges",
    )(observations, depth_start, albedo_start, valid_mask)
    low = lax.ppermute(fwd, "strip", [(i, i + 1) for i in range(ns - 1)])
    high = lax.ppermute(bwd, "strip", [(i + 1, i) for i in range(ns - 1)])
    *small, srow = call(
        functools.partial(halos_body, nl),
        tuple(shape(3 * lights, rows) for _ in range(nl)) + (shape(16, rows),),
        name="halos",
    )(eh, sr, low, high, light_table)
    send3, small[3] = lax.optimization_barrier((block(observations, 3), small[3]))
    small = [small[0]] + [lax.ppermute(small[k], "light", over(k)) for k in range(1, nl)]
    obs3 = lax.ppermute(send3, "light", over(3))

    pb = pltpu.VMEM((2 * lights, 5, 8, w), F32)
    field = (rows, w)
    ctx, mask, state = call(
        functools.partial(first_body, nl),
        (shape(4, *field), shape(2, *field), shape(7, *field)),
        [pb],
        name="first",
    )(depth_start, albedo_start, valid_mask, srow, small[0], small[1], obs0, obs1)
    state = call(more_body, shape(7, *field), [pb], name="more")(ctx, state, small[2], obs2)
    grad, edge, pay = call(
        functools.partial(last_body, nl),
        (shape(2, *field), shape(8, rows), shape(nd, 4, rows)),
        [pb, pltpu.VMEM((7, *field), F32)],
        name="last",
    )(ctx, mask, state, srow, *small, obs3)
    recv = lax.all_to_all(pay, AXES, 0, 0, tiled=True)
    own, pay = call(
        functools.partial(second_body, nl),
        (shape(4, *field), shape(nd, 1, rows)),
        [
            pltpu.VMEM((4, *field), F32),
            pltpu.VMEM((7, *field), F32),
            pltpu.VMEM((nl * lights, 5, 8, w), F32),
            pltpu.VMEM((16, rows), F32),
        ],
        name="second",
    )(recv, grad, edge, ctx, mask, srow, *small, obs0, obs1, obs2, obs3)
    part2 = lax.ppermute(own, "light", over(2))
    part1 = lax.ppermute(own, "light", over(1))
    recv = lax.all_to_all(pay, AXES, 0, 0, tiled=True)
    part3 = lax.ppermute(part2, "light", over(1))
    return tuple(
        call(functools.partial(final_body, nl), (shape(rows, cols), shape(rows, cols)), name="final")(
            recv, own, part1, part2, part3
        )
    )


def solution(mesh):
    in_specs = (
        P(None, "strip"),
        P(None, "strip"),
        P("light", None, "strip"),
        P("light", None),
        P(None, "strip"),
    )
    out_specs = (P(None, "strip"), P(None, "strip"))
    return jax.shard_map(shards, mesh=mesh, in_specs=in_specs, out_specs=out_specs, check_vma=False)
```

time: 336 us -> 65.5 us (0.19)
  waiting for transfers between devices: 214 us -> 16.3 us
  other arithmetic: 37 us -> 0 us
  blocking collectives: 40.4 us -> 22.9 us
  between operations: 17.1 us -> 0.81 us
  starting transfers between devices: 22.2 us -> 11.3 us
  Pallas kernels: 0 us -> 9.46 us
    psum x4 -> x0, waiting for transfers between devices: 138 us -> none  [the longest x2 73.2 us: shards(): lax.psum((grad_x, grad_y, grad_direct, grad_albedo), 'light')]
    pmax x2 -> x0, waiting for transfers between devices: 67 us -> none  [shards(): highest = lax.pmax(local_high, 'light')]
    psum x2 -> x0, blocking collectives: 40.4 us -> none  [shards(): lax.psum((jnp.sum(full_depth * full_depth), jnp.sum(full_albedo * full_al...]
    reduce_sum x8 -> x0, other arithmetic: 23.1 us -> none  [the longest x2 11.5 us: light_gradients(): grad_x = jnp.sum(scaled * (-delta_x - facing * slope_x / norm_sq), axis=0)]
    all_to_all x0 -> x2, blocking collectives: none -> 22.9 us  [shards(): recv = lax.all_to_all(pay, AXES, 0, 0, tiled=True)]
    ppermute x8 -> x11, starting transfers between devices: 22 us -> 11.3 us  [the longest x1 4.91 us: shards(): low = lax.ppermute(fwd, 'strip', [(i, i + 1) for i in range(ns - 1)])]
    pallas_call x0 -> x7, Pallas kernels: none -> 9.46 us  [the longest x1 3.63 us: shards(): call(functools.partial(second_body, nl), (shape(4, *field), shape(nd, 1,...]
    ppermute x8 -> x11, waiting for transfers between devices: 8.4 us -> 16.3 us  [the longest x1 7.63 us: shards(): part2 = lax.ppermute(own, 'light', over(2))]
  transfers between devices with their start and end apart: 14 -> 11, of which waited for: 11 -> 4; matrix products, arithmetic and copies ran while one was open for 2% -> 0% of each run, Pallas kernels for 0% -> 4%
where the time goes in v1:
time: 65.5 us; the launch traced here: 65.2 us
  blocking collectives  22.9 us (35%)
  waiting for transfers between devices  16.3 us (25%)
  starting transfers between devices  11.3 us (17%)
  Pallas kernels  9.46 us (14%)
  local copies, waits for them, and re-layouts  4.37 us (7%)
  between operations  0.81 us (1%)
    all_to_all x2, blocking collectives, shards(): recv = lax.all_to_all(pay, AXES, 0, 0, tiled=True)  22.9 us
    ppermute x1, waiting for transfers between devices, shards(): part2 = lax.ppermute(own, 'light', over(2))  7.63 us
    ppermute x3, waiting for transfers between devices, shards(): lax.ppermute(small[k], 'light', over(k))  6.43 us
    ppermute x1, starting transfers between devices, shards(): low = lax.ppermute(fwd, 'strip', [(i, i + 1) for i in range(ns - 1)])  4.91 us
    unnamed x19, local copies, waits for them, and re-layouts  4.18 us
    pallas_call x1, Pallas kernels, shards(): call(functools.partial(second_body, nl), (shape(4, *field), shape(nd, 1,...  3.63 us
    ppermute x3, starting transfers between devices, shards(): lax.ppermute(small[k], 'light', over(k))  2.65 us
    ppermute x1, waiting for transfers between devices, shards(): high = lax.ppermute(bwd, 'strip', [(i + 1, i) for i in range(ns - 1)])  2.24 us
  transfers between devices with their start and end apart: 11, of which 4 were waited for; matrix products, arithmetic and copies ran while one was open for 0% of the time, Pallas kernels for 4%

profile of v1, /device:TPU:0, one launch (start us, length us, event | category | flops | bytes accessed | tf_op | source)
XLA Modules:
  0.0 65.2 jit_solution(7652955038867249995)
XLA Ops:
  0.6 1.2 %copy-done = bf16[8,128,512]{2,1,0:T(8,128)(2,1)S(1)} copy-done((bf16[8,128,512]{2,1,0:T(8,128)(2,1)S(1)}, bf16[8,128,512]{2,1,0:T(8,128)(2,1)}, u32[]{:S(2)}) %copy-start) | copy-done | bytes 1048600
  1.9 0.9 %copy-done.2 = f32[128,512]{1,0:T(8,128)S(1)} copy-done((f32[128,512]{1,0:T(8,128)S(1)}, f32[128,512]{1,0:T(8,128)}, u32[]{:S(2)}) %copy-start.2) | copy-done | bytes 262168
  2.8 0.9 %copy-done.4 = f32[128,512]{1,0:T(8,128)S(1)} copy-done((f32[128,512]{1,0:T(8,128)S(1)}, f32[128,512]{1,0:T(8,128)}, u32[]{:S(2)}) %copy-start.4) | copy-done | bytes 262168
  3.8 0.9 %copy-done.6 = s32[128,512]{1,0:T(8,128)S(1)} copy-done((s32[128,512]{1,0:T(8,128)S(1)}, s32[128,512]{1,0:T(8,128)}, u32[]{:S(2)}) %copy-start.6) | copy-done | bytes 262168
  4.7 1.0 %edges.1 = (f32[16,128]{1,0:T(8,128)S(1)}, f32[16,128]{1,0:T(8,128)S(1)}, f32[4,16,128]{2,1,0:T(8,128)S(1)}, f32[4,16,128]{2,1,0:T(8,128)S(1)}) custom-call(bf16[8,128,512]{2,1,0:T(8,128)(2,1)S(1)} %copy-done, f32[128,512]{1,0:T(8,128)S(1)} %copy-done.2, f32[128,512]{1,0:T(8,128)S(1)} %copy-done.4, s32[128,512]{1,0:T(8,128)S(1)} %copy-done.6), custom_call_target="tpu_custom_call" | custom-call | tf_op jit(solution)/shard_map/edges/pallas_call | solution.py:484
  5.7 4.9 %collective-permute-start = (f32[16,128]{1,0:T(8,128)S(1)}, f32[16,128]{1,0:T(8,128)S(1)}, u32[]{:S(2)}, u32[]{:S(2)}) collective-permute-start(f32[16,128]{1,0:T(8,128)S(1)} %get-tuple-element.23), channel_id=1, source_target_pairs={{0,1},{1,2},{2,3},{3,4},{4,5},{5,6},{6,7},{8,9},{9,10},{10,11},{11... | collective-permute-start | bytes 24584 | tf_op jit(solution)/shard_map/ppermute | solution.py:489
  10.6 1.3 %collective-permute-start.1 = (f32[16,128]{1,0:T(8,128)S(1)}, f32[16,128]{1,0:T(8,128)S(1)}, u32[]{:S(2)}, u32[]{:S(2)}) collective-permute-start(f32[16,128]{1,0:T(8,128)S(1)} %get-tuple-element.24), channel_id=1, source_target_pairs={{1,0},{2,1},{3,2},{4,3},{5,4},{6,5},{7,6},{9,8},{10,9},{11,10},{12... | collective-permute-start | bytes 24584 | tf_op jit(solution)/shard_map/ppermute | solution.py:490
  12.0 0.2 constant_dynamic-slice_fusion
  12.3 1.6 %collective-permute-start.5 = (bf16[8,128,128]{2,1,0:T(8,128)(2,1)S(1)}, bf16[8,128,128]{2,1,0:T(8,128)(2,1)S(1)}, u32[]{:S(2)}, u32[]{:S(2)}) collective-permute-start(bf16[8,128,128]{2,1,0:T(8,128)(2,1)S(1)} %get-tuple-element.43), channel_id=1, source_target_pairs={{0,16},{8,24},{16,0},{24,8},{1,17},{9,25},{17,1},{25,9},{2,18},{10... | collective-permute-start | bytes 786440 | tf_op jit(solution)/shard_map/ppermute | solution.py:480
  13.9 2.2 %collective-permute-done.1.high_ref = f32[16,128]{1,0:T(8,128)S(1)} collective-permute-done((f32[16,128]{1,0:T(8,128)S(1)}, f32[16,128]{1,0:T(8,128)S(1)}, u32[]{:S(2)}, u32[]{:S(2)}) %collective-permute-start.1) | collective-permute-done | bytes 8224 | tf_op jit(solution)/shard_map/ppermute | solution.py:490
  16.3 1.6 %collective-permute-start.2 = (f32[24,128]{1,0:T(8,128)S(1)}, f32[24,128]{1,0:T(8,128)S(1)}, u32[]{:S(2)}, u32[]{:S(2)}) collective-permute-start(f32[24,128]{1,0:T(8,128)S(1)} %get-tuple-element.27), channel_id=1, source_target_pairs={{0,8},{8,0},{16,24},{24,16},{1,9},{9,1},{17,25},{25,17},{2,10},{10... | collective-permute-start | bytes 36872 | tf_op jit(solution)/shard_map/ppermute | solution.py:497
  17.9 0.5 collective-permute-start.4
  18.4 0.3 collective-permute-done.2.small1.rest_1_
  18.7 0.5 collective-permute-start.6
  19.3 1.6 %first.1 = (f32[4,128,128]{2,1,0:T(8,128)S(1)}, f32[2,128,128]{2,1,0:T(8,128)S(1)}, f32[7,128,128]{2,1,0:T(8,128)S(1)}) custom-call(f32[128,512]{1,0:T(8,128)S(1)} %copy-done.3, f32[128,512]{1,0:T(8,128)S(1)} %copy-done.5, s32[128,512]{1,0:T(8,128)S(1)} %copy-done.7, f32[16,128]{1,0:T(8,128)S(1)} %get-tuple-element.25.srow_ref.srow0_ref, ...), custom_call_target="tpu_custom_call" | custom-call | tf_op jit(solution)/shard_map/first/pallas_call | solution.py:502
  20.9 6.1 %collective-permute-done.4.small.rest_2_ = f32[24,128]{1,0:T(8,128)S(1)} collective-permute-done((f32[24,128]{1,0:T(8,128)S(1)}, f32[24,128]{1,0:T(8,128)S(1)}, u32[]{:S(2)}, u32[]{:S(2)}) %collective-permute-start.4) | collective-permute-done | bytes 12320 | tf_op jit(solution)/shard_map/ppermute | solution.py:497
  27.0 0.9 %more.1.in_ref = f32[7,128,128]{2,1,0:T(8,128)S(1)} custom-call(f32[4,128,128]{2,1,0:T(8,128)S(1)} %get-tuple-element.28.ctx_ref.ctx0_ref, f32[7,128,128]{2,1,0:T(8,128)S(1)} %get-tuple-element.30.in_ref, f32[24,128]{1,0:T(8,128)S(1)} %collective-permute-done.4.small.rest_2_, bf16[8,128,128]{2,1,0:T(8,128)(2,1)S(1)} %collective-permute-done.5.obs.rest_6_), custom_call_target="tpu_custom_call" | custom-call | tf_op jit(solution)/shard_map/more/pallas_call | solution.py:508
  27.9 1.3 %last.1 = (f32[2,128,128]{2,1,0:T(8,128)S(1)}, f32[8,128]{1,0:T(8,128)S(1)}, f32[32,4,128]{2,1,0:T(4,128)S(1)}) custom-call(f32[4,128,128]{2,1,0:T(8,128)S(1)} %get-tuple-element.28.ctx_ref.ctx0_ref, f32[2,128,128]{2,1,0:T(8,128)S(1)} %get-tuple-element.29.mask_ref, f32[7,128,128]{2,1,0:T(8,128)S(1)} %more.1.in_ref, ...), custom_call_target="tpu_custom_call" | custom-call | tf_op jit(solution)/shard_map/last/pallas_call | solution.py:509
  29.2 14.1 %all_to_all.10.recv_ref = f32[32,4,128]{2,1,0:T(4,128)S(1)} all-to-all(f32[32,4,128]{2,1,0:T(4,128)S(1)} %get-tuple-element.35), channel_id=1, replica_groups=mesh['light'=4,'strip'=8] {'light','strip'}, dimensions={0} | all-to-all | bytes 131072 | tf_op jit(solution)/shard_map/all_to_all | solution.py:515
  43.3 3.6 %second.1 = (f32[4,128,128]{2,1,0:T(8,128)S(1)}, f32[32,1,128]{2,1,0:T(1,128)S(1)}) custom-call(f32[32,4,128]{2,1,0:T(4,128)S(1)} %all_to_all.10.recv_ref, f32[2,128,128]{2,1,0:T(8,128)S(1)} %get-tuple-element.36.grad_ref, f32[8,128]{1,0:T(8,128)S(1)} %get-tuple-element.37.edge_ref, f32[4,128,128]{2,1,0:T(8,128)S(1)} %get-tuple-element.28.ctx_ref.ctx0_ref, ...), custom_call_target="tpu_custom_call" | custom-call | tf_op jit(solution)/shard_map/second/pallas_call | solution.py:516
  46.9 0.8 %collective-permute-start.9 = (f32[4,128,128]{2,1,0:T(8,128)S(1)}, f32[4,128,128]{2,1,0:T(8,128)S(1)}, u32[]{:S(2)}, u32[]{:S(2)}) collective-permute-start(f32[4,128,128]{2,1,0:T(8,128)S(1)} %get-tuple-element.39.rest_0_), channel_id=1, source_target_pairs={{0,16},{8,24},{16,0},{24,8},{1,17},{9,25},{17,1},{25,9},{2,18},{10... | collective-permute-start | bytes 786440 | tf_op jit(solution)/shard_map/ppermute | solution.py:527
  47.7 7.6 %collective-permute-done.9.rest_2_ = f32[4,128,128]{2,1,0:T(8,128)S(1)} collective-permute-done((f32[4,128,128]{2,1,0:T(8,128)S(1)}, f32[4,128,128]{2,1,0:T(8,128)S(1)}, u32[]{:S(2)}, u32[]{:S(2)}) %collective-permute-start.9) | collective-permute-done | bytes 262176 | tf_op jit(solution)/shard_map/ppermute | solution.py:527
  55.3 8.8 %all_to_all.11.recv_ref = f32[32,1,128]{2,1,0:T(1,128)S(1)} all-to-all(f32[32,1,128]{2,1,0:T(1,128)S(1)} %get-tuple-element.38), channel_id=1, replica_groups=mesh['light'=4,'strip'=8] {'light','strip'}, dimensions={0} | all-to-all | bytes 32768 | tf_op jit(solution)/shard_map/all_to_all | solution.py:529
  64.1 1.0 %final.1 = (f32[128,512]{1,0:T(8,128)}, f32[128,512]{1,0:T(8,128)}) custom-call(f32[32,1,128]{2,1,0:T(1,128)S(1)} %all_to_all.11.recv_ref, f32[4,128,128]{2,1,0:T(8,128)S(1)} %get-tuple-element.39.rest_0_, f32[4,128,128]{2,1,0:T(8,128)S(1)} %collective-permute-done.8.rest_1_, f32[4,128,128]{2,1,0:T(8,128)S(1)} %collective-permute-done.9.rest_2_, ...), custom_call_target="tpu_custom_call" | custom-call | tf_op jit(solution)/shard_map/final/pallas_call | solution.py:532
  (27 shorter events, 0.3 us)
Async XLA Ops:
  0.6 1.2 %copy-start = (bf16[8,128,512]{2,1,0:T(8,128)(2,1)S(1)}, bf16[8,128,512]{2,1,0:T(8,128)(2,1)}, u32[]{:S(2)}) copy-start(bf16[8,128,512]{2,1,0:T(8,128)(2,1)} %obs_ref.1) | copy-start | bytes 3145732
  1.9 0.9 %copy-start.2 = (f32[128,512]{1,0:T(8,128)S(1)}, f32[128,512]{1,0:T(8,128)}, u32[]{:S(2)}) copy-start(f32[128,512]{1,0:T(8,128)} %depth_ref.3) | copy-start | bytes 786436
  2.8 0.9 %copy-start.4 = (f32[128,512]{1,0:T(8,128)S(1)}, f32[128,512]{1,0:T(8,128)}, u32[]{:S(2)}) copy-start(f32[128,512]{1,0:T(8,128)} %albedo_ref.3) | copy-start | bytes 786436
  3.8 0.9 %copy-start.6 = (s32[128,512]{1,0:T(8,128)S(1)}, s32[128,512]{1,0:T(8,128)}, u32[]{:S(2)}) copy-start(s32[128,512]{1,0:T(8,128)} %valid_ref.3) | copy-start | bytes 786436
  4.7 7.2 %copy-start.1 = (bf16[8,128,512]{2,1,0:T(8,128)(2,1)S(1)}, bf16[8,128,512]{2,1,0:T(8,128)(2,1)}, u32[]{:S(2)}) copy-start(bf16[8,128,512]{2,1,0:T(8,128)(2,1)} %obs_ref.1) | copy-start | bytes 3145732
  5.7 8.2 %collective-permute-start = (f32[16,128]{1,0:T(8,128)S(1)}, f32[16,128]{1,0:T(8,128)S(1)}, u32[]{:S(2)}, u32[]{:S(2)}) collective-permute-start(f32[16,128]{1,0:T(8,128)S(1)} %get-tuple-element.23), channel_id=1, source_target_pairs={{0,1},{1,2},{2,3},{3,4},{4,5},{5,6},{6,7},{8,9},{9,10},{10,11},{11... | collective-permute-start | bytes 24584 | tf_op jit(solution)/shard_map/ppermute | solution.py:489
  10.6 5.5 %collective-permute-start.1 = (f32[16,128]{1,0:T(8,128)S(1)}, f32[16,128]{1,0:T(8,128)S(1)}, u32[]{:S(2)}, u32[]{:S(2)}) collective-permute-start(f32[16,128]{1,0:T(8,128)S(1)} %get-tuple-element.24), channel_id=1, source_target_pairs={{1,0},{2,1},{3,2},{4,3},{5,4},{6,5},{7,6},{9,8},{10,9},{11,10},{12... | collective-permute-start | bytes 24584 | tf_op jit(solution)/shard_map/ppermute | solution.py:490
  11.9 7.3 %copy-start.3 = (f32[128,512]{1,0:T(8,128)S(1)}, f32[128,512]{1,0:T(8,128)}, u32[]{:S(2)}) copy-start(f32[128,512]{1,0:T(8,128)} %depth_ref.3) | copy-start | bytes 786436
  12.0 7.3 %copy-start.5 = (f32[128,512]{1,0:T(8,128)S(1)}, f32[128,512]{1,0:T(8,128)}, u32[]{:S(2)}) copy-start(f32[128,512]{1,0:T(8,128)} %albedo_ref.3) | copy-start | bytes 786436
  12.0 7.3 %copy-start.7 = (s32[128,512]{1,0:T(8,128)S(1)}, s32[128,512]{1,0:T(8,128)}, u32[]{:S(2)}) copy-start(s32[128,512]{1,0:T(8,128)} %valid_ref.3) | copy-start | bytes 786436
  12.2 1.7 %copy-start.8 = (s32[8,4]{0,1:T(4,128)S(1)}, s32[8,4]{0,1:T(4,128)}, u32[]{:S(2)}) copy-start(s32[8,4]{0,1:T(4,128)} %param.8) | copy-start | bytes 388
  12.2 7.0 %collective-permute-start.3 = (bf16[8,128,128]{2,1,0:T(8,128)(2,1)S(1)}, bf16[8,128,128]{2,1,0:T(8,128)(2,1)S(1)}, u32[]{:S(2)}, u32[]{:S(2)}) collective-permute-start(bf16[8,128,128]{2,1,0:T(8,128)(2,1)S(1)} %get-tuple-element.41), channel_id=1, source_target_pairs={{0,8},{8,0},{16,24},{24,16},{1,9},{9,1},{17,25},{25,17},{2,10},{10... | collective-permute-start | bytes 786440 | tf_op jit(solution)/shard_map/ppermute | solution.py:481
  12.3 14.7 %collective-permute-start.5 = (bf16[8,128,128]{2,1,0:T(8,128)(2,1)S(1)}, bf16[8,128,128]{2,1,0:T(8,128)(2,1)S(1)}, u32[]{:S(2)}, u32[]{:S(2)}) collective-permute-start(bf16[8,128,128]{2,1,0:T(8,128)(2,1)S(1)} %get-tuple-element.43), channel_id=1, source_target_pairs={{0,16},{8,24},{16,0},{24,8},{1,17},{9,25},{17,1},{25,9},{2,18},{10... | collective-permute-start | bytes 786440 | tf_op jit(solution)/shard_map/ppermute | solution.py:480
  16.2 11.7 %collective-permute-start.7 = (bf16[8,128,128]{2,1,0:T(8,128)(2,1)S(1)}, bf16[8,128,128]{2,1,0:T(8,128)(2,1)S(1)}, u32[]{:S(2)}, u32[]{:S(2)}) collective-permute-start(bf16[8,128,128]{2,1,0:T(8,128)(2,1)S(1)} %get-tuple-element.34), channel_id=1, source_target_pairs={{0,24},{8,16},{16,8},{24,0},{1,25},{9,17},{17,9},{25,1},{2,26},{10... | collective-permute-start | bytes 786440 | tf_op jit(solution)/shard_map/ppermute | solution.py:498
  16.3 2.4 %collective-permute-start.2 = (f32[24,128]{1,0:T(8,128)S(1)}, f32[24,128]{1,0:T(8,128)S(1)}, u32[]{:S(2)}, u32[]{:S(2)}) collective-permute-start(f32[24,128]{1,0:T(8,128)S(1)} %get-tuple-element.27), channel_id=1, source_target_pairs={{0,8},{8,0},{16,24},{24,16},{1,9},{9,1},{17,25},{25,17},{2,10},{10... | collective-permute-start | bytes 36872 | tf_op jit(solution)/shard_map/ppermute | solution.py:497
  17.9 9.1 %collective-permute-start.4 = (f32[24,128]{1,0:T(8,128)S(1)}, f32[24,128]{1,0:T(8,128)S(1)}, u32[]{:S(2)}, u32[]{:S(2)}) collective-permute-start(f32[24,128]{1,0:T(8,128)S(1)} %get-tuple-element.31), channel_id=1, source_target_pairs={{0,16},{8,24},{16,0},{24,8},{1,17},{9,25},{17,1},{25,9},{2,18},{10... | collective-permute-start | bytes 36872 | tf_op jit(solution)/shard_map/ppermute | solution.py:497
  18.7 9.2 %collective-permute-start.6 = (f32[24,128]{1,0:T(8,128)S(1)}, f32[24,128]{1,0:T(8,128)S(1)}, u32[]{:S(2)}, u32[]{:S(2)}) collective-permute-start(f32[24,128]{1,0:T(8,128)S(1)} %get-tuple-element.33), channel_id=1, source_target_pairs={{0,24},{8,16},{16,8},{24,0},{1,25},{9,17},{17,9},{25,1},{2,26},{10... | collective-permute-start | bytes 36872 | tf_op jit(solution)/shard_map/ppermute | solution.py:497
  46.9 8.4 %collective-permute-start.9 = (f32[4,128,128]{2,1,0:T(8,128)S(1)}, f32[4,128,128]{2,1,0:T(8,128)S(1)}, u32[]{:S(2)}, u32[]{:S(2)}) collective-permute-start(f32[4,128,128]{2,1,0:T(8,128)S(1)} %get-tuple-element.39.rest_0_), channel_id=1, source_target_pairs={{0,16},{8,24},{16,0},{24,8},{1,17},{9,25},{17,1},{25,9},{2,18},{10... | collective-permute-start | bytes 786440 | tf_op jit(solution)/shard_map/ppermute | solution.py:527
  47.7 16.5 %collective-permute-start.8 = (f32[4,128,128]{2,1,0:T(8,128)S(1)}, f32[4,128,128]{2,1,0:T(8,128)S(1)}, u32[]{:S(2)}, u32[]{:S(2)}) collective-permute-start(f32[4,128,128]{2,1,0:T(8,128)S(1)} %get-tuple-element.39.rest_0_), channel_id=1, source_target_pairs={{0,8},{8,0},{16,24},{24,16},{1,9},{9,1},{17,25},{25,17},{2,10},{10... | collective-permute-start | bytes 786440 | tf_op jit(solution)/shard_map/ppermute | solution.py:528
  55.3 8.8 %collective-permute-start.10 = (f32[4,128,128]{2,1,0:T(8,128)S(1)}, f32[4,128,128]{2,1,0:T(8,128)S(1)}, u32[]{:S(2)}, u32[]{:S(2)}) collective-permute-start(f32[4,128,128]{2,1,0:T(8,128)S(1)} %collective-permute-done.9.rest_2_), channel_id=1, source_target_pairs={{0,8},{8,0},{16,24},{24,16},{1,9},{9,1},{17,25},{25,17},{2,10},{10... | collective-permute-start | bytes 786440 | tf_op jit(solution)/shard_map/ppermute | solution.py:530

commit v2 on v1

--- a/solution.py
+++ b/solution.py
@@ -7,6 +7,7 @@
 from jax.experimental import pallas as pl
 from jax.experimental.pallas import tpu as pltpu
 from jax.sharding import PartitionSpec as P
+
 
 AXES = ("light", "strip")
 STEP_DEPTH = 0.1
@@ -33,63 +34,86 @@
     return lax.rem(place, nl) * ns + lax.div(place, nl)
 
 
-def call(body, out, scratch=(), name=None, aliases=None, cost=None):
+def call(body, out, scratch=(), vmem=40 << 20, **more):
     return pl.pallas_call(
         body,
         out_shape=out,
         scratch_shapes=list(scratch),
-        name=name,
-        input_output_aliases=aliases or {},
-        compiler_params=pltpu.CompilerParams(vmem_limit_bytes=40 << 20),
-        cost_estimate=cost,
-    )
-
-
-def edges_body(nl, obs_ref, depth_ref, albedo_ref, valid_ref, fwd_ref, bwd_ref, eh_ref, sr_ref):
+        compiler_params=pltpu.CompilerParams(vmem_limit_bytes=vmem),
+        **more,
+    )
+
+
+def cut_body(nl, obs_ref, table_ref, *rest):
+    outs, (table, sems) = rest[:nl], rest[nl:]
     lights, rows, cols = obs_ref.shape
     w = cols // nl
-
-    def picks(columns):
+    li = lax.axis_index("light")
+    copies = []
+    for k in (2, 3, 1, 0):
+        at = pl.ds(pl.multiple_of((li ^ k) * w, w), w)
+        for l in range(lights):
+            copy = pltpu.make_async_copy(
+                obs_ref.at[l, :, at], outs[k].at[pl.ds(l * rows, rows)], sems.at[k * lights + l]
+            )
+            copy.start()
+            copies.append(copy)
+    fetch = pltpu.make_async_copy(table_ref, table, sems.at[nl * lights])
+    fetch.start()
+    fetch.wait()
+    entries = table[...]
+    high = lax.shift_right_logical(entries, 5)
+    both = jnp.concatenate([high, entries - high * 32], axis=0).astype(F32)
+    wide = jnp.concatenate([both, jnp.zeros((8, w - lights), F32)], axis=1)
+    under = jnp.concatenate([wide, jnp.zeros((8, w), F32)], axis=0).astype(jnp.bfloat16)
+    for k in range(nl):
+        outs[k][pl.ds(lights * rows, 16), :] = under
+    for copy in copies:
+        copy.wait()
+
+
+def edges_body(nl, depth_ref, albedo_ref, valid_ref, *rest):
+    block_refs, (fwd_ref, bwd_ref, eh_ref, sr_ref) = rest[:nl], rest[nl:]
+    rows, cols = depth_ref.shape
+    w = cols // nl
+    lights = block_refs[0].shape[0] // rows
+    li = lax.axis_index("light")
+
+    def picks(columns, size):
         pad = -len(columns) % 8
-        row = iota((len(columns) + pad, cols), 0)
-        col = iota((len(columns) + pad, cols), 1)
+        row = iota((len(columns) + pad, size), 0)
+        col = iota((len(columns) + pad, size), 1)
         hit = jnp.zeros(row.shape, jnp.bool_)
         for index, column in enumerate(columns):
             hit = hit | ((row == index) & (col == column))
         return hit.astype(F32)
 
-    ends = []
+    ends, pairs = [], []
     for q in range(nl):
         ends += [q * w, q * w + w - 1]
-    pairs = []
-    for q in range(nl):
         pairs += [q * w, q * w + 1, q * w + w - 2, q * w + w - 1]
     contract = (((1,), (1,)), ((), ()))
-    pick_ends = picks(ends)
-    pick_pairs = picks(pairs)
-    exact = lax.Precision.HIGHEST
-    depth = lax.dot_general(pick_pairs, depth_ref[...], contract, precision=exact, preferred_element_type=F32)
-    albedo = lax.dot_general(pick_ends, albedo_ref[...], contract, precision=exact, preferred_element_type=F32)
-    valid = lax.dot_general(
-        pick_ends, valid_ref[...].astype(F32), contract, precision=exact, preferred_element_type=F32
-    )
-    zero = jnp.zeros((1, rows), F32)
+    pick_ends = picks(ends, cols)
+    exact = dict(precision=lax.Precision.HIGHEST, preferred_element_type=F32)
+    depth = lax.dot_general(picks(pairs, cols), depth_ref[...], contract, **exact)
+    albedo = lax.dot_general(pick_ends, albedo_ref[...], contract, **exact)
+    valid = lax.dot_general(pick_ends, valid_ref[...].astype(F32), contract, **exact)
     fwd_ref[...] = jnp.zeros_like(fwd_ref)
     bwd_ref[...] = jnp.zeros_like(bwd_ref)
-    eh_ref[...] = jnp.zeros_like(eh_ref)
     sr_ref[...] = jnp.zeros_like(sr_ref)
-    pick16 = pick_ends.astype(jnp.bfloat16)
-    for l in range(lights):
-        e = lax.dot_general(pick16, obs_ref[l], contract, preferred_element_type=F32)
-        bwd_ref[l : l + 1, :] = e[0:1]
-        fwd_ref[l : l + 1, :] = e[2 * nl - 1 : 2 * nl]
-        for q in range(nl):
-            if q > 0:
-                eh_ref[q, l : l + 1, :] = e[2 * q - 1 : 2 * q]
-            if q < nl - 1:
-                eh_ref[q, lights + l : lights + l + 1, :] = e[2 * q + 2 : 2 * q + 3]
+    pick16 = picks([0, w - 1], w).astype(jnp.bfloat16)
+    for k in range(nl):
+        q = li ^ k
+        for l in range(lights):
+            e = lax.dot_general(
+                pick16, block_refs[k][pl.ds(l * rows, rows), :], contract, preferred_element_type=F32
+            )
+            eh_ref[q, lights + l : lights + l + 1, :] = e[0:1]
+            eh_ref[q + 2, l : l + 1, :] = e[1:2]
     n = lights
     last = 4 * (nl - 1)
+    bwd_ref[0:n, :] = eh_ref[0, n : 2 * n, :]
+    fwd_ref[0:n, :] = eh_ref[nl + 1, 0:n, :]
     fwd_ref[n : n + 2, :] = depth[last + 2 : last + 4]
     fwd_ref[n + 2 : n + 3, :] = albedo[2 * nl - 1 : 2 * nl]
     fwd_ref[n + 3 : n + 4, :] = valid[2 * nl - 1 : 2 * nl]
@@ -117,7 +141,7 @@
     for k in range(nl):
         q = li ^ k
         ref = small_refs[k]
-        ref[0 : 2 * n, :] = eh_ref[q]
+        ref[0 : 2 * n, :] = eh_ref[q + 1]
         ref[2 * n :, :] = jnp.zeros((ref.shape[0] - 2 * n, ref.shape[1]), F32)
         ref[2 * n : 3 * n, 0:4] = table
 
@@ -150,6 +174,15 @@
         table[:, 1:2] / 500.0 - 1.0,
         1.0 + table[:, 2:3] / 1000.0,
         0.5 + table[:, 3:4] / 1000.0,
+    )
+
+
+def decode_rows(table):
+    return (
+        table[0:1] / 500.0 - 1.0,
+        table[1:2] / 500.0 - 1.0,
+        1.0 + table[2:3] / 1000.0,
+        0.5 + table[3:4] / 1000.0,
     )
 
 
@@ -187,18 +220,18 @@
     ctx_ref[3] = albedo * lax.rsqrt(1.0 + sx * sx + sy * sy)
 
 
-def fill_params(pb_ref, base, small_ref, w, place, total):
-    n = small_ref.shape[0] // 3
-    lx, ly, lz, le = decode(small_ref[2 * n : 3 * n, :])
+def fill_params(pb_ref, base, block_ref, n, w, place, total):
+    under = block_ref[pl.ds(block_ref.shape[0] - 16, 16), :].astype(F32)
+    lx, ly, lz, le = decode_rows(under[0:4] * 32.0 + under[4:8])
     col = iota((8, w), 1) + place * w
     px = (col.astype(F32) + 0.5) / total - 0.5
     for j in range(n):
-        dx = jnp.broadcast_to(lx[j : j + 1], (8, w)) - px
+        dx = jnp.broadcast_to(lx[:, j : j + 1], (8, w)) - px
         pb_ref[base + j, 0] = dx
         pb_ref[base + j, 1] = dx * dx
-        pb_ref[base + j, 2] = jnp.broadcast_to(ly[j : j + 1], (8, w))
-        pb_ref[base + j, 3] = jnp.broadcast_to(lz[j : j + 1], (8, w))
-        pb_ref[base + j, 4] = jnp.broadcast_to(le[j : j + 1], (8, w))
+        pb_ref[base + j, 2] = jnp.broadcast_to(ly[:, j : j + 1], (8, w))
+        pb_ref[base + j, 3] = jnp.broadcast_to(lz[:, j : j + 1], (8, w))
+        pb_ref[base + j, 4] = jnp.broadcast_to(le[:, j : j + 1], (8, w))
 
 
 def accumulate(state, tile, py, obs, pb_ref, base):
@@ -236,6 +269,7 @@
 
 def sweep(ctx_ref, pb_ref, obs_refs, bases, total, load, store):
     rows, w = ctx_ref.shape[1:]
+    lights = obs_refs[0].shape[0] // rows
     split = (TR // 8, 8, w)
 
     def step(i, carry):
@@ -245,7 +279,10 @@
         py = (row.astype(F32) + (0.5 - rows / 2.0)) / total
         state = load(at)
         for obs_ref, base in zip(obs_refs, bases):
-            obs = [obs_ref[j, at, :].astype(F32).reshape(split) for j in range(obs_ref.shape[0])]
+            obs = [
+                obs_ref[pl.ds(pl.multiple_of(j * rows + i * TR, TR), TR), :].astype(F32).reshape(split)
+                for j in range(lights)
+            ]
             state = accumulate(state, tile, py, obs, pb_ref, base)
         store(at, state)
         return carry
@@ -339,8 +376,8 @@
     return lax.rsqrt(d / count + EPS), lax.rsqrt(a / count + EPS)
 
 
-def first_body(nl, depth_ref, albedo_ref, valid_ref, srow_ref, small0, small1, obs0, obs1, ctx_ref, mask_ref, state_ref, pb_ref):
-    li, si, place, count = position()
+def first_body(depth_ref, albedo_ref, valid_ref, srow_ref, obs0, obs1, ctx_ref, mask_ref, state_ref, pb_ref):
+    li, _, place, count = position()
     rows, w = ctx_ref.shape[1:]
     at = pl.ds(pl.multiple_of(li * w, w), w)
     albedo = albedo_ref[:, at]
@@ -348,22 +385,22 @@
     mask_ref[1] = valid_ref[:, at].astype(F32)
     fill_context(ctx_ref, depth_ref[:, at], albedo, srow_ref[1:2, :], srow_ref[4:5, :])
     total = w * count
-    n = obs0.shape[0]
-    fill_params(pb_ref, 0, small0, w, place, total)
-    fill_params(pb_ref, n, small1, w, place, total)
+    n = obs0.shape[0] // rows
+    fill_params(pb_ref, 0, obs0, n, w, place, total)
+    fill_params(pb_ref, n, obs1, n, w, place, total)
     sweep(ctx_ref, pb_ref, (obs0, obs1), (0, n), total, lambda at: None, state_store(state_ref, w))
 
 
-def more_body(ctx_ref, in_ref, small, obs, state_ref, pb_ref):
-    li, si, place, count = position()
+def more_body(ctx_ref, in_ref, obs, state_ref, pb_ref):
+    _, _, place, count = position()
     rows, w = ctx_ref.shape[1:]
     total = w * count
-    fill_params(pb_ref, 0, small, w, place, total)
+    fill_params(pb_ref, 0, obs, obs.shape[0] // rows, w, place, total)
     sweep(ctx_ref, pb_ref, (obs,), (0,), total, state_load(in_ref, w), state_store(state_ref, w))
 
 
 def finish(state_ref, ctx_ref, albedo, valid, small_refs, srow_ref, grad_ref, edge_ref, pay_ref):
-    li, si, place, count = position()
+    _, _, place, count = position()
     rows, w = ctx_ref.shape[1:]
     total = w * count
     low = halo_slope(place * w - 1, 0, small_refs, srow_ref, rows, total)
@@ -392,13 +429,8 @@
     return depth, grad_albedo
 
 
-def last_body(nl, ctx_ref, mask_ref, in_ref, srow_ref, *rest):
-    small_refs, (obs, grad_ref, edge_ref, pay_ref, pb_ref, state_ref) = rest[:nl], rest[nl:]
-    li, si, place, count = position()
-    rows, w = ctx_ref.shape[1:]
-    total = w * count
-    fill_params(pb_ref, 0, small_refs[nl - 1], w, place, total)
-    sweep(ctx_ref, pb_ref, (obs,), (0,), total, state_load(in_ref, w), state_store(state_ref, w))
+def last_body(nl, ctx_ref, mask_ref, state_ref, srow_ref, *rest):
+    small_refs, (grad_ref, edge_ref, pay_ref) = rest[:nl], rest[nl:]
     edge_ref[...] = jnp.zeros_like(edge_ref)
     finish(state_ref, ctx_ref, mask_ref[0], mask_ref[1], small_refs, srow_ref, grad_ref, edge_ref, pay_ref)
 
@@ -406,7 +438,7 @@
 def second_body(nl, recv_ref, grad_ref, edge_ref, ctx0_ref, mask_ref, srow0_ref, *rest):
     small_refs, obs_refs = rest[:nl], rest[nl : 2 * nl]
     out_ref, pay_ref, ctx_ref, state_ref, pb_ref, srow_ref = rest[2 * nl :]
-    li, si, place, count = position()
+    _, _, place, count = position()
     rows, w = ctx_ref.shape[1:]
     total = w * count
     inv_depth, inv_albedo = inverse_scales(recv_ref, 3, float(rows * total))
@@ -437,10 +469,10 @@
     srow_ref[0:8, :] = srow0_ref[0:8, :] - changes
     srow_ref[8:16, :] = srow0_ref[8:16, :]
     fill_context(ctx_ref, surface, albedo, srow_ref[1:2, :], srow_ref[4:5, :])
-    n = obs_refs[0].shape[0]
+    n = obs_refs[0].shape[0] // rows
     bases = tuple(k * n for k in range(nl))
     for k in range(nl):
-        fill_params(pb_ref, bases[k], small_refs[k], w, place, total)
+        fill_params(pb_ref, bases[k], obs_refs[k], n, w, place, total)
     sweep(ctx_ref, pb_ref, obs_refs, bases, total, lambda at: None, state_store(state_ref, w))
     depth, grad_albedo = finish(
         state_ref, ctx_ref, albedo, mask_ref[1], small_refs, srow_ref, None, None, pay_ref
@@ -451,7 +483,7 @@
 
 def final_body(nl, recv_ref, *rest):
     parts, (depth_ref, albedo_ref) = rest[:nl], rest[nl:]
-    li, si, place, count = position()
+    li, _, _, count = position()
     rows, w = parts[0].shape[1:]
     inv_depth, inv_albedo = inverse_scales(recv_ref, 0, float(rows * w * count))
     for k in range(nl):
@@ -464,54 +496,49 @@
     return jax.ShapeDtypeStruct(dims, dtype)
 
 
-def shards(depth_start, albedo_start, observations, light_table, valid_mask):
+def program(depth_start, albedo_start, observations, light_table, valid_mask):
     nl, ns = lax.axis_size("light"), lax.axis_size("strip")
     nd = nl * ns
     lights, rows, cols = observations.shape
     w = cols // nl
-    li = lax.axis_index("light")
-
-    def over(k):
-        return [(i, i ^ k) for i in range(nl)]
-
-    def block(x, k):
-        return lax.dynamic_slice_in_dim(x, (li ^ k) * w, w, axis=2)
-
-    obs2 = lax.ppermute(block(observations, 2), "light", over(2))
-    obs1 = lax.ppermute(block(observations, 1), "light", over(1))
-    obs0 = block(observations, 0)
+
+    def swap(x, k):
+        return lax.ppermute(x, "light", [(i, i ^ k) for i in range(nl)])
+
+    hbm = pl.BlockSpec(memory_space=pltpu.HBM)
+    blocks = call(
+        functools.partial(cut_body, nl),
+        tuple(shape(lights * rows + 16, w, dtype=jnp.bfloat16) for _ in range(nl)),
+        [pltpu.VMEM((4, lights), jnp.int32), pltpu.SemaphoreType.DMA((nl * lights + 1,))],
+        vmem=54_750_000,
+        in_specs=[hbm, hbm],
+    )(observations, light_table.T)
+    obs2 = swap(blocks[2], 2)
+    obs3 = swap(blocks[3], 3)
+    obs1 = swap(blocks[1], 1)
+    obs0 = blocks[0]
     up = 2 * lights
     fwd, bwd, eh, sr = call(
         functools.partial(edges_body, nl),
-        (shape(up, rows), shape(up, rows), shape(nl, up, rows), shape(nl, 16, rows)),
-        name="edges",
-    )(observations, depth_start, albedo_start, valid_mask)
+        (shape(up, rows), shape(up, rows), shape(nl + 2, up, rows), shape(nl, 16, rows)),
+    )(depth_start, albedo_start, valid_mask, *blocks)
     low = lax.ppermute(fwd, "strip", [(i, i + 1) for i in range(ns - 1)])
     high = lax.ppermute(bwd, "strip", [(i + 1, i) for i in range(ns - 1)])
     *small, srow = call(
-        functools.partial(halos_body, nl),
-        tuple(shape(3 * lights, rows) for _ in range(nl)) + (shape(16, rows),),
-        name="halos",
+        functools.partial(halos_body, nl), tuple(shape(3 * lights, rows) for _ in range(nl)) + (shape(16, rows),)
     )(eh, sr, low, high, light_table)
-    send3, small[3] = lax.optimization_barrier((block(observations, 3), small[3]))
-    small = [small[0]] + [lax.ppermute(small[k], "light", over(k)) for k in range(1, nl)]
-    obs3 = lax.ppermute(send3, "light", over(3))
+    small = [small[0]] + [swap(small[k], k) for k in range(1, nl)]
 
     pb = pltpu.VMEM((2 * lights, 5, 8, w), F32)
     field = (rows, w)
     ctx, mask, state = call(
-        functools.partial(first_body, nl),
-        (shape(4, *field), shape(2, *field), shape(7, *field)),
-        [pb],
-        name="first",
-    )(depth_start, albedo_start, valid_mask, srow, small[0], small[1], obs0, obs1)
-    state = call(more_body, shape(7, *field), [pb], name="more")(ctx, state, small[2], obs2)
+        first_body, (shape(4, *field), shape(2, *field), shape(7, *field)), [pb]
+    )(depth_start, albedo_start, valid_mask, srow, obs0, obs1)
+    state = call(more_body, shape(7, *field), [pb])(ctx, state, obs2)
+    state = call(more_body, shape(7, *field), [pb])(ctx, state, obs3)
     grad, edge, pay = call(
-        functools.partial(last_body, nl),
-        (shape(2, *field), shape(8, rows), shape(nd, 4, rows)),
-        [pb, pltpu.VMEM((7, *field), F32)],
-        name="last",
-    )(ctx, mask, state, srow, *small, obs3)
+        functools.partial(last_body, nl), (shape(2, *field), shape(8, rows), shape(nd, 4, rows))
+    )(ctx, mask, state, srow, *small)
     recv = lax.all_to_all(pay, AXES, 0, 0, tiled=True)
     own, pay = call(
         functools.partial(second_body, nl),
@@ -522,16 +549,14 @@
             pltpu.VMEM((nl * lights, 5, 8, w), F32),
             pltpu.VMEM((16, rows), F32),
         ],
-        name="second",
     )(recv, grad, edge, ctx, mask, srow, *small, obs0, obs1, obs2, obs3)
-    part2 = lax.ppermute(own, "light", over(2))
-    part1 = lax.ppermute(own, "light", over(1))
+    part2 = swap(own, 2)
+    part1 = swap(own, 1)
     recv = lax.all_to_all(pay, AXES, 0, 0, tiled=True)
-    part3 = lax.ppermute(part2, "light", over(1))
+    recv, part2 = lax.optimization_barrier((recv, part2))
+    part3 = swap(part2, 1)
     return tuple(
-        call(functools.partial(final_body, nl), (shape(rows, cols), shape(rows, cols)), name="final")(
-            recv, own, part1, part2, part3
-        )
+        call(functools.partial(final_body, nl), (shape(rows, cols), shape(rows, cols)))(recv, own, part1, part2, part3)
     )
 
 
@@ -544,4 +569,4 @@
         P(None, "strip"),
     )
     out_specs = (P(None, "strip"), P(None, "strip"))
-    return jax.shard_map(shards, mesh=mesh, in_specs=in_specs, out_specs=out_specs, check_vma=False)
+    return jax.shard_map(program, mesh=mesh, in_specs=in_specs, out_specs=out_specs, check_vma=False)

time: 65.5 us -> 52.8 us (0.81)
  blocking collectives: 22.9 us -> 12.8 us
  waiting for transfers between devices: 16.3 us -> 12.6 us
  local copies, waits for them, and re-layouts: 4.37 us -> 0.77 us
  Pallas kernels: 9.46 us -> 12 us
  starting transfers between devices: 11.3 us -> 13.6 us
    ppermute x11, waiting for transfers between devices: 16.3 us -> 5.7 us  [the longest x1 4.15 us: program(): high = lax.ppermute(bwd, 'strip', [(i + 1, i) for i in range(ns - 1)])]
    all_to_all x2 -> x1, blocking collectives: 22.9 us -> 12.8 us  [program(): recv = lax.all_to_all(pay, AXES, 0, 0, tiled=True)]
    all_to_all x0 -> x1, waiting for transfers between devices: none -> 6.89 us  [program(): recv = lax.all_to_all(pay, AXES, 0, 0, tiled=True)]
    unnamed x19 -> x11, local copies, waits for them, and re-layouts: 4.18 us -> 0.77 us
    all_to_all x0 -> x1, starting transfers between devices: none -> 2.54 us  [program(): recv = lax.all_to_all(pay, AXES, 0, 0, tiled=True)]
    pallas_call x7 -> x9, Pallas kernels: 9.46 us -> 12 us  [the longest x1 4.27 us: program(): call(functools.partial(second_body, nl), (shape(4, *field), shape(nd, 1,...]
  transfers between devices with their start and end apart: 11 -> 12, of which waited for: 4 -> 3; matrix products, arithmetic and copies ran while one was open for 0% -> 0% of each run, Pallas kernels for 4% -> 9%
where the time goes in v2:
time: 52.8 us; the launch traced here: 52.6 us
  starting transfers between devices  13.6 us (26%)
  blocking collectives  12.8 us (24%)
  waiting for transfers between devices  12.6 us (24%)
  Pallas kernels  12 us (23%)
  local copies, waits for them, and re-layouts  0.77 us (1%)
  between operations  0.77 us (1%)
    all_to_all x1, blocking collectives, program(): recv = lax.all_to_all(pay, AXES, 0, 0, tiled=True)  12.8 us
    all_to_all x1, waiting for transfers between devices, program(): recv = lax.all_to_all(pay, AXES, 0, 0, tiled=True)  6.89 us
    ppermute x9, starting transfers between devices, swap(): return lax.ppermute(x, 'light', [(i, i ^ k) for i in range(nl)])  5.95 us
    pallas_call x1, Pallas kernels, program(): call(functools.partial(second_body, nl), (shape(4, *field), shape(nd, 1,...  4.27 us
    ppermute x1, waiting for transfers between devices, program(): high = lax.ppermute(bwd, 'strip', [(i + 1, i) for i in range(ns - 1)])  4.15 us
    ppermute x1, starting transfers between devices, program(): low = lax.ppermute(fwd, 'strip', [(i, i + 1) for i in range(ns - 1)])  3.82 us
    all_to_all x1, starting transfers between devices, program(): recv = lax.all_to_all(pay, AXES, 0, 0, tiled=True)  2.54 us
    pallas_call x1, Pallas kernels, program(): call(first_body, (shape(4, *field), shape(2, *field), shape(7, *field)),...  1.63 us
  transfers between devices with their start and end apart: 12, of which 3 were waited for; matrix products, arithmetic and copies ran while one was open for 0% of the time, Pallas kernels for 9%

profile of v2, /device:TPU:0, one launch (start us, length us, event | category | flops | bytes accessed | tf_op | source)
XLA Modules:
  0.0 52.6 jit_solution(12418047370902660928)
XLA Ops:
  0.6 0.7 %copy-done.3 = s32[8,4]{0,1:T(4,128)S(1)} copy-done((s32[8,4]{0,1:T(4,128)S(1)}, s32[8,4]{0,1:T(4,128)}, u32[]{:S(2)}) %copy-start.3) | copy-done | bytes 152
  1.3 1.5 %shard_map.68 = (bf16[1040,128]{1,0:T(8,128)(2,1)S(1)}, bf16[1040,128]{1,0:T(8,128)(2,1)S(1)}, bf16[1040,128]{1,0:T(8,128)(2,1)S(1)}, bf16[1040,128]{1,0:T(8,128)(2,1)S(1)}) custom-call(bf16[8,128,512]{2,1,0:T(8,128)(2,1)} %obs_ref.1, s32[4,8]{1,0:T(4,128)S(1)} %bitcast.1), custom_call_target="tpu_custom_call" | custom-call | tf_op jit(solution)/shard_map/pallas_call | solution.py:509
  2.9 0.6 %collective-permute-start.2 = (bf16[1040,128]{1,0:T(8,128)(2,1)S(1)}, bf16[1040,128]{1,0:T(8,128)(2,1)S(1)}, u32[]{:S(2)}, u32[]{:S(2)}) collective-permute-start(bf16[1040,128]{1,0:T(8,128)(2,1)S(1)} %get-tuple-element.26.rest_1_), channel_id=1, source_target_pairs={{0,8},{8,0},{16,24},{24,16},{1,9},{9,1},{17,25},{25,17},{2,10},{10... | collective-permute-start | bytes 798728 | tf_op jit(solution)/shard_map/ppermute | solution.py:506
  3.4 2.6 %collective-permute-start.3 = (bf16[1040,128]{1,0:T(8,128)(2,1)S(1)}, bf16[1040,128]{1,0:T(8,128)(2,1)S(1)}, u32[]{:S(2)}, u32[]{:S(2)}) collective-permute-start(bf16[1040,128]{1,0:T(8,128)(2,1)S(1)} %get-tuple-element.27.rest_2_), channel_id=1, source_target_pairs={{0,16},{8,24},{16,0},{24,8},{1,17},{9,25},{17,1},{25,9},{2,18},{10... | collective-permute-start | bytes 798728 | tf_op jit(solution)/shard_map/ppermute | solution.py:506
  6.0 1.3 %shard_map.69 = (f32[16,128]{1,0:T(8,128)S(1)}, f32[16,128]{1,0:T(8,128)S(1)}, f32[6,16,128]{2,1,0:T(8,128)S(1)}, f32[4,16,128]{2,1,0:T(8,128)S(1)}) custom-call(f32[128,512]{1,0:T(8,128)S(1)} %copy-done, f32[128,512]{1,0:T(8,128)S(1)} %copy-done.1, s32[128,512]{1,0:T(8,128)S(1)} %copy-done.2, bf16[1040,128]{1,0:T(8,128)(2,1)S(1)} %get-tuple-element.25.rest_0_.obs0.rest_4_, ...), custom_call_target="tpu_custom_call" | custom-call | tf_op jit(solution)/shard_map/pallas_call | solution.py:521
  7.3 3.8 %collective-permute-start = (f32[16,128]{1,0:T(8,128)S(1)}, f32[16,128]{1,0:T(8,128)S(1)}, u32[]{:S(2)}, u32[]{:S(2)}) collective-permute-start(f32[16,128]{1,0:T(8,128)S(1)} %get-tuple-element.31), channel_id=1, source_target_pairs={{0,1},{1,2},{2,3},{3,4},{4,5},{5,6},{6,7},{8,9},{9,10},{10,11},{11... | collective-permute-start | bytes 24584 | tf_op jit(solution)/shard_map/ppermute | solution.py:525
  11.1 1.3 %collective-permute-start.1 = (f32[16,128]{1,0:T(8,128)S(1)}, f32[16,128]{1,0:T(8,128)S(1)}, u32[]{:S(2)}, u32[]{:S(2)}) collective-permute-start(f32[16,128]{1,0:T(8,128)S(1)} %get-tuple-element.32), channel_id=1, source_target_pairs={{1,0},{2,1},{3,2},{4,3},{5,4},{6,5},{7,6},{9,8},{10,9},{11,10},{12... | collective-permute-start | bytes 24584 | tf_op jit(solution)/shard_map/ppermute | solution.py:526
  12.4 0.1 copy.7.table_ref
  12.5 4.1 %collective-permute-done.1.high_ref = f32[16,128]{1,0:T(8,128)S(1)} collective-permute-done((f32[16,128]{1,0:T(8,128)S(1)}, f32[16,128]{1,0:T(8,128)S(1)}, u32[]{:S(2)}, u32[]{:S(2)}) %collective-permute-start.1) | collective-permute-done | bytes 8224 | tf_op jit(solution)/shard_map/ppermute | solution.py:526
  16.7 0.1 collective-permute-start.5
  16.8 1.6 %collective-permute-start.6 = (f32[24,128]{1,0:T(8,128)S(1)}, f32[24,128]{1,0:T(8,128)S(1)}, u32[]{:S(2)}, u32[]{:S(2)}) collective-permute-start(f32[24,128]{1,0:T(8,128)S(1)} %get-tuple-element.39), channel_id=1, source_target_pairs={{0,16},{8,24},{16,0},{24,8},{1,17},{9,25},{17,1},{25,9},{2,18},{10... | collective-permute-start | bytes 36872 | tf_op jit(solution)/shard_map/ppermute | solution.py:506
  18.3 0.3 collective-permute-start.7
  18.6 1.6 %shard_map.71 = (f32[4,128,128]{2,1,0:T(8,128)S(1)}, f32[2,128,128]{2,1,0:T(8,128)S(1)}, f32[7,128,128]{2,1,0:T(8,128)S(1)}) custom-call(f32[128,512]{1,0:T(8,128)S(1)} %copy-done, f32[128,512]{1,0:T(8,128)S(1)} %copy-done.1, s32[128,512]{1,0:T(8,128)S(1)} %copy-done.2, f32[16,128]{1,0:T(8,128)S(1)} %get-tuple-element.33.srow_ref.srow0_ref, ...), custom_call_target="tpu_custom_call" | custom-call | tf_op jit(solution)/shard_map/pallas_call | solution.py:534
  20.3 0.9 %shard_map.72.in_ref = f32[7,128,128]{2,1,0:T(8,128)S(1)} custom-call(f32[4,128,128]{2,1,0:T(8,128)S(1)} %get-tuple-element.34.ctx_ref.ctx0_ref, f32[7,128,128]{2,1,0:T(8,128)S(1)} %get-tuple-element.36.in_ref, bf16[1040,128]{1,0:T(8,128)(2,1)S(1)} %collective-permute-done.3.obs.rest_6_), custom_call_target="tpu_custom_call" | custom-call | tf_op jit(solution)/shard_map/pallas_call | solution.py:537
  21.2 0.9 %shard_map.73.state_ref = f32[7,128,128]{2,1,0:T(8,128)S(1)} custom-call(f32[4,128,128]{2,1,0:T(8,128)S(1)} %get-tuple-element.34.ctx_ref.ctx0_ref, f32[7,128,128]{2,1,0:T(8,128)S(1)} %shard_map.72.in_ref, bf16[1040,128]{1,0:T(8,128)(2,1)S(1)} %collective-permute-done.4.obs.rest_7_), custom_call_target="tpu_custom_call" | custom-call | tf_op jit(solution)/shard_map/pallas_call | solution.py:538
  22.2 0.4 shard_map.74
  22.6 12.8 %all_to_all.10.recv_ref = f32[32,4,128]{2,1,0:T(4,128)S(1)} all-to-all(f32[32,4,128]{2,1,0:T(4,128)S(1)} %get-tuple-element.41), channel_id=1, replica_groups=mesh['light'=4,'strip'=8] {'light','strip'}, dimensions={0} | all-to-all | bytes 131072 | tf_op jit(solution)/shard_map/all_to_all | solution.py:542
  35.4 4.3 %shard_map.75 = (f32[4,128,128]{2,1,0:T(8,128)S(1)}, f32[32,1,128]{2,1,0:T(1,128)}) custom-call(f32[32,4,128]{2,1,0:T(4,128)S(1)} %all_to_all.10.recv_ref, f32[2,128,128]{2,1,0:T(8,128)S(1)} %get-tuple-element.42.grad_ref, f32[8,128]{1,0:T(8,128)S(1)} %get-tuple-element.43.edge_ref, f32[4,128,128]{2,1,0:T(8,128)S(1)} %get-tuple-element.34.ctx_ref.ctx0_ref, ...), custom_call_target="tpu_custom_call" | custom-call | tf_op jit(solution)/shard_map/pallas_call | solution.py:543
  39.7 0.7 %collective-permute-start.8 = (f32[4,128,128]{2,1,0:T(8,128)S(1)}, f32[4,128,128]{2,1,0:T(8,128)S(1)}, u32[]{:S(2)}, u32[]{:S(2)}) collective-permute-start(f32[4,128,128]{2,1,0:T(8,128)S(1)} %get-tuple-element.45.rest_0_), channel_id=1, source_target_pairs={{0,16},{8,24},{16,0},{24,8},{1,17},{9,25},{17,1},{25,9},{2,18},{10... | collective-permute-start | bytes 786440 | tf_op jit(solution)/shard_map/ppermute | solution.py:506
  40.4 2.5 %all-to-all-start.1 = ((f32[32,1,128]{2,1,0:T(1,128)}), f32[32,1,128]{2,1,0:T(1,128)S(1)}, u32[]{:S(2)}, u32[]{:S(2)}) async-start(f32[32,1,128]{2,1,0:T(1,128)} %get-tuple-element.44), calls=%async_computation.1 | async-start | bytes 32768 | tf_op jit(solution)/shard_map/all_to_all | solution.py:555
  42.9 0.2 collective-permute-start.9
  43.1 6.9 %all-to-all-done.1.recv_ref = f32[32,1,128]{2,1,0:T(1,128)S(1)} async-done(((f32[32,1,128]{2,1,0:T(1,128)}), f32[32,1,128]{2,1,0:T(1,128)S(1)}, u32[]{:S(2)}, u32[]{:S(2)}) %all-to-all-start.1) | async-done | bytes 16416 | tf_op jit(solution)/shard_map/all_to_all | solution.py:555
  50.0 1.5 %collective-permute-done.10.rest_3_ = f32[4,128,128]{2,1,0:T(8,128)S(1)} collective-permute-done((f32[4,128,128]{2,1,0:T(8,128)S(1)}, f32[4,128,128]{2,1,0:T(8,128)S(1)}, u32[]{:S(2)}, u32[]{:S(2)}) %collective-permute-start.10) | collective-permute-done | bytes 262176 | tf_op jit(solution)/shard_map/ppermute | solution.py:506
  51.5 1.0 %shard_map.76 = (f32[128,512]{1,0:T(8,128)}, f32[128,512]{1,0:T(8,128)}) custom-call(f32[32,1,128]{2,1,0:T(1,128)S(1)} %all-to-all-done.1.recv_ref, f32[4,128,128]{2,1,0:T(8,128)S(1)} %get-tuple-element.45.rest_0_, f32[4,128,128]{2,1,0:T(8,128)S(1)} %collective-permute-done.9.rest_1_, f32[4,128,128]{2,1,0:T(8,128)S(1)} %collective-permute-done.8.rest_2_, ...), custom_call_target="tpu_custom_call" | custom-call | tf_op jit(solution)/shard_map/pallas_call | solution.py:559
  (21 shorter events, 0.1 us)
Async XLA Ops:
  0.6 0.7 %copy-start.3 = (s32[8,4]{0,1:T(4,128)S(1)}, s32[8,4]{0,1:T(4,128)}, u32[]{:S(2)}) copy-start(s32[8,4]{0,1:T(4,128)} %param.8) | copy-start | bytes 388
  1.3 4.7 %copy-start = (f32[128,512]{1,0:T(8,128)S(1)}, f32[128,512]{1,0:T(8,128)}, u32[]{:S(2)}) copy-start(f32[128,512]{1,0:T(8,128)} %depth_ref.3) | copy-start | bytes 786436
  1.3 4.7 %copy-start.1 = (f32[128,512]{1,0:T(8,128)S(1)}, f32[128,512]{1,0:T(8,128)}, u32[]{:S(2)}) copy-start(f32[128,512]{1,0:T(8,128)} %albedo_ref.3) | copy-start | bytes 786436
  1.3 4.7 %copy-start.2 = (s32[128,512]{1,0:T(8,128)S(1)}, s32[128,512]{1,0:T(8,128)}, u32[]{:S(2)}) copy-start(s32[128,512]{1,0:T(8,128)} %valid_ref.3) | copy-start | bytes 786436
  2.9 15.5 %collective-permute-start.2 = (bf16[1040,128]{1,0:T(8,128)(2,1)S(1)}, bf16[1040,128]{1,0:T(8,128)(2,1)S(1)}, u32[]{:S(2)}, u32[]{:S(2)}) collective-permute-start(bf16[1040,128]{1,0:T(8,128)(2,1)S(1)} %get-tuple-element.26.rest_1_), channel_id=1, source_target_pairs={{0,8},{8,0},{16,24},{24,16},{1,9},{9,1},{17,25},{25,17},{2,10},{10... | collective-permute-start | bytes 798728 | tf_op jit(solution)/shard_map/ppermute | solution.py:506
  3.4 16.9 %collective-permute-start.3 = (bf16[1040,128]{1,0:T(8,128)(2,1)S(1)}, bf16[1040,128]{1,0:T(8,128)(2,1)S(1)}, u32[]{:S(2)}, u32[]{:S(2)}) collective-permute-start(bf16[1040,128]{1,0:T(8,128)(2,1)S(1)} %get-tuple-element.27.rest_2_), channel_id=1, source_target_pairs={{0,16},{8,24},{16,0},{24,8},{1,17},{9,25},{17,1},{25,9},{2,18},{10... | collective-permute-start | bytes 798728 | tf_op jit(solution)/shard_map/ppermute | solution.py:506
  6.0 15.2 %collective-permute-start.4 = (bf16[1040,128]{1,0:T(8,128)(2,1)S(1)}, bf16[1040,128]{1,0:T(8,128)(2,1)S(1)}, u32[]{:S(2)}, u32[]{:S(2)}) collective-permute-start(bf16[1040,128]{1,0:T(8,128)(2,1)S(1)} %get-tuple-element.28.rest_3_), channel_id=1, source_target_pairs={{0,24},{8,16},{16,8},{24,0},{1,25},{9,17},{17,9},{25,1},{2,26},{10... | collective-permute-start | bytes 798728 | tf_op jit(solution)/shard_map/ppermute | solution.py:506
  7.3 5.1 %copy-start.4 = (s32[8,4]{0,1:T(4,128)S(1)}, s32[8,4]{0,1:T(4,128)}, u32[]{:S(2)}) copy-start(s32[8,4]{0,1:T(4,128)} %param.8) | copy-start | bytes 388
  7.3 5.2 %collective-permute-start = (f32[16,128]{1,0:T(8,128)S(1)}, f32[16,128]{1,0:T(8,128)S(1)}, u32[]{:S(2)}, u32[]{:S(2)}) collective-permute-start(f32[16,128]{1,0:T(8,128)S(1)} %get-tuple-element.31), channel_id=1, source_target_pairs={{0,1},{1,2},{2,3},{3,4},{4,5},{5,6},{6,7},{8,9},{9,10},{10,11},{11... | collective-permute-start | bytes 24584 | tf_op jit(solution)/shard_map/ppermute | solution.py:525
  11.1 5.5 %collective-permute-start.1 = (f32[16,128]{1,0:T(8,128)S(1)}, f32[16,128]{1,0:T(8,128)S(1)}, u32[]{:S(2)}, u32[]{:S(2)}) collective-permute-start(f32[16,128]{1,0:T(8,128)S(1)} %get-tuple-element.32), channel_id=1, source_target_pairs={{1,0},{2,1},{3,2},{4,3},{5,4},{6,5},{7,6},{9,8},{10,9},{11,10},{12... | collective-permute-start | bytes 24584 | tf_op jit(solution)/shard_map/ppermute | solution.py:526
  16.7 5.5 %collective-permute-start.5 = (f32[24,128]{1,0:T(8,128)S(1)}, f32[24,128]{1,0:T(8,128)S(1)}, u32[]{:S(2)}, u32[]{:S(2)}) collective-permute-start(f32[24,128]{1,0:T(8,128)S(1)} %get-tuple-element.38), channel_id=1, source_target_pairs={{0,8},{8,0},{16,24},{24,16},{1,9},{9,1},{17,25},{25,17},{2,10},{10... | collective-permute-start | bytes 36872 | tf_op jit(solution)/shard_map/ppermute | solution.py:506
  16.8 5.4 %collective-permute-start.6 = (f32[24,128]{1,0:T(8,128)S(1)}, f32[24,128]{1,0:T(8,128)S(1)}, u32[]{:S(2)}, u32[]{:S(2)}) collective-permute-start(f32[24,128]{1,0:T(8,128)S(1)} %get-tuple-element.39), channel_id=1, source_target_pairs={{0,16},{8,24},{16,0},{24,8},{1,17},{9,25},{17,1},{25,9},{2,18},{10... | collective-permute-start | bytes 36872 | tf_op jit(solution)/shard_map/ppermute | solution.py:506
  18.3 3.8 %collective-permute-start.7 = (f32[24,128]{1,0:T(8,128)S(1)}, f32[24,128]{1,0:T(8,128)S(1)}, u32[]{:S(2)}, u32[]{:S(2)}) collective-permute-start(f32[24,128]{1,0:T(8,128)S(1)} %get-tuple-element.40), channel_id=1, source_target_pairs={{0,24},{8,16},{16,8},{24,0},{1,25},{9,17},{17,9},{25,1},{2,26},{10... | collective-permute-start | bytes 36872 | tf_op jit(solution)/shard_map/ppermute | solution.py:506
  39.7 10.3 %collective-permute-start.8 = (f32[4,128,128]{2,1,0:T(8,128)S(1)}, f32[4,128,128]{2,1,0:T(8,128)S(1)}, u32[]{:S(2)}, u32[]{:S(2)}) collective-permute-start(f32[4,128,128]{2,1,0:T(8,128)S(1)} %get-tuple-element.45.rest_0_), channel_id=1, source_target_pairs={{0,16},{8,24},{16,0},{24,8},{1,17},{9,25},{17,1},{25,9},{2,18},{10... | collective-permute-start | bytes 786440 | tf_op jit(solution)/shard_map/ppermute | solution.py:506
  40.4 9.6 %all-to-all-start.1 = ((f32[32,1,128]{2,1,0:T(1,128)}), f32[32,1,128]{2,1,0:T(1,128)S(1)}, u32[]{:S(2)}, u32[]{:S(2)}) async-start(f32[32,1,128]{2,1,0:T(1,128)} %get-tuple-element.44), calls=%async_computation.1 | async-start | bytes 32768 | tf_op jit(solution)/shard_map/all_to_all | solution.py:555
  42.9 7.1 %collective-permute-start.9 = (f32[4,128,128]{2,1,0:T(8,128)S(1)}, f32[4,128,128]{2,1,0:T(8,128)S(1)}, u32[]{:S(2)}, u32[]{:S(2)}) collective-permute-start(f32[4,128,128]{2,1,0:T(8,128)S(1)} %get-tuple-element.45.rest_0_), channel_id=1, source_target_pairs={{0,8},{8,0},{16,24},{24,16},{1,9},{9,1},{17,25},{25,17},{2,10},{10... | collective-permute-start | bytes 786440 | tf_op jit(solution)/shard_map/ppermute | solution.py:506
  50.0 1.5 %collective-permute-start.10 = (f32[4,128,128]{2,1,0:T(8,128)S(1)}, f32[4,128,128]{2,1,0:T(8,128)S(1)}, u32[]{:S(2)}, u32[]{:S(2)}) collective-permute-start(f32[4,128,128]{2,1,0:T(8,128)S(1)} %collective-permute-done.8.rest_2_), channel_id=1, source_target_pairs={{0,8},{8,0},{16,24},{24,16},{1,9},{9,1},{17,25},{25,17},{2,10},{10... | collective-permute-start | bytes 786440 | tf_op jit(solution)/shard_map/ppermute | solution.py:506

commit v3 on v2

--- a/solution.py
+++ b/solution.py
@@ -17,6 +17,7 @@
 F32 = jnp.float32
 VM = pl.BlockSpec(memory_space=pltpu.VMEM)
 TR = 16
+CUT_VMEM = 40 << 20
 
 
 def iota(shape, dim):
@@ -44,22 +45,32 @@
     )
 
 
-def cut_body(nl, obs_ref, table_ref, *rest):
-    outs, (table, sems) = rest[:nl], rest[nl:]
+def cut_body(nl, obs_ref, table_ref, depth_ref, albedo_ref, valid_ref, *rest):
+    blocks, (tile_ref, surf_ref, sr_ref), (table, near, mask, sems, extra) = rest[:nl], rest[nl : nl + 3], rest[nl + 3 :]
     lights, rows, cols = obs_ref.shape
     w = cols // nl
     li = lax.axis_index("light")
+
+    def columns(q):
+        return pl.ds(pl.multiple_of(q * w, w), w)
+
+    fetch = pltpu.make_async_copy(table_ref, table, extra.at[0])
+    fetch.start()
+    sides = (jnp.maximum(li - 1, 0), li, jnp.minimum(li + 1, nl - 1))
+    edges = []
+    for f, (source, target) in enumerate(((depth_ref, near), (albedo_ref, near), (valid_ref, mask))):
+        for side, q in enumerate(sides):
+            slot = target.at[side] if f == 2 else target.at[f, side]
+            edges.append(pltpu.make_async_copy(source.at[:, columns(q)], slot, extra.at[1 + 3 * f + side]))
+            edges[-1].start()
     copies = []
     for k in (2, 3, 1, 0):
-        at = pl.ds(pl.multiple_of((li ^ k) * w, w), w)
         for l in range(lights):
             copy = pltpu.make_async_copy(
-                obs_ref.at[l, :, at], outs[k].at[pl.ds(l * rows, rows)], sems.at[k * lights + l]
+                obs_ref.at[l, :, columns(li ^ k)], blocks[k].at[pl.ds(l * rows, rows)], sems.at[k * lights + l]
             )
             copy.start()
             copies.append(copy)
-    fetch = pltpu.make_async_copy(table_ref, table, sems.at[nl * lights])
-    fetch.start()
     fetch.wait()
     entries = table[...]
     high = lax.shift_right_logical(entries, 5)
@@ -67,74 +78,58 @@
     wide = jnp.concatenate([both, jnp.zeros((8, w - lights), F32)], axis=1)
     under = jnp.concatenate([wide, jnp.zeros((8, w), F32)], axis=0).astype(jnp.bfloat16)
     for k in range(nl):
-        outs[k][pl.ds(lights * rows, 16), :] = under
+        blocks[k][pl.ds(lights * rows, 16), :] = under
+    for copy in edges:
+        copy.wait()
+    lane = iota((rows, w), 1)
+    is_last = li == nl - 1
+    surf_ref[...] = jnp.zeros_like(surf_ref)
+    sr_ref[...] = jnp.zeros_like(sr_ref)
+    for f in range(3):
+        before, own, after = (mask[s].astype(F32) if f == 2 else near[f, s] for s in range(3))
+        tile_ref[f] = own
+        inner = jnp.transpose(own)
+        outer = jnp.transpose(jnp.where(lane < w // 2, after, before))
+        low = jnp.where(li == 0, 0.0, outer[w - 2 : w])
+        high = jnp.where(is_last, 0.0, outer[0:2])
+        if f == 0:
+            sr_ref[0:2, :] = low
+            sr_ref[2:3, :] = inner[0:1]
+            sr_ref[3:4, :] = inner[w - 1 : w]
+            sr_ref[4:6, :] = high
+            surf_ref[0:2, :] = jnp.where(is_last, inner[w - 2 : w], inner[0:2])
+        else:
+            at = 4 + 2 * f
+            sr_ref[at : at + 1, :] = low[1:2]
+            sr_ref[at + 1 : at + 2, :] = high[0:1]
+            surf_ref[1 + f : 2 + f, :] = jnp.where(is_last, inner[w - 1 : w], inner[0:1])
     for copy in copies:
         copy.wait()
 
 
-def edges_body(nl, depth_ref, albedo_ref, valid_ref, *rest):
-    block_refs, (fwd_ref, bwd_ref, eh_ref, sr_ref) = rest[:nl], rest[nl:]
-    rows, cols = depth_ref.shape
-    w = cols // nl
-    lights = block_refs[0].shape[0] // rows
+def edges_body(nl, *rest):
+    block_refs, (fwd_ref, bwd_ref, eh_ref) = rest[:nl], rest[nl:]
+    w = block_refs[0].shape[1]
+    rows, n = eh_ref.shape[2], eh_ref.shape[1] // 2
     li = lax.axis_index("light")
-
-    def picks(columns, size):
-        pad = -len(columns) % 8
-        row = iota((len(columns) + pad, size), 0)
-        col = iota((len(columns) + pad, size), 1)
-        hit = jnp.zeros(row.shape, jnp.bool_)
-        for index, column in enumerate(columns):
-            hit = hit | ((row == index) & (col == column))
-        return hit.astype(F32)
-
-    ends, pairs = [], []
-    for q in range(nl):
-        ends += [q * w, q * w + w - 1]
-        pairs += [q * w, q * w + 1, q * w + w - 2, q * w + w - 1]
-    contract = (((1,), (1,)), ((), ()))
-    pick_ends = picks(ends, cols)
-    exact = dict(precision=lax.Precision.HIGHEST, preferred_element_type=F32)
-    depth = lax.dot_general(picks(pairs, cols), depth_ref[...], contract, **exact)
-    albedo = lax.dot_general(pick_ends, albedo_ref[...], contract, **exact)
-    valid = lax.dot_general(pick_ends, valid_ref[...].astype(F32), contract, **exact)
-    fwd_ref[...] = jnp.zeros_like(fwd_ref)
-    bwd_ref[...] = jnp.zeros_like(bwd_ref)
-    sr_ref[...] = jnp.zeros_like(sr_ref)
-    pick16 = picks([0, w - 1], w).astype(jnp.bfloat16)
+    at, col = iota((8, w), 0), iota((8, w), 1)
+    pick = (((at == 0) & (col == 0)) | ((at == 1) & (col == w - 1))).astype(jnp.bfloat16)
     for k in range(nl):
         q = li ^ k
-        for l in range(lights):
+        for l in range(n):
             e = lax.dot_general(
-                pick16, block_refs[k][pl.ds(l * rows, rows), :], contract, preferred_element_type=F32
+                pick,
+                block_refs[k][pl.ds(l * rows, rows), :],
+                (((1,), (1,)), ((), ())),
+                preferred_element_type=F32,
             )
-            eh_ref[q, lights + l : lights + l + 1, :] = e[0:1]
+            eh_ref[q, n + l : n + l + 1, :] = e[0:1]
             eh_ref[q + 2, l : l + 1, :] = e[1:2]
-    n = lights
-    last = 4 * (nl - 1)
-    bwd_ref[0:n, :] = eh_ref[0, n : 2 * n, :]
-    fwd_ref[0:n, :] = eh_ref[nl + 1, 0:n, :]
-    fwd_ref[n : n + 2, :] = depth[last + 2 : last + 4]
-    fwd_ref[n + 2 : n + 3, :] = albedo[2 * nl - 1 : 2 * nl]
-    fwd_ref[n + 3 : n + 4, :] = valid[2 * nl - 1 : 2 * nl]
-    bwd_ref[n : n + 2, :] = depth[0:2]
-    bwd_ref[n + 2 : n + 3, :] = albedo[0:1]
-    bwd_ref[n + 3 : n + 4, :] = valid[0:1]
-    for q in range(nl):
-        sr_ref[q, 2:3, :] = depth[4 * q : 4 * q + 1]
-        sr_ref[q, 3:4, :] = depth[4 * q + 3 : 4 * q + 4]
-        if q > 0:
-            sr_ref[q, 0:2, :] = depth[4 * q - 2 : 4 * q]
-            sr_ref[q, 6:7, :] = albedo[2 * q - 1 : 2 * q]
-            sr_ref[q, 8:9, :] = valid[2 * q - 1 : 2 * q]
-        if q < nl - 1:
-            sr_ref[q, 4:6, :] = depth[4 * q + 4 : 4 * q + 6]
-            sr_ref[q, 7:8, :] = albedo[2 * q + 2 : 2 * q + 3]
-            sr_ref[q, 9:10, :] = valid[2 * q + 2 : 2 * q + 3]
-
-
-def halos_body(nl, eh_ref, sr_ref, low_ref, high_ref, table_ref, *outs):
-    small_refs, own_ref = outs[:nl], outs[nl]
+    bwd_ref[...] = eh_ref[0, n : 2 * n, :]
+    fwd_ref[...] = eh_ref[nl + 1, 0:n, :]
+
+
+def halos_body(nl, eh_ref, low_ref, high_ref, table_ref, *small_refs):
     li = lax.axis_index("light")
     n = table_ref.shape[0]
     table = table_ref[...].astype(F32)
@@ -147,25 +142,11 @@
 
         @pl.when(q == 0)
         def _():
-            ref[0:n, :] = low_ref[0:n, :]
+            ref[0:n, :] = low_ref[...]
 
         @pl.when(q == nl - 1)
         def _():
-            ref[n : 2 * n, :] = high_ref[0:n, :]
-
-    own_ref[...] = sr_ref[li]
-
-    @pl.when(li == 0)
-    def _():
-        own_ref[0:2, :] = low_ref[n : n + 2, :]
-        own_ref[6:7, :] = low_ref[n + 2 : n + 3, :]
-        own_ref[8:9, :] = low_ref[n + 3 : n + 4, :]
-
-    @pl.when(li == nl - 1)
-    def _():
-        own_ref[4:6, :] = high_ref[n : n + 2, :]
-        own_ref[7:8, :] = high_ref[n + 2 : n + 3, :]
-        own_ref[9:10, :] = high_ref[n + 3 : n + 4, :]
+            ref[n : 2 * n, :] = high_ref[...]
 
 
 def decode(table):
@@ -376,14 +357,24 @@
     return lax.rsqrt(d / count + EPS), lax.rsqrt(a / count + EPS)
 
 
-def first_body(depth_ref, albedo_ref, valid_ref, srow_ref, obs0, obs1, ctx_ref, mask_ref, state_ref, pb_ref):
+def first_body(nl, tile_ref, sr_ref, surf_ref, obs0, obs1, ctx_ref, srow_ref, state_ref, pb_ref):
     li, _, place, count = position()
     rows, w = ctx_ref.shape[1:]
-    at = pl.ds(pl.multiple_of(li * w, w), w)
-    albedo = albedo_ref[:, at]
-    mask_ref[0] = albedo
-    mask_ref[1] = valid_ref[:, at].astype(F32)
-    fill_context(ctx_ref, depth_ref[:, at], albedo, srow_ref[1:2, :], srow_ref[4:5, :])
+    srow_ref[...] = sr_ref[...]
+
+    @pl.when(li == 0)
+    def _():
+        srow_ref[0:2, :] = surf_ref[0:2, :]
+        srow_ref[6:7, :] = surf_ref[2:3, :]
+        srow_ref[8:9, :] = surf_ref[3:4, :]
+
+    @pl.when(li == nl - 1)
+    def _():
+        srow_ref[4:6, :] = surf_ref[0:2, :]
+        srow_ref[7:8, :] = surf_ref[2:3, :]
+        srow_ref[9:10, :] = surf_ref[3:4, :]
+
+    fill_context(ctx_ref, tile_ref[0], tile_ref[1], srow_ref[1:2, :], srow_ref[4:5, :])
     total = w * count
     n = obs0.shape[0] // rows
     fill_params(pb_ref, 0, obs0, n, w, place, total)
@@ -429,21 +420,21 @@
     return depth, grad_albedo
 
 
-def last_body(nl, ctx_ref, mask_ref, state_ref, srow_ref, *rest):
+def last_body(nl, ctx_ref, tile_ref, state_ref, srow_ref, *rest):
     small_refs, (grad_ref, edge_ref, pay_ref) = rest[:nl], rest[nl:]
     edge_ref[...] = jnp.zeros_like(edge_ref)
-    finish(state_ref, ctx_ref, mask_ref[0], mask_ref[1], small_refs, srow_ref, grad_ref, edge_ref, pay_ref)
-
-
-def second_body(nl, recv_ref, grad_ref, edge_ref, ctx0_ref, mask_ref, srow0_ref, *rest):
+    finish(state_ref, ctx_ref, tile_ref[1], tile_ref[2], small_refs, srow_ref, grad_ref, edge_ref, pay_ref)
+
+
+def second_body(nl, recv_ref, grad_ref, edge_ref, tile_ref, srow0_ref, *rest):
     small_refs, obs_refs = rest[:nl], rest[nl : 2 * nl]
     out_ref, pay_ref, ctx_ref, state_ref, pb_ref, srow_ref = rest[2 * nl :]
     _, _, place, count = position()
     rows, w = ctx_ref.shape[1:]
     total = w * count
     inv_depth, inv_albedo = inverse_scales(recv_ref, 3, float(rows * total))
-    surface = ctx0_ref[0] - STEP_DEPTH * jnp.tanh(grad_ref[0] * inv_depth)
-    albedo = mask_ref[0] - STEP_ALBEDO * jnp.tanh(grad_ref[1] * inv_albedo)
+    surface = tile_ref[0] - STEP_DEPTH * jnp.tanh(grad_ref[0] * inv_depth)
+    albedo = tile_ref[1] - STEP_ALBEDO * jnp.tanh(grad_ref[1] * inv_albedo)
     out_ref[0] = surface
     out_ref[1] = albedo
     srow_ref[...] = jnp.zeros_like(srow_ref)
@@ -475,7 +466,7 @@
         fill_params(pb_ref, bases[k], obs_refs[k], n, w, place, total)
     sweep(ctx_ref, pb_ref, obs_refs, bases, total, lambda at: None, state_store(state_ref, w))
     depth, grad_albedo = finish(
-        state_ref, ctx_ref, albedo, mask_ref[1], small_refs, srow_ref, None, None, pay_ref
+        state_ref, ctx_ref, albedo, tile_ref[2], small_refs, srow_ref, None, None, pay_ref
     )
     out_ref[2] = depth
     out_ref[3] = grad_albedo
@@ -506,39 +497,47 @@
         return lax.ppermute(x, "light", [(i, i ^ k) for i in range(nl)])
 
     hbm = pl.BlockSpec(memory_space=pltpu.HBM)
-    blocks = call(
+    field = (rows, w)
+    whole = (observations, light_table.T, depth_start, albedo_start, valid_mask)
+    *blocks, tile, surf, sr = call(
         functools.partial(cut_body, nl),
-        tuple(shape(lights * rows + 16, w, dtype=jnp.bfloat16) for _ in range(nl)),
-        [pltpu.VMEM((4, lights), jnp.int32), pltpu.SemaphoreType.DMA((nl * lights + 1,))],
-        vmem=54_750_000,
-        in_specs=[hbm, hbm],
-    )(observations, light_table.T)
+        tuple(shape(lights * rows + 16, w, dtype=jnp.bfloat16) for _ in range(nl))
+        + (shape(3, *field), shape(8, rows), shape(16, rows)),
+        [
+            pltpu.VMEM((4, lights), jnp.int32),
+            pltpu.VMEM((2, 3, *field), F32),
+            pltpu.VMEM((3, *field), jnp.int32),
+            pltpu.SemaphoreType.DMA((nl * lights,)),
+            pltpu.SemaphoreType.DMA((10,)),
+        ],
+        vmem=CUT_VMEM,
+        in_specs=[hbm] * 5,
+    )(*(pltpu.with_memory_space_constraint(x, pltpu.HBM) for x in whole))
     obs2 = swap(blocks[2], 2)
     obs3 = swap(blocks[3], 3)
     obs1 = swap(blocks[1], 1)
     obs0 = blocks[0]
-    up = 2 * lights
-    fwd, bwd, eh, sr = call(
-        functools.partial(edges_body, nl),
-        (shape(up, rows), shape(up, rows), shape(nl + 2, up, rows), shape(nl, 16, rows)),
-    )(depth_start, albedo_start, valid_mask, *blocks)
+    up = [((nl - 1) * ns + i, i + 1) for i in range(ns - 1)]
+    surf = lax.ppermute(surf, AXES, up + [(target, source) for source, target in up])
+    fwd, bwd, eh = call(
+        functools.partial(edges_body, nl), (shape(lights, rows), shape(lights, rows), shape(nl + 2, 2 * lights, rows))
+    )(*blocks)
     low = lax.ppermute(fwd, "strip", [(i, i + 1) for i in range(ns - 1)])
     high = lax.ppermute(bwd, "strip", [(i + 1, i) for i in range(ns - 1)])
-    *small, srow = call(
-        functools.partial(halos_body, nl), tuple(shape(3 * lights, rows) for _ in range(nl)) + (shape(16, rows),)
-    )(eh, sr, low, high, light_table)
+    small = call(
+        functools.partial(halos_body, nl), tuple(shape(3 * lights, rows) for _ in range(nl))
+    )(eh, low, high, light_table)
     small = [small[0]] + [swap(small[k], k) for k in range(1, nl)]
 
     pb = pltpu.VMEM((2 * lights, 5, 8, w), F32)
-    field = (rows, w)
-    ctx, mask, state = call(
-        first_body, (shape(4, *field), shape(2, *field), shape(7, *field)), [pb]
-    )(depth_start, albedo_start, valid_mask, srow, obs0, obs1)
+    ctx, srow, state = call(
+        functools.partial(first_body, nl), (shape(4, *field), shape(16, rows), shape(7, *field)), [pb]
+    )(tile, sr, surf, obs0, obs1)
     state = call(more_body, shape(7, *field), [pb])(ctx, state, obs2)
     state = call(more_body, shape(7, *field), [pb])(ctx, state, obs3)
     grad, edge, pay = call(
         functools.partial(last_body, nl), (shape(2, *field), shape(8, rows), shape(nd, 4, rows))
-    )(ctx, mask, state, srow, *small)
+    )(ctx, tile, state, srow, *small)
     recv = lax.all_to_all(pay, AXES, 0, 0, tiled=True)
     own, pay = call(
         functools.partial(second_body, nl),
@@ -549,7 +548,7 @@
             pltpu.VMEM((nl * lights, 5, 8, w), F32),
             pltpu.VMEM((16, rows), F32),
         ],
-    )(recv, grad, edge, ctx, mask, srow, *small, obs0, obs1, obs2, obs3)
+    )(recv, grad, edge, tile, srow, *small, obs0, obs1, obs2, obs3)
     part2 = swap(own, 2)
     part1 = swap(own, 1)
     recv = lax.all_to_all(pay, AXES, 0, 0, tiled=True)

time: 52.8 us -> 54.5 us (1.032)
  starting transfers between devices: 13.6 us -> 17.1 us
  waiting for transfers between devices: 12.6 us -> 11.9 us
  local copies, waits for them, and re-layouts: 0.77 us -> 0.09 us
    ppermute x9, starting transfers between devices: 5.95 us -> 8.83 us  [swap(): return lax.ppermute(x, 'light', [(i, i ^ k) for i in range(nl)])]
    ppermute x1, waiting for transfers between devices: 4.15 us -> 3.43 us  [program(): high = lax.ppermute(bwd, 'strip', [(i + 1, i) for i in range(ns - 1)])]
    unnamed x11 -> x3, local copies, waits for them, and re-layouts: 0.77 us -> 0.09 us
    ppermute x0 -> x1, starting transfers between devices: none -> 0.66 us  [program(): lax.ppermute(surf, AXES, up + [(target, source) for source, target in up])]
    pallas_call x2, Pallas kernels: 2.9 us -> 2.26 us  [the longest x1 1.62 us: program(): call(functools.partial(first_body, nl), (shape(4, *field), shape(16, rows...]
  transfers between devices with their start and end apart: 12 -> 13, of which waited for: 3 -> 3; matrix products, arithmetic and copies ran while one was open for 0% -> 0% of each run, Pallas kernels for 9% -> 8%
where the time goes in v3:
time: 54.5 us; the launch traced here: 54.2 us
  starting transfers between devices  17.1 us (31%)
  blocking collectives  12.5 us (23%)
  waiting for transfers between devices  11.9 us (22%)
  Pallas kernels  11.8 us (22%)
  between operations  0.78 us (1%)
    all_to_all x1, blocking collectives, program(): recv = lax.all_to_all(pay, AXES, 0, 0, tiled=True)  12.5 us
    ppermute x9, starting transfers between devices, swap(): return lax.ppermute(x, 'light', [(i, i ^ k) for i in range(nl)])  8.83 us
    all_to_all x1, waiting for transfers between devices, program(): recv = lax.all_to_all(pay, AXES, 0, 0, tiled=True)  6.89 us
    pallas_call x1, Pallas kernels, program(): call(functools.partial(second_body, nl), (shape(4, *field), shape(nd, 1,...  4.27 us
    ppermute x1, starting transfers between devices, program(): low = lax.ppermute(fwd, 'strip', [(i, i + 1) for i in range(ns - 1)])  3.82 us
    ppermute x1, waiting for transfers between devices, program(): high = lax.ppermute(bwd, 'strip', [(i + 1, i) for i in range(ns - 1)])  3.43 us
    all_to_all x1, starting transfers between devices, program(): recv = lax.all_to_all(pay, AXES, 0, 0, tiled=True)  2.54 us
    pallas_call x1, Pallas kernels, program(): call(functools.partial(cut_body, nl), tuple((shape(lights * rows + 16, w,...  2.07 us
  transfers between devices with their start and end apart: 13, of which 3 were waited for; matrix products, arithmetic and copies ran while one was open for 0% of the time, Pallas kernels for 8%

profile of v3, /device:TPU:0, one launch (start us, length us, event | category | flops | bytes accessed | tf_op | source)
XLA Modules:
  0.0 54.2 jit_solution(2590160360872904700)
XLA Ops:
  0.6 2.1 %shard_map.68 = (bf16[1040,128]{1,0:T(8,128)(2,1)S(1)}, bf16[1040,128]{1,0:T(8,128)(2,1)S(1)}, bf16[1040,128]{1,0:T(8,128)(2,1)S(1)}, bf16[1040,128]{1,0:T(8,128...) custom-call(bf16[8,128,512]{2,1,0:T(8,128)(2,1)} %obs_ref.1, s32[4,8]{1,0:T(4,128)} %bitcast.1, ...), custom_call_target="tpu_custom_call" | custom-call | tf_op jit(solution)/shard_map/pallas_call | solution.py:502
  2.7 0.6 %collective-permute-start.1 = (bf16[1040,128]{1,0:T(8,128)(2,1)S(1)}, bf16[1040,128]{1,0:T(8,128)(2,1)S(1)}, u32[]{:S(2)}, u32[]{:S(2)}) collective-permute-start(bf16[1040,128]{1,0:T(8,128)(2,1)S(1)} %get-tuple-element.30.rest_1_), channel_id=1, source_target_pairs={{0,8},{8,0},{16,24},{24,16},{1,9},{9,1},{17,25},{25,17},{2,10},{10... | collective-permute-start | bytes 798728 | tf_op jit(solution)/shard_map/ppermute | solution.py:497
  3.3 2.6 %collective-permute-start.2 = (bf16[1040,128]{1,0:T(8,128)(2,1)S(1)}, bf16[1040,128]{1,0:T(8,128)(2,1)S(1)}, u32[]{:S(2)}, u32[]{:S(2)}) collective-permute-start(bf16[1040,128]{1,0:T(8,128)(2,1)S(1)} %get-tuple-element.33.rest_2_), channel_id=1, source_target_pairs={{0,16},{8,24},{16,0},{24,8},{1,17},{9,25},{17,1},{25,9},{2,18},{10... | collective-permute-start | bytes 798728 | tf_op jit(solution)/shard_map/ppermute | solution.py:497
  5.9 0.6 %shard_map.72 = (f32[8,128]{1,0:T(8,128)S(1)}, f32[8,128]{1,0:T(8,128)S(1)}, f32[6,16,128]{2,1,0:T(8,128)S(1)}) custom-call(bf16[1040,128]{1,0:T(8,128)(2,1)S(1)} %get-tuple-element.29.obs0.rest_0_.rest_4_, bf16[1040,128]{1,0:T(8,128)(2,1)S(1)} %get-tuple-element.30.rest_1_, bf16[1040,128]{1,0:T(8,128)(2,1)S(1)} %get-tuple-element.33.rest_2_, ...), custom_call_target="tpu_custom_call" | custom-call | tf_op jit(solution)/shard_map/pallas_call | solution.py:522
  6.5 3.8 %collective-permute-start.4 = (f32[8,128]{1,0:T(8,128)S(1)}, f32[8,128]{1,0:T(8,128)S(1)}, u32[]{:S(2)}, u32[]{:S(2)}) collective-permute-start(f32[8,128]{1,0:T(8,128)S(1)} %get-tuple-element.37), channel_id=1, source_target_pairs={{0,1},{1,2},{2,3},{3,4},{4,5},{5,6},{6,7},{8,9},{9,10},{10,11},{11... | collective-permute-start | bytes 12296 | tf_op jit(solution)/shard_map/ppermute | solution.py:525
  10.3 1.3 %collective-permute-start.5 = (f32[8,128]{1,0:T(8,128)S(1)}, f32[8,128]{1,0:T(8,128)S(1)}, u32[]{:S(2)}, u32[]{:S(2)}) collective-permute-start(f32[8,128]{1,0:T(8,128)S(1)} %get-tuple-element.38), channel_id=1, source_target_pairs={{1,0},{2,1},{3,2},{4,3},{5,4},{6,5},{7,6},{9,8},{10,9},{11,10},{12... | collective-permute-start | bytes 12296 | tf_op jit(solution)/shard_map/ppermute | solution.py:526
  11.6 0.7 %collective-permute-start = (f32[8,128]{1,0:T(8,128)S(1)}, f32[8,128]{1,0:T(8,128)S(1)}, u32[]{:S(2)}, u32[]{:S(2)}) collective-permute-start(f32[8,128]{1,0:T(8,128)S(1)} %get-tuple-element.28), channel_id=1, source_target_pairs={{24,1},{25,2},{26,3},{27,4},{28,5},{29,6},{30,7},{1,24},{2,25},{3,... | collective-permute-start | bytes 12296 | tf_op jit(solution)/shard_map/ppermute | solution.py:521
  12.3 0.1 copy.7.table_ref
  12.4 3.4 %collective-permute-done.5.high_ref = f32[8,128]{1,0:T(8,128)S(1)} collective-permute-done((f32[8,128]{1,0:T(8,128)S(1)}, f32[8,128]{1,0:T(8,128)S(1)}, u32[]{:S(2)}, u32[]{:S(2)}) %collective-permute-start.5) | collective-permute-done | bytes 4128 | tf_op jit(solution)/shard_map/ppermute | solution.py:526
  15.9 0.1 collective-permute-start.6
  15.9 2.0 %collective-permute-start.7 = (f32[24,128]{1,0:T(8,128)S(1)}, f32[24,128]{1,0:T(8,128)S(1)}, u32[]{:S(2)}, u32[]{:S(2)}) collective-permute-start(f32[24,128]{1,0:T(8,128)S(1)} %get-tuple-element.41), channel_id=1, source_target_pairs={{0,16},{8,24},{16,0},{24,8},{1,17},{9,25},{17,1},{25,9},{2,18},{10... | collective-permute-start | bytes 36872 | tf_op jit(solution)/shard_map/ppermute | solution.py:497
  18.0 2.7 %collective-permute-start.8 = (f32[24,128]{1,0:T(8,128)S(1)}, f32[24,128]{1,0:T(8,128)S(1)}, u32[]{:S(2)}, u32[]{:S(2)}) collective-permute-start(f32[24,128]{1,0:T(8,128)S(1)} %get-tuple-element.42), channel_id=1, source_target_pairs={{0,24},{8,16},{16,8},{24,0},{1,25},{9,17},{17,9},{25,1},{2,26},{10... | collective-permute-start | bytes 36872 | tf_op jit(solution)/shard_map/ppermute | solution.py:497
  20.7 1.6 %shard_map.69 = (f32[4,128,128]{2,1,0:T(8,128)S(1)}, f32[16,128]{1,0:T(8,128)S(1)}, f32[7,128,128]{2,1,0:T(8,128)S(1)}) custom-call(f32[3,128,128]{2,1,0:T(8,128)S(1)} %get-tuple-element.26.tile_ref, f32[16,128]{1,0:T(8,128)S(1)} %get-tuple-element.27.sr_ref, f32[8,128]{1,0:T(8,128)S(1)} %collective-permute-done.surf_ref, ...), custom_call_target="tpu_custom_call" | custom-call | tf_op jit(solution)/shard_map/pallas_call | solution.py:533
  22.3 0.9 %shard_map.70.in_ref = f32[7,128,128]{2,1,0:T(8,128)S(1)} custom-call(f32[4,128,128]{2,1,0:T(8,128)S(1)} %get-tuple-element.31.ctx_ref, f32[7,128,128]{2,1,0:T(8,128)S(1)} %get-tuple-element.32.in_ref, bf16[1040,128]{1,0:T(8,128)(2,1)S(1)} %collective-permute-done.2.obs.rest_6_), custom_call_target="tpu_custom_call" | custom-call | tf_op jit(solution)/shard_map/pallas_call | solution.py:536
  23.2 0.9 %shard_map.71.state_ref = f32[7,128,128]{2,1,0:T(8,128)S(1)} custom-call(f32[4,128,128]{2,1,0:T(8,128)S(1)} %get-tuple-element.31.ctx_ref, f32[7,128,128]{2,1,0:T(8,128)S(1)} %shard_map.70.in_ref, bf16[1040,128]{1,0:T(8,128)(2,1)S(1)} %collective-permute-done.3.obs.rest_7_), custom_call_target="tpu_custom_call" | custom-call | tf_op jit(solution)/shard_map/pallas_call | solution.py:537
  24.2 0.4 shard_map.74
  24.6 12.5 %all_to_all.10.recv_ref = f32[32,4,128]{2,1,0:T(4,128)S(1)} all-to-all(f32[32,4,128]{2,1,0:T(4,128)S(1)} %get-tuple-element.43), channel_id=1, replica_groups=mesh['light'=4,'strip'=8] {'light','strip'}, dimensions={0} | all-to-all | bytes 131072 | tf_op jit(solution)/shard_map/all_to_all | solution.py:541
  37.1 4.3 %shard_map.75 = (f32[4,128,128]{2,1,0:T(8,128)S(1)}, f32[32,1,128]{2,1,0:T(1,128)}) custom-call(f32[32,4,128]{2,1,0:T(4,128)S(1)} %all_to_all.10.recv_ref, f32[2,128,128]{2,1,0:T(8,128)S(1)} %get-tuple-element.44.grad_ref, f32[8,128]{1,0:T(8,128)S(1)} %get-tuple-element.45.edge_ref, f32[3,128,128]{2,1,0:T(8,128)S(1)} %get-tuple-element.26.tile_ref, ...), custom_call_target="tpu_custom_call" | custom-call | tf_op jit(solution)/shard_map/pallas_call | solution.py:542
  41.4 0.7 %collective-permute-start.9 = (f32[4,128,128]{2,1,0:T(8,128)S(1)}, f32[4,128,128]{2,1,0:T(8,128)S(1)}, u32[]{:S(2)}, u32[]{:S(2)}) collective-permute-start(f32[4,128,128]{2,1,0:T(8,128)S(1)} %get-tuple-element.47.rest_0_), channel_id=1, source_target_pairs={{0,16},{8,24},{16,0},{24,8},{1,17},{9,25},{17,1},{25,9},{2,18},{10... | collective-permute-start | bytes 786440 | tf_op jit(solution)/shard_map/ppermute | solution.py:497
  42.1 2.5 %all-to-all-start.1 = ((f32[32,1,128]{2,1,0:T(1,128)}), f32[32,1,128]{2,1,0:T(1,128)S(1)}, u32[]{:S(2)}, u32[]{:S(2)}) async-start(f32[32,1,128]{2,1,0:T(1,128)} %get-tuple-element.46), calls=%async_computation.1 | async-start | bytes 32768 | tf_op jit(solution)/shard_map/all_to_all | solution.py:554
  44.6 0.2 collective-permute-start.10
  44.8 6.9 %all-to-all-done.1.recv_ref = f32[32,1,128]{2,1,0:T(1,128)S(1)} async-done(((f32[32,1,128]{2,1,0:T(1,128)}), f32[32,1,128]{2,1,0:T(1,128)S(1)}, u32[]{:S(2)}, u32[]{:S(2)}) %all-to-all-start.1) | async-done | bytes 16416 | tf_op jit(solution)/shard_map/all_to_all | solution.py:554
  51.7 1.5 %collective-permute-done.11.rest_3_ = f32[4,128,128]{2,1,0:T(8,128)S(1)} collective-permute-done((f32[4,128,128]{2,1,0:T(8,128)S(1)}, f32[4,128,128]{2,1,0:T(8,128)S(1)}, u32[]{:S(2)}, u32[]{:S(2)}) %collective-permute-start.11) | collective-permute-done | bytes 262176 | tf_op jit(solution)/shard_map/ppermute | solution.py:497
  53.2 1.0 %shard_map.76 = (f32[128,512]{1,0:T(8,128)}, f32[128,512]{1,0:T(8,128)}) custom-call(f32[32,1,128]{2,1,0:T(1,128)S(1)} %all-to-all-done.1.recv_ref, f32[4,128,128]{2,1,0:T(8,128)S(1)} %get-tuple-element.47.rest_0_, f32[4,128,128]{2,1,0:T(8,128)S(1)} %collective-permute-done.10.rest_1_, f32[4,128,128]{2,1,0:T(8,128)S(1)} %collective-permute-done.9.rest_2_, ...), custom_call_target="tpu_custom_call" | custom-call | tf_op jit(solution)/shard_map/pallas_call | solution.py:558
  (15 shorter events, 0.1 us)
Async XLA Ops:
  2.7 15.3 %collective-permute-start.1 = (bf16[1040,128]{1,0:T(8,128)(2,1)S(1)}, bf16[1040,128]{1,0:T(8,128)(2,1)S(1)}, u32[]{:S(2)}, u32[]{:S(2)}) collective-permute-start(bf16[1040,128]{1,0:T(8,128)(2,1)S(1)} %get-tuple-element.30.rest_1_), channel_id=1, source_target_pairs={{0,8},{8,0},{16,24},{24,16},{1,9},{9,1},{17,25},{25,17},{2,10},{10... | collective-permute-start | bytes 798728 | tf_op jit(solution)/shard_map/ppermute | solution.py:497
  3.3 19.1 %collective-permute-start.2 = (bf16[1040,128]{1,0:T(8,128)(2,1)S(1)}, bf16[1040,128]{1,0:T(8,128)(2,1)S(1)}, u32[]{:S(2)}, u32[]{:S(2)}) collective-permute-start(bf16[1040,128]{1,0:T(8,128)(2,1)S(1)} %get-tuple-element.33.rest_2_), channel_id=1, source_target_pairs={{0,16},{8,24},{16,0},{24,8},{1,17},{9,25},{17,1},{25,9},{2,18},{10... | collective-permute-start | bytes 798728 | tf_op jit(solution)/shard_map/ppermute | solution.py:497
  5.8 17.4 %collective-permute-start.3 = (bf16[1040,128]{1,0:T(8,128)(2,1)S(1)}, bf16[1040,128]{1,0:T(8,128)(2,1)S(1)}, u32[]{:S(2)}, u32[]{:S(2)}) collective-permute-start(bf16[1040,128]{1,0:T(8,128)(2,1)S(1)} %get-tuple-element.34.rest_3_), channel_id=1, source_target_pairs={{0,24},{8,16},{16,8},{24,0},{1,25},{9,17},{17,9},{25,1},{2,26},{10... | collective-permute-start | bytes 798728 | tf_op jit(solution)/shard_map/ppermute | solution.py:497
  6.5 5.8 %copy-start = (s32[8,4]{0,1:T(4,128)S(1)}, s32[8,4]{0,1:T(4,128)}, u32[]{:S(2)}) copy-start(s32[8,4]{0,1:T(4,128)} %param.8) | copy-start | bytes 388
  6.5 5.1 %collective-permute-start.4 = (f32[8,128]{1,0:T(8,128)S(1)}, f32[8,128]{1,0:T(8,128)S(1)}, u32[]{:S(2)}, u32[]{:S(2)}) collective-permute-start(f32[8,128]{1,0:T(8,128)S(1)} %get-tuple-element.37), channel_id=1, source_target_pairs={{0,1},{1,2},{2,3},{3,4},{4,5},{5,6},{6,7},{8,9},{9,10},{10,11},{11... | collective-permute-start | bytes 12296 | tf_op jit(solution)/shard_map/ppermute | solution.py:525
  10.3 5.5 %collective-permute-start.5 = (f32[8,128]{1,0:T(8,128)S(1)}, f32[8,128]{1,0:T(8,128)S(1)}, u32[]{:S(2)}, u32[]{:S(2)}) collective-permute-start(f32[8,128]{1,0:T(8,128)S(1)} %get-tuple-element.38), channel_id=1, source_target_pairs={{1,0},{2,1},{3,2},{4,3},{5,4},{6,5},{7,6},{9,8},{10,9},{11,10},{12... | collective-permute-start | bytes 12296 | tf_op jit(solution)/shard_map/ppermute | solution.py:526
  11.6 4.3 %collective-permute-start = (f32[8,128]{1,0:T(8,128)S(1)}, f32[8,128]{1,0:T(8,128)S(1)}, u32[]{:S(2)}, u32[]{:S(2)}) collective-permute-start(f32[8,128]{1,0:T(8,128)S(1)} %get-tuple-element.28), channel_id=1, source_target_pairs={{24,1},{25,2},{26,3},{27,4},{28,5},{29,6},{30,7},{1,24},{2,25},{3,... | collective-permute-start | bytes 12296 | tf_op jit(solution)/shard_map/ppermute | solution.py:521
  15.9 8.3 %collective-permute-start.6 = (f32[24,128]{1,0:T(8,128)S(1)}, f32[24,128]{1,0:T(8,128)S(1)}, u32[]{:S(2)}, u32[]{:S(2)}) collective-permute-start(f32[24,128]{1,0:T(8,128)S(1)} %get-tuple-element.40), channel_id=1, source_target_pairs={{0,8},{8,0},{16,24},{24,16},{1,9},{9,1},{17,25},{25,17},{2,10},{10... | collective-permute-start | bytes 36872 | tf_op jit(solution)/shard_map/ppermute | solution.py:497
  15.9 8.2 %collective-permute-start.7 = (f32[24,128]{1,0:T(8,128)S(1)}, f32[24,128]{1,0:T(8,128)S(1)}, u32[]{:S(2)}, u32[]{:S(2)}) collective-permute-start(f32[24,128]{1,0:T(8,128)S(1)} %get-tuple-element.41), channel_id=1, source_target_pairs={{0,16},{8,24},{16,0},{24,8},{1,17},{9,25},{17,1},{25,9},{2,18},{10... | collective-permute-start | bytes 36872 | tf_op jit(solution)/shard_map/ppermute | solution.py:497
  18.0 6.2 %collective-permute-start.8 = (f32[24,128]{1,0:T(8,128)S(1)}, f32[24,128]{1,0:T(8,128)S(1)}, u32[]{:S(2)}, u32[]{:S(2)}) collective-permute-start(f32[24,128]{1,0:T(8,128)S(1)} %get-tuple-element.42), channel_id=1, source_target_pairs={{0,24},{8,16},{16,8},{24,0},{1,25},{9,17},{17,9},{25,1},{2,26},{10... | collective-permute-start | bytes 36872 | tf_op jit(solution)/shard_map/ppermute | solution.py:497
  41.4 10.3 %collective-permute-start.9 = (f32[4,128,128]{2,1,0:T(8,128)S(1)}, f32[4,128,128]{2,1,0:T(8,128)S(1)}, u32[]{:S(2)}, u32[]{:S(2)}) collective-permute-start(f32[4,128,128]{2,1,0:T(8,128)S(1)} %get-tuple-element.47.rest_0_), channel_id=1, source_target_pairs={{0,16},{8,24},{16,0},{24,8},{1,17},{9,25},{17,1},{25,9},{2,18},{10... | collective-permute-start | bytes 786440 | tf_op jit(solution)/shard_map/ppermute | solution.py:497
  42.1 9.6 %all-to-all-start.1 = ((f32[32,1,128]{2,1,0:T(1,128)}), f32[32,1,128]{2,1,0:T(1,128)S(1)}, u32[]{:S(2)}, u32[]{:S(2)}) async-start(f32[32,1,128]{2,1,0:T(1,128)} %get-tuple-element.46), calls=%async_computation.1 | async-start | bytes 32768 | tf_op jit(solution)/shard_map/all_to_all | solution.py:554
  44.6 7.1 %collective-permute-start.10 = (f32[4,128,128]{2,1,0:T(8,128)S(1)}, f32[4,128,128]{2,1,0:T(8,128)S(1)}, u32[]{:S(2)}, u32[]{:S(2)}) collective-permute-start(f32[4,128,128]{2,1,0:T(8,128)S(1)} %get-tuple-element.47.rest_0_), channel_id=1, source_target_pairs={{0,8},{8,0},{16,24},{24,16},{1,9},{9,1},{17,25},{25,17},{2,10},{10... | collective-permute-start | bytes 786440 | tf_op jit(solution)/shard_map/ppermute | solution.py:497
  51.7 1.5 %collective-permute-start.11 = (f32[4,128,128]{2,1,0:T(8,128)S(1)}, f32[4,128,128]{2,1,0:T(8,128)S(1)}, u32[]{:S(2)}, u32[]{:S(2)}) collective-permute-start(f32[4,128,128]{2,1,0:T(8,128)S(1)} %collective-permute-done.9.rest_2_), channel_id=1, source_target_pairs={{0,8},{8,0},{16,24},{24,16},{1,9},{9,1},{17,25},{25,17},{2,10},{10... | collective-permute-start | bytes 786440 | tf_op jit(solution)/shard_map/ppermute | solution.py:497

commit v4 on v3

--- a/solution.py
+++ b/solution.py
@@ -17,7 +17,6 @@
 F32 = jnp.float32
 VM = pl.BlockSpec(memory_space=pltpu.VMEM)
 TR = 16
-CUT_VMEM = 40 << 20
 
 
 def iota(shape, dim):
@@ -45,8 +44,16 @@
     )
 
 
+UNDER = 16
+
+
+def block_rows(lights, rows, k):
+    return lights * rows + UNDER + 2 * lights + (2 * lights if k == 1 else 0)
+
+
 def cut_body(nl, obs_ref, table_ref, depth_ref, albedo_ref, valid_ref, *rest):
-    blocks, (tile_ref, surf_ref, sr_ref), (table, near, mask, sems, extra) = rest[:nl], rest[nl : nl + 3], rest[nl + 3 :]
+    blocks, (tile_ref, surf_ref, sr_ref, end_ref) = rest[:nl], rest[nl : nl + 4]
+    table, near, mask, eh_ref, sems, extra = rest[nl + 4 :]
     lights, rows, cols = obs_ref.shape
     w = cols // nl
     li = lax.axis_index("light")
@@ -54,99 +61,86 @@
     def columns(q):
         return pl.ds(pl.multiple_of(q * w, w), w)
 
+    order = (2, 3, 1, 0)
+    copies = {}
+    for k in order:
+        for l in range(lights):
+            copies[k, l] = pltpu.make_async_copy(
+                obs_ref.at[l, :, columns(li ^ k)], blocks[k].at[pl.ds(l * rows, rows)], sems.at[k * lights + l]
+            )
+            copies[k, l].start()
     fetch = pltpu.make_async_copy(table_ref, table, extra.at[0])
     fetch.start()
-    sides = (jnp.maximum(li - 1, 0), li, jnp.minimum(li + 1, nl - 1))
+    right = lax.rem(li, 2) == 0
+    sides = (jnp.maximum(li - 1, 0), li, jnp.minimum(li + 1, nl - 1), jnp.where(right, nl - 1, 0))
     edges = []
     for f, (source, target) in enumerate(((depth_ref, near), (albedo_ref, near), (valid_ref, mask))):
         for side, q in enumerate(sides):
             slot = target.at[side] if f == 2 else target.at[f, side]
-            edges.append(pltpu.make_async_copy(source.at[:, columns(q)], slot, extra.at[1 + 3 * f + side]))
+            edges.append(pltpu.make_async_copy(source.at[:, columns(q)], slot, extra.at[1 + 4 * f + side]))
             edges[-1].start()
-    copies = []
-    for k in (2, 3, 1, 0):
-        for l in range(lights):
-            copy = pltpu.make_async_copy(
-                obs_ref.at[l, :, columns(li ^ k)], blocks[k].at[pl.ds(l * rows, rows)], sems.at[k * lights + l]
-            )
-            copy.start()
-            copies.append(copy)
     fetch.wait()
     entries = table[...]
     high = lax.shift_right_logical(entries, 5)
     both = jnp.concatenate([high, entries - high * 32], axis=0).astype(F32)
     wide = jnp.concatenate([both, jnp.zeros((8, w - lights), F32)], axis=1)
-    under = jnp.concatenate([wide, jnp.zeros((8, w), F32)], axis=0).astype(jnp.bfloat16)
+    under = jnp.concatenate([wide, jnp.zeros((UNDER - 8, w), F32)], axis=0).astype(jnp.bfloat16)
     for k in range(nl):
-        blocks[k][pl.ds(lights * rows, 16), :] = under
+        blocks[k][pl.ds(lights * rows, UNDER), :] = under
+    eh_ref[...] = jnp.zeros_like(eh_ref)
+    at, col = iota((8, w), 0), iota((8, w), 1)
+    pick = (((at == 0) & (col == 0)) | ((at == 1) & (col == w - 1))).astype(jnp.bfloat16)
+    for k in order:
+        q = li ^ k
+        for l in range(lights):
+            copies[k, l].wait()
+            e = lax.dot_general(
+                pick,
+                blocks[k][pl.ds(l * rows, rows), :],
+                (((1,), (1,)), ((), ())),
+                preferred_element_type=F32,
+            )
+            eh_ref[q, lights + l : lights + l + 1, :] = e[0:1]
+            eh_ref[q + 2, l : l + 1, :] = e[1:2]
+    ends = jnp.concatenate([eh_ref[nl + 1, 0:lights, :], eh_ref[0, lights:, :]], axis=0)
+    end_ref[...] = ends
+    halo = pl.ds(lights * rows + UNDER, 2 * lights)
+    for k in range(nl):
+        blocks[k][halo, :] = eh_ref[(li ^ k) + 1].astype(jnp.bfloat16)
+    blocks[1][pl.ds(lights * rows + UNDER + 2 * lights, 2 * lights), :] = ends.astype(jnp.bfloat16)
     for copy in edges:
         copy.wait()
     lane = iota((rows, w), 1)
-    is_last = li == nl - 1
     surf_ref[...] = jnp.zeros_like(surf_ref)
     sr_ref[...] = jnp.zeros_like(sr_ref)
     for f in range(3):
-        before, own, after = (mask[s].astype(F32) if f == 2 else near[f, s] for s in range(3))
+        before, own, after, edge = (mask[s].astype(F32) if f == 2 else near[f, s] for s in range(4))
         tile_ref[f] = own
         inner = jnp.transpose(own)
         outer = jnp.transpose(jnp.where(lane < w // 2, after, before))
+        edge = jnp.transpose(edge)
         low = jnp.where(li == 0, 0.0, outer[w - 2 : w])
-        high = jnp.where(is_last, 0.0, outer[0:2])
+        high = jnp.where(li == nl - 1, 0.0, outer[0:2])
         if f == 0:
             sr_ref[0:2, :] = low
             sr_ref[2:3, :] = inner[0:1]
             sr_ref[3:4, :] = inner[w - 1 : w]
             sr_ref[4:6, :] = high
-            surf_ref[0:2, :] = jnp.where(is_last, inner[w - 2 : w], inner[0:2])
+            surf_ref[0:2, :] = jnp.where(right, edge[w - 2 : w], edge[0:2])
         else:
             at = 4 + 2 * f
             sr_ref[at : at + 1, :] = low[1:2]
             sr_ref[at + 1 : at + 2, :] = high[0:1]
-            surf_ref[1 + f : 2 + f, :] = jnp.where(is_last, inner[w - 1 : w], inner[0:1])
-    for copy in copies:
-        copy.wait()
-
-
-def edges_body(nl, *rest):
-    block_refs, (fwd_ref, bwd_ref, eh_ref) = rest[:nl], rest[nl:]
-    w = block_refs[0].shape[1]
-    rows, n = eh_ref.shape[2], eh_ref.shape[1] // 2
-    li = lax.axis_index("light")
-    at, col = iota((8, w), 0), iota((8, w), 1)
-    pick = (((at == 0) & (col == 0)) | ((at == 1) & (col == w - 1))).astype(jnp.bfloat16)
-    for k in range(nl):
-        q = li ^ k
-        for l in range(n):
-            e = lax.dot_general(
-                pick,
-                block_refs[k][pl.ds(l * rows, rows), :],
-                (((1,), (1,)), ((), ())),
-                preferred_element_type=F32,
-            )
-            eh_ref[q, n + l : n + l + 1, :] = e[0:1]
-            eh_ref[q + 2, l : l + 1, :] = e[1:2]
-    bwd_ref[...] = eh_ref[0, n : 2 * n, :]
-    fwd_ref[...] = eh_ref[nl + 1, 0:n, :]
-
-
-def halos_body(nl, eh_ref, low_ref, high_ref, table_ref, *small_refs):
-    li = lax.axis_index("light")
-    n = table_ref.shape[0]
-    table = table_ref[...].astype(F32)
-    for k in range(nl):
-        q = li ^ k
-        ref = small_refs[k]
-        ref[0 : 2 * n, :] = eh_ref[q + 1]
-        ref[2 * n :, :] = jnp.zeros((ref.shape[0] - 2 * n, ref.shape[1]), F32)
-        ref[2 * n : 3 * n, 0:4] = table
-
-        @pl.when(q == 0)
-        def _():
-            ref[0:n, :] = low_ref[...]
-
-        @pl.when(q == nl - 1)
-        def _():
-            ref[n : 2 * n, :] = high_ref[...]
+            surf_ref[1 + f : 2 + f, :] = jnp.where(right, edge[w - 1 : w], edge[0:1])
+
+
+def join_body(block_ref, end_ref, surf_ref, out_ref):
+    n = end_ref.shape[0] // 2
+    other = block_ref[pl.ds(block_ref.shape[0] - 2 * n, 2 * n), :].astype(F32)
+    right = lax.rem(lax.axis_index("light"), 2) == 0
+    out_ref[0:n, :] = jnp.where(right, end_ref[0:n, :], end_ref[n:, :])
+    out_ref[n : 2 * n, :] = jnp.where(right, other[0:n], other[n:])
+    out_ref[2 * n :, :] = surf_ref[...]
 
 
 def decode(table):
@@ -201,9 +195,17 @@
     ctx_ref[3] = albedo * lax.rsqrt(1.0 + sx * sx + sy * sy)
 
 
-def fill_params(pb_ref, base, block_ref, n, w, place, total):
-    under = block_ref[pl.ds(block_ref.shape[0] - 16, 16), :].astype(F32)
-    lx, ly, lz, le = decode_rows(under[0:4] * 32.0 + under[4:8])
+def lights_of(block_ref, rows):
+    return block_ref.shape[0] // rows
+
+
+def table_rows(block_ref, n, rows):
+    under = block_ref[pl.ds(n * rows, UNDER), :].astype(F32)
+    return under[0:4] * 32.0 + under[4:8]
+
+
+def fill_params(pb_ref, base, block_ref, n, rows, w, place, total):
+    lx, ly, lz, le = decode_rows(table_rows(block_ref, n, rows))
     col = iota((8, w), 1) + place * w
     px = (col.astype(F32) + 0.5) / total - 0.5
     for j in range(n):
@@ -250,7 +252,7 @@
 
 def sweep(ctx_ref, pb_ref, obs_refs, bases, total, load, store):
     rows, w = ctx_ref.shape[1:]
-    lights = obs_refs[0].shape[0] // rows
+    lights = lights_of(obs_refs[0], rows)
     split = (TR // 8, 8, w)
 
     def step(i, carry):
@@ -283,11 +285,9 @@
     return store
 
 
-def halo_slope(column, side, small_refs, srow_ref, rows, total):
-    n = small_refs[0].shape[0] // 3
-    obs = jnp.concatenate([ref[side * n : (side + 1) * n, :] for ref in small_refs], axis=0)
-    table = jnp.concatenate([ref[2 * n : 3 * n, :] for ref in small_refs], axis=0)
-    lx, ly, lz, le = decode(table)
+def halo_slope(column, side, pack_ref, srow_ref, rows, total):
+    obs = pack_ref[side]
+    lx, ly, lz, le = decode(pack_ref[2])
     outer, inner = (0, 2) if side == 0 else (5, 3)
     here = 1 if side == 0 else 4
     surface = srow_ref[here : here + 1, :]
@@ -357,28 +357,29 @@
     return lax.rsqrt(d / count + EPS), lax.rsqrt(a / count + EPS)
 
 
-def first_body(nl, tile_ref, sr_ref, surf_ref, obs0, obs1, ctx_ref, srow_ref, state_ref, pb_ref):
+def first_body(nl, tile_ref, sr_ref, strip_ref, obs0, obs1, ctx_ref, srow_ref, state_ref, pb_ref):
     li, _, place, count = position()
     rows, w = ctx_ref.shape[1:]
     srow_ref[...] = sr_ref[...]
+    at = strip_ref.shape[0] - 8
 
     @pl.when(li == 0)
     def _():
-        srow_ref[0:2, :] = surf_ref[0:2, :]
-        srow_ref[6:7, :] = surf_ref[2:3, :]
-        srow_ref[8:9, :] = surf_ref[3:4, :]
+        srow_ref[0:2, :] = strip_ref[at : at + 2, :]
+        srow_ref[6:7, :] = strip_ref[at + 2 : at + 3, :]
+        srow_ref[8:9, :] = strip_ref[at + 3 : at + 4, :]
 
     @pl.when(li == nl - 1)
     def _():
-        srow_ref[4:6, :] = surf_ref[0:2, :]
-        srow_ref[7:8, :] = surf_ref[2:3, :]
-        srow_ref[9:10, :] = surf_ref[3:4, :]
+        srow_ref[4:6, :] = strip_ref[at : at + 2, :]
+        srow_ref[7:8, :] = strip_ref[at + 2 : at + 3, :]
+        srow_ref[9:10, :] = strip_ref[at + 3 : at + 4, :]
 
     fill_context(ctx_ref, tile_ref[0], tile_ref[1], srow_ref[1:2, :], srow_ref[4:5, :])
     total = w * count
-    n = obs0.shape[0] // rows
-    fill_params(pb_ref, 0, obs0, n, w, place, total)
-    fill_params(pb_ref, n, obs1, n, w, place, total)
+    n = lights_of(obs0, rows)
+    fill_params(pb_ref, 0, obs0, n, rows, w, place, total)
+    fill_params(pb_ref, n, obs1, n, rows, w, place, total)
     sweep(ctx_ref, pb_ref, (obs0, obs1), (0, n), total, lambda at: None, state_store(state_ref, w))
 
 
@@ -386,16 +387,16 @@
     _, _, place, count = position()
     rows, w = ctx_ref.shape[1:]
     total = w * count
-    fill_params(pb_ref, 0, obs, obs.shape[0] // rows, w, place, total)
+    fill_params(pb_ref, 0, obs, lights_of(obs, rows), rows, w, place, total)
     sweep(ctx_ref, pb_ref, (obs,), (0,), total, state_load(in_ref, w), state_store(state_ref, w))
 
 
-def finish(state_ref, ctx_ref, albedo, valid, small_refs, srow_ref, grad_ref, edge_ref, pay_ref):
+def finish(state_ref, ctx_ref, albedo, valid, pack_ref, srow_ref, grad_ref, edge_ref, pay_ref):
     _, _, place, count = position()
     rows, w = ctx_ref.shape[1:]
     total = w * count
-    low = halo_slope(place * w - 1, 0, small_refs, srow_ref, rows, total)
-    high = halo_slope(place * w + w, 1, small_refs, srow_ref, rows, total)
+    low = halo_slope(place * w - 1, 0, pack_ref, srow_ref, rows, total)
+    high = halo_slope(place * w + w, 1, pack_ref, srow_ref, rows, total)
     depth, grad_albedo = gradients(state_ref, ctx_ref, albedo, valid, low, high)
     sums = partial_sums(depth, grad_albedo)
     if edge_ref is None:
@@ -420,15 +421,32 @@
     return depth, grad_albedo
 
 
-def last_body(nl, ctx_ref, tile_ref, state_ref, srow_ref, *rest):
-    small_refs, (grad_ref, edge_ref, pay_ref) = rest[:nl], rest[nl:]
+def fill_pack(nl, pack_ref, block_refs, direct_ref, relayed_ref, rows, w):
+    li = lax.axis_index("light")
+    n = lights_of(block_refs[0], rows)
+    table = jnp.zeros((4, w), F32)
+    for k in range(nl):
+        halo = block_refs[k][pl.ds(n * rows + UNDER, 2 * n), :].astype(F32)
+        beyond = (relayed_ref if k < 2 else direct_ref)[(k % 2) * n : (k % 2 + 1) * n, :]
+        pack_ref[0, k * n : (k + 1) * n, :] = jnp.where(li == 0, beyond, halo[0:n])
+        pack_ref[1, k * n : (k + 1) * n, :] = jnp.where(li == nl - 1, beyond, halo[n:])
+        entries = jnp.concatenate([table_rows(block_refs[k], n, rows)] * 2, axis=0)
+        table = table + (pltpu.roll(entries, k * n, 1) if k else entries)[0:4]
+    tall = jnp.concatenate([table, jnp.zeros((w - 4, w), F32)], axis=0)
+    pack_ref[2] = jnp.transpose(tall)[0 : nl * n]
+
+
+def last_body(nl, ctx_ref, tile_ref, state_ref, srow_ref, direct_ref, relayed_ref, *rest):
+    block_refs, (grad_ref, edge_ref, pay_ref, pack_ref) = rest[:nl], rest[nl:]
+    rows, w = ctx_ref.shape[1:]
+    fill_pack(nl, pack_ref, block_refs, direct_ref, relayed_ref, rows, w)
     edge_ref[...] = jnp.zeros_like(edge_ref)
-    finish(state_ref, ctx_ref, tile_ref[1], tile_ref[2], small_refs, srow_ref, grad_ref, edge_ref, pay_ref)
-
-
-def second_body(nl, recv_ref, grad_ref, edge_ref, tile_ref, srow0_ref, *rest):
-    small_refs, obs_refs = rest[:nl], rest[nl : 2 * nl]
-    out_ref, pay_ref, ctx_ref, state_ref, pb_ref, srow_ref = rest[2 * nl :]
+    finish(state_ref, ctx_ref, tile_ref[1], tile_ref[2], pack_ref, srow_ref, grad_ref, edge_ref, pay_ref)
+
+
+def second_body(nl, recv_ref, grad_ref, edge_ref, tile_ref, srow0_ref, pack_ref, *rest):
+    obs_refs = rest[:nl]
+    out_ref, pay_ref, ctx_ref, state_ref, pb_ref, srow_ref = rest[nl:]
     _, _, place, count = position()
     rows, w = ctx_ref.shape[1:]
     total = w * count
@@ -460,13 +478,13 @@
     srow_ref[0:8, :] = srow0_ref[0:8, :] - changes
     srow_ref[8:16, :] = srow0_ref[8:16, :]
     fill_context(ctx_ref, surface, albedo, srow_ref[1:2, :], srow_ref[4:5, :])
-    n = obs_refs[0].shape[0] // rows
+    n = lights_of(obs_refs[0], rows)
     bases = tuple(k * n for k in range(nl))
     for k in range(nl):
-        fill_params(pb_ref, bases[k], obs_refs[k], n, w, place, total)
+        fill_params(pb_ref, bases[k], obs_refs[k], n, rows, w, place, total)
     sweep(ctx_ref, pb_ref, obs_refs, bases, total, lambda at: None, state_store(state_ref, w))
     depth, grad_albedo = finish(
-        state_ref, ctx_ref, albedo, tile_ref[2], small_refs, srow_ref, None, None, pay_ref
+        state_ref, ctx_ref, albedo, tile_ref[2], pack_ref, srow_ref, None, None, pay_ref
     )
     out_ref[2] = depth
     out_ref[3] = grad_albedo
@@ -499,45 +517,41 @@
     hbm = pl.BlockSpec(memory_space=pltpu.HBM)
     field = (rows, w)
     whole = (observations, light_table.T, depth_start, albedo_start, valid_mask)
-    *blocks, tile, surf, sr = call(
+    *blocks, tile, surf, sr, end = call(
         functools.partial(cut_body, nl),
-        tuple(shape(lights * rows + 16, w, dtype=jnp.bfloat16) for _ in range(nl))
-        + (shape(3, *field), shape(8, rows), shape(16, rows)),
+        tuple(shape(block_rows(lights, rows, k), w, dtype=jnp.bfloat16) for k in range(nl))
+        + (shape(3, *field), shape(8, rows), shape(16, rows), shape(2 * lights, rows)),
         [
             pltpu.VMEM((4, lights), jnp.int32),
-            pltpu.VMEM((2, 3, *field), F32),
-            pltpu.VMEM((3, *field), jnp.int32),
+            pltpu.VMEM((2, 4, *field), F32),
+            pltpu.VMEM((4, *field), jnp.int32),
+            pltpu.VMEM((nl + 2, 2 * lights, rows), F32),
             pltpu.SemaphoreType.DMA((nl * lights,)),
-            pltpu.SemaphoreType.DMA((10,)),
+            pltpu.SemaphoreType.DMA((13,)),
         ],
-        vmem=CUT_VMEM,
         in_specs=[hbm] * 5,
     )(*(pltpu.with_memory_space_constraint(x, pltpu.HBM) for x in whole))
     obs2 = swap(blocks[2], 2)
     obs3 = swap(blocks[3], 3)
     obs1 = swap(blocks[1], 1)
     obs0 = blocks[0]
-    up = [((nl - 1) * ns + i, i + 1) for i in range(ns - 1)]
-    surf = lax.ppermute(surf, AXES, up + [(target, source) for source, target in up])
-    fwd, bwd, eh = call(
-        functools.partial(edges_body, nl), (shape(lights, rows), shape(lights, rows), shape(nl + 2, 2 * lights, rows))
-    )(*blocks)
-    low = lax.ppermute(fwd, "strip", [(i, i + 1) for i in range(ns - 1)])
-    high = lax.ppermute(bwd, "strip", [(i + 1, i) for i in range(ns - 1)])
-    small = call(
-        functools.partial(halos_body, nl), tuple(shape(3 * lights, rows) for _ in range(nl))
-    )(eh, low, high, light_table)
-    small = [small[0]] + [swap(small[k], k) for k in range(1, nl)]
+    strip = call(join_body, shape(2 * lights + 8, rows))(obs1, end, surf)
+    pairs = []
+    for i in range(ns - 1):
+        pairs += [(2 * ns + i, i + 1), (i, ns + i + 1), (ns + i + 1, 3 * ns + i), (3 * ns + i + 1, 2 * ns + i)]
+    direct = lax.ppermute(strip, AXES, pairs)
+    relayed = swap(direct, 1)
 
     pb = pltpu.VMEM((2 * lights, 5, 8, w), F32)
     ctx, srow, state = call(
         functools.partial(first_body, nl), (shape(4, *field), shape(16, rows), shape(7, *field)), [pb]
-    )(tile, sr, surf, obs0, obs1)
+    )(tile, sr, direct, obs0, obs1)
     state = call(more_body, shape(7, *field), [pb])(ctx, state, obs2)
     state = call(more_body, shape(7, *field), [pb])(ctx, state, obs3)
-    grad, edge, pay = call(
-        functools.partial(last_body, nl), (shape(2, *field), shape(8, rows), shape(nd, 4, rows))
-    )(ctx, tile, state, srow, *small)
+    grad, edge, pay, pack = call(
+        functools.partial(last_body, nl),
+        (shape(2, *field), shape(8, rows), shape(nd, 4, rows), shape(3, nl * lights, rows)),
+    )(ctx, tile, state, srow, direct, relayed, obs0, obs1, obs2, obs3)
     recv = lax.all_to_all(pay, AXES, 0, 0, tiled=True)
     own, pay = call(
         functools.partial(second_body, nl),
@@ -548,7 +562,7 @@
             pltpu.VMEM((nl * lights, 5, 8, w), F32),
             pltpu.VMEM((16, rows), F32),
         ],
-    )(recv, grad, edge, tile, srow, *small, obs0, obs1, obs2, obs3)
+    )(recv, grad, edge, tile, srow, pack, obs0, obs1, obs2, obs3)
     part2 = swap(own, 2)
     part1 = swap(own, 1)
     recv = lax.all_to_all(pay, AXES, 0, 0, tiled=True)

time: 54.5 us -> 57.2 us (1.050)
  starting transfers between devices: 17.1 us -> 10.2 us
  Pallas kernels: 11.8 us -> 15.7 us
  blocking collectives: 12.5 us -> 15.6 us
  waiting for transfers between devices: 11.9 us -> 14.8 us
    ppermute x9 -> x7, waiting for transfers between devices: 1.55 us -> 6.51 us  [swap(): return lax.ppermute(x, 'light', [(i, i ^ k) for i in range(nl)])]
    ppermute x9 -> x7, starting transfers between devices: 8.83 us -> 4.03 us  [swap(): return lax.ppermute(x, 'light', [(i, i ^ k) for i in range(nl)])]
    pallas_call x3 -> x2, Pallas kernels: 2.73 us -> 6.43 us  [the longest x1 6.43 us: program(): call(functools.partial(cut_body, nl), tuple((shape(block_rows(lights, row...]
    all_to_all x1, blocking collectives: 12.5 us -> 15.6 us  [program(): recv = lax.all_to_all(pay, AXES, 0, 0, tiled=True)]
    ppermute x3 -> x1, starting transfers between devices: 5.77 us -> 3.63 us  [program(): direct = lax.ppermute(strip, AXES, pairs)]
    ppermute x3 -> x1, waiting for transfers between devices: 3.44 us -> 1.39 us  [program(): direct = lax.ppermute(strip, AXES, pairs)]
  transfers between devices with their start and end apart: 13 -> 9, of which waited for: 3 -> 5; matrix products, arithmetic and copies ran while one was open for 0% -> 0% of each run, Pallas kernels for 8% -> 6%
where the time goes in v4:
time: 57.2 us; the launch traced here: 57 us
  Pallas kernels  15.7 us (27%)
  blocking collectives  15.6 us (27%)
  waiting for transfers between devices  14.8 us (26%)
  starting transfers between devices  10.2 us (18%)
  between operations  0.7 us (1%)
    all_to_all x1, blocking collectives, program(): recv = lax.all_to_all(pay, AXES, 0, 0, tiled=True)  15.6 us
    all_to_all x1, waiting for transfers between devices, program(): recv = lax.all_to_all(pay, AXES, 0, 0, tiled=True)  6.89 us
    ppermute x7, waiting for transfers between devices, swap(): return lax.ppermute(x, 'light', [(i, i ^ k) for i in range(nl)])  6.51 us
    pallas_call x1, Pallas kernels, program(): call(functools.partial(cut_body, nl), tuple((shape(block_rows(lights, row...  6.43 us
    pallas_call x1, Pallas kernels, program(): call(functools.partial(second_body, nl), (shape(4, *field), shape(nd, 1,...  4.27 us
    ppermute x7, starting transfers between devices, swap(): return lax.ppermute(x, 'light', [(i, i ^ k) for i in range(nl)])  4.03 us
    ppermute x1, starting transfers between devices, program(): direct = lax.ppermute(strip, AXES, pairs)  3.63 us
    all_to_all x1, starting transfers between devices, program(): recv = lax.all_to_all(pay, AXES, 0, 0, tiled=True)  2.54 us
  transfers between devices with their start and end apart: 9, of which 5 were waited for; matrix products, arithmetic and copies ran while one was open for 0% of the time, Pallas kernels for 6%

profile of v4, /device:TPU:0, one launch (start us, length us, event | category | flops | bytes accessed | tf_op | source)
XLA Modules:
  0.0 57.0 jit_solution(1315971613372608963)
XLA Ops:
  0.6 6.4 %shard_map.68 = (bf16[1056,128]{1,0:T(8,128)(2,1)S(1)}, bf16[1072,128]{1,0:T(8,128)(2,1)S(1)}, bf16[1056,128]{1,0:T(8,128)(2,1)S(1)}, bf16[1056,128]{1,0:T(8,128...) custom-call(bf16[8,128,512]{2,1,0:T(8,128)(2,1)} %obs_ref.1, ...), custom_call_target="tpu_custom_call" | custom-call | tf_op jit(solution)/shard_map/pallas_call | solution.py:520
  7.1 0.6 collective-permute-start
  7.6 2.6 %collective-permute-start.2 = (bf16[1056,128]{1,0:T(8,128)(2,1)S(1)}, bf16[1056,128]{1,0:T(8,128)(2,1)S(1)}, u32[]{:S(2)}, u32[]{:S(2)}) collective-permute-start(bf16[1056,128]{1,0:T(8,128)(2,1)S(1)} %get-tuple-element.29), channel_id=1, source_target_pairs={{0,16},{8,24},{16,0},{24,8},{1,17},{9,25},{17,1},{25,9},{2,18},{10... | collective-permute-start | bytes 811016 | tf_op jit(solution)/shard_map/ppermute | solution.py:515
  10.2 0.0 collective-permute-start.3
  10.2 0.0 collective-permute-done.block_ref.obs1.rest_1_
  10.2 3.6 %collective-permute-start.1 = (f32[24,128]{1,0:T(8,128)S(1)}, f32[24,128]{1,0:T(8,128)S(1)}, u32[]{:S(2)}, u32[]{:S(2)}) collective-permute-start(f32[24,128]{1,0:T(8,128)S(1)} %shard_map.69), channel_id=1, source_target_pairs={{16,1},{0,9},{9,24},{25,16},{17,2},{1,10},{10,25},{26,17},{18,3},{... | collective-permute-start | bytes 36872 | tf_op jit(solution)/shard_map/ppermute | solution.py:542
  13.9 1.4 %collective-permute-done.1.strip_ref.direct_ref = f32[24,128]{1,0:T(8,128)S(1)} collective-permute-done((f32[24,128]{1,0:T(8,128)S(1)}, f32[24,128]{1,0:T(8,128)S(1)}, u32[]{:S(2)}, u32[]{:S(2)}) %collective-permute-start.1) | collective-permute-done | bytes 12320 | tf_op jit(solution)/shard_map/ppermute | solution.py:542
  15.3 1.6 %shard_map.70 = (f32[4,128,128]{2,1,0:T(8,128)S(1)}, f32[16,128]{1,0:T(8,128)S(1)}, f32[7,128,128]{2,1,0:T(8,128)S(1)}) custom-call(f32[3,128,128]{2,1,0:T(8,128)S(1)} %get-tuple-element.21.tile_ref, f32[16,128]{1,0:T(8,128)S(1)} %get-tuple-element.22.sr_ref, f32[24,128]{1,0:T(8,128)S(1)} %collective-permute-done.1.strip_ref.direct_ref, ...), custom_call_target="tpu_custom_call" | custom-call | tf_op jit(solution)/shard_map/pallas_call | solution.py:546
  16.9 0.6 %collective-permute-done.2.obs.rest_2_ = bf16[1056,128]{1,0:T(8,128)(2,1)S(1)} collective-permute-done((bf16[1056,128]{1,0:T(8,128)(2,1)S(1)}, bf16[1056,128]{1,0:T(8,128)(2,1)S(1)}, u32[]{:S(2)}, u32[]{:S(2)}) %collective-permute-start.2) | collective-permute-done | bytes 270368 | tf_op jit(solution)/shard_map/ppermute | solution.py:515
  17.5 0.9 %shard_map.71.in_ref = f32[7,128,128]{2,1,0:T(8,128)S(1)} custom-call(f32[4,128,128]{2,1,0:T(8,128)S(1)} %get-tuple-element.27.ctx_ref, f32[7,128,128]{2,1,0:T(8,128)S(1)} %get-tuple-element.28.in_ref, bf16[1056,128]{1,0:T(8,128)(2,1)S(1)} %collective-permute-done.2.obs.rest_2_), custom_call_target="tpu_custom_call" | custom-call | tf_op jit(solution)/shard_map/pallas_call | solution.py:549
  18.4 4.3 %collective-permute-done.3.obs.rest_3_ = bf16[1056,128]{1,0:T(8,128)(2,1)S(1)} collective-permute-done((bf16[1056,128]{1,0:T(8,128)(2,1)S(1)}, bf16[1056,128]{1,0:T(8,128)(2,1)S(1)}, u32[]{:S(2)}, u32[]{:S(2)}) %collective-permute-start.3) | collective-permute-done | bytes 270368 | tf_op jit(solution)/shard_map/ppermute | solution.py:515
  22.8 0.9 %shard_map.72.state_ref = f32[7,128,128]{2,1,0:T(8,128)S(1)} custom-call(f32[4,128,128]{2,1,0:T(8,128)S(1)} %get-tuple-element.27.ctx_ref, f32[7,128,128]{2,1,0:T(8,128)S(1)} %shard_map.71.in_ref, bf16[1056,128]{1,0:T(8,128)(2,1)S(1)} %collective-permute-done.3.obs.rest_3_), custom_call_target="tpu_custom_call" | custom-call | tf_op jit(solution)/shard_map/pallas_call | solution.py:550
  23.7 0.0 collective-permute-done.4.relayed_ref
  23.7 0.5 shard_map.73
  24.2 15.6 %all_to_all.10.recv_ref = f32[32,4,128]{2,1,0:T(4,128)S(1)} all-to-all(f32[32,4,128]{2,1,0:T(4,128)S(1)} %get-tuple-element.32), channel_id=1, replica_groups=mesh['light'=4,'strip'=8] {'light','strip'}, dimensions={0} | all-to-all | bytes 131072 | tf_op jit(solution)/shard_map/all_to_all | solution.py:555
  39.8 4.3 %shard_map.74 = (f32[4,128,128]{2,1,0:T(8,128)S(1)}, f32[32,1,128]{2,1,0:T(1,128)}) custom-call(f32[32,4,128]{2,1,0:T(4,128)S(1)} %all_to_all.10.recv_ref, f32[2,128,128]{2,1,0:T(8,128)S(1)} %get-tuple-element.33.grad_ref, f32[8,128]{1,0:T(8,128)S(1)} %get-tuple-element.34.edge_ref, f32[3,128,128]{2,1,0:T(8,128)S(1)} %get-tuple-element.21.tile_ref, ...), custom_call_target="tpu_custom_call" | custom-call | tf_op jit(solution)/shard_map/pallas_call | solution.py:556
  44.1 0.7 %collective-permute-start.5 = (f32[4,128,128]{2,1,0:T(8,128)S(1)}, f32[4,128,128]{2,1,0:T(8,128)S(1)}, u32[]{:S(2)}, u32[]{:S(2)}) collective-permute-start(f32[4,128,128]{2,1,0:T(8,128)S(1)} %get-tuple-element.37.rest_0_), channel_id=1, source_target_pairs={{0,16},{8,24},{16,0},{24,8},{1,17},{9,25},{17,1},{25,9},{2,18},{10... | collective-permute-start | bytes 786440 | tf_op jit(solution)/shard_map/ppermute | solution.py:515
  44.8 2.5 %all-to-all-start.1 = ((f32[32,1,128]{2,1,0:T(1,128)}), f32[32,1,128]{2,1,0:T(1,128)S(1)}, u32[]{:S(2)}, u32[]{:S(2)}) async-start(f32[32,1,128]{2,1,0:T(1,128)} %get-tuple-element.36), calls=%async_computation.1 | async-start | bytes 32768 | tf_op jit(solution)/shard_map/all_to_all | solution.py:568
  47.3 0.2 collective-permute-start.6
  47.5 6.9 %all-to-all-done.1.recv_ref = f32[32,1,128]{2,1,0:T(1,128)S(1)} async-done(((f32[32,1,128]{2,1,0:T(1,128)}), f32[32,1,128]{2,1,0:T(1,128)S(1)}, u32[]{:S(2)}, u32[]{:S(2)}) %all-to-all-start.1) | async-done | bytes 16416 | tf_op jit(solution)/shard_map/all_to_all | solution.py:568
  54.4 0.0 collective-permute-start.7
  54.4 0.0 collective-permute-done.6.rest_1_
  54.4 1.5 %collective-permute-done.7.rest_3_ = f32[4,128,128]{2,1,0:T(8,128)S(1)} collective-permute-done((f32[4,128,128]{2,1,0:T(8,128)S(1)}, f32[4,128,128]{2,1,0:T(8,128)S(1)}, u32[]{:S(2)}, u32[]{:S(2)}) %collective-permute-start.7) | collective-permute-done | bytes 262176 | tf_op jit(solution)/shard_map/ppermute | solution.py:515
  55.9 1.0 %shard_map.75 = (f32[128,512]{1,0:T(8,128)}, f32[128,512]{1,0:T(8,128)}) custom-call(f32[32,1,128]{2,1,0:T(1,128)S(1)} %all-to-all-done.1.recv_ref, f32[4,128,128]{2,1,0:T(8,128)S(1)} %get-tuple-element.37.rest_0_, f32[4,128,128]{2,1,0:T(8,128)S(1)} %collective-permute-done.6.rest_1_, f32[4,128,128]{2,1,0:T(8,128)S(1)} %collective-permute-done.5.rest_2_, ...), custom_call_target="tpu_custom_call" | custom-call | tf_op jit(solution)/shard_map/pallas_call | solution.py:572
  (3 shorter events, 0.0 us)
Async XLA Ops:
  7.1 3.2 %collective-permute-start = (bf16[1072,128]{1,0:T(8,128)(2,1)S(1)}, bf16[1072,128]{1,0:T(8,128)(2,1)S(1)}, u32[]{:S(2)}, u32[]{:S(2)}) collective-permute-start(bf16[1072,128]{1,0:T(8,128)(2,1)S(1)} %get-tuple-element.23), channel_id=1, source_target_pairs={{0,8},{8,0},{16,24},{24,16},{1,9},{9,1},{17,25},{25,17},{2,10},{10... | collective-permute-start | bytes 823304 | tf_op jit(solution)/shard_map/ppermute | solution.py:515
  7.6 9.9 %collective-permute-start.2 = (bf16[1056,128]{1,0:T(8,128)(2,1)S(1)}, bf16[1056,128]{1,0:T(8,128)(2,1)S(1)}, u32[]{:S(2)}, u32[]{:S(2)}) collective-permute-start(bf16[1056,128]{1,0:T(8,128)(2,1)S(1)} %get-tuple-element.29), channel_id=1, source_target_pairs={{0,16},{8,24},{16,0},{24,8},{1,17},{9,25},{17,1},{25,9},{2,18},{10... | collective-permute-start | bytes 811016 | tf_op jit(solution)/shard_map/ppermute | solution.py:515
  10.2 12.6 %collective-permute-start.3 = (bf16[1056,128]{1,0:T(8,128)(2,1)S(1)}, bf16[1056,128]{1,0:T(8,128)(2,1)S(1)}, u32[]{:S(2)}, u32[]{:S(2)}) collective-permute-start(bf16[1056,128]{1,0:T(8,128)(2,1)S(1)} %get-tuple-element.30), channel_id=1, source_target_pairs={{0,24},{8,16},{16,8},{24,0},{1,25},{9,17},{17,9},{25,1},{2,26},{10... | collective-permute-start | bytes 811016 | tf_op jit(solution)/shard_map/ppermute | solution.py:515
  10.2 5.0 %collective-permute-start.1 = (f32[24,128]{1,0:T(8,128)S(1)}, f32[24,128]{1,0:T(8,128)S(1)}, u32[]{:S(2)}, u32[]{:S(2)}) collective-permute-start(f32[24,128]{1,0:T(8,128)S(1)} %shard_map.69), channel_id=1, source_target_pairs={{16,1},{0,9},{9,24},{25,16},{17,2},{1,10},{10,25},{26,17},{18,3},{... | collective-permute-start | bytes 36872 | tf_op jit(solution)/shard_map/ppermute | solution.py:542
  15.2 8.4 %collective-permute-start.4 = (f32[24,128]{1,0:T(8,128)S(1)}, f32[24,128]{1,0:T(8,128)S(1)}, u32[]{:S(2)}, u32[]{:S(2)}) collective-permute-start(f32[24,128]{1,0:T(8,128)S(1)} %collective-permute-done.1.strip_ref.direct_ref), channel_id=1, source_target_pairs={{0,8},{8,0},{16,24},{24,16},{1,9},{9,1},{17,25},{25,17},{2,10},{10... | collective-permute-start | bytes 36872 | tf_op jit(solution)/shard_map/ppermute | solution.py:515
  44.1 10.3 %collective-permute-start.5 = (f32[4,128,128]{2,1,0:T(8,128)S(1)}, f32[4,128,128]{2,1,0:T(8,128)S(1)}, u32[]{:S(2)}, u32[]{:S(2)}) collective-permute-start(f32[4,128,128]{2,1,0:T(8,128)S(1)} %get-tuple-element.37.rest_0_), channel_id=1, source_target_pairs={{0,16},{8,24},{16,0},{24,8},{1,17},{9,25},{17,1},{25,9},{2,18},{10... | collective-permute-start | bytes 786440 | tf_op jit(solution)/shard_map/ppermute | solution.py:515
  44.8 9.6 %all-to-all-start.1 = ((f32[32,1,128]{2,1,0:T(1,128)}), f32[32,1,128]{2,1,0:T(1,128)S(1)}, u32[]{:S(2)}, u32[]{:S(2)}) async-start(f32[32,1,128]{2,1,0:T(1,128)} %get-tuple-element.36), calls=%async_computation.1 | async-start | bytes 32768 | tf_op jit(solution)/shard_map/all_to_all | solution.py:568
  47.3 7.1 %collective-permute-start.6 = (f32[4,128,128]{2,1,0:T(8,128)S(1)}, f32[4,128,128]{2,1,0:T(8,128)S(1)}, u32[]{:S(2)}, u32[]{:S(2)}) collective-permute-start(f32[4,128,128]{2,1,0:T(8,128)S(1)} %get-tuple-element.37.rest_0_), channel_id=1, source_target_pairs={{0,8},{8,0},{16,24},{24,16},{1,9},{9,1},{17,25},{25,17},{2,10},{10... | collective-permute-start | bytes 786440 | tf_op jit(solution)/shard_map/ppermute | solution.py:515
  54.4 1.5 %collective-permute-start.7 = (f32[4,128,128]{2,1,0:T(8,128)S(1)}, f32[4,128,128]{2,1,0:T(8,128)S(1)}, u32[]{:S(2)}, u32[]{:S(2)}) collective-permute-start(f32[4,128,128]{2,1,0:T(8,128)S(1)} %collective-permute-done.5.rest_2_), channel_id=1, source_target_pairs={{0,8},{8,0},{16,24},{24,16},{1,9},{9,1},{17,25},{25,17},{2,10},{10... | collective-permute-start | bytes 786440 | tf_op jit(solution)/shard_map/ppermute | solution.py:515

commit v5 on v4

--- a/solution.py
+++ b/solution.py
@@ -51,34 +51,26 @@
     return lights * rows + UNDER + 2 * lights + (2 * lights if k == 1 else 0)
 
 
-def cut_body(nl, obs_ref, table_ref, depth_ref, albedo_ref, valid_ref, *rest):
-    blocks, (tile_ref, surf_ref, sr_ref, end_ref) = rest[:nl], rest[nl : nl + 4]
-    table, near, mask, eh_ref, sems, extra = rest[nl + 4 :]
+def cut_body(nl, obs_ref, table_ref, *rest):
+    blocks, (end_ref, table, eh_ref, sems, extra) = rest[:nl], rest[nl:]
     lights, rows, cols = obs_ref.shape
     w = cols // nl
     li = lax.axis_index("light")
-
-    def columns(q):
-        return pl.ds(pl.multiple_of(q * w, w), w)
-
-    order = (2, 3, 1, 0)
-    copies = {}
-    for k in order:
+    copies = []
+    for k in (2, 3, 1, 0):
         for l in range(lights):
-            copies[k, l] = pltpu.make_async_copy(
-                obs_ref.at[l, :, columns(li ^ k)], blocks[k].at[pl.ds(l * rows, rows)], sems.at[k * lights + l]
+            at = pl.ds(pl.multiple_of((li ^ k) * w, w), w)
+            copies.append(
+                pltpu.make_async_copy(
+                    obs_ref.at[l, :, at], blocks[k].at[pl.ds(l * rows, rows)], sems.at[k * lights + l]
+                )
             )
-            copies[k, l].start()
+            copies[-1].start()
     fetch = pltpu.make_async_copy(table_ref, table, extra.at[0])
     fetch.start()
-    right = lax.rem(li, 2) == 0
-    sides = (jnp.maximum(li - 1, 0), li, jnp.minimum(li + 1, nl - 1), jnp.where(right, nl - 1, 0))
-    edges = []
-    for f, (source, target) in enumerate(((depth_ref, near), (albedo_ref, near), (valid_ref, mask))):
-        for side, q in enumerate(sides):
-            slot = target.at[side] if f == 2 else target.at[f, side]
-            edges.append(pltpu.make_async_copy(source.at[:, columns(q)], slot, extra.at[1 + 4 * f + side]))
-            edges[-1].start()
+    eh_ref[...] = jnp.zeros_like(eh_ref)
+    at, col = iota((8, w), 0), iota((8, w), 1)
+    pick = (((at == 0) & (col == 0)) | ((at == 1) & (col == w - 1))).astype(jnp.bfloat16)
     fetch.wait()
     entries = table[...]
     high = lax.shift_right_logical(entries, 5)
@@ -87,13 +79,11 @@
     under = jnp.concatenate([wide, jnp.zeros((UNDER - 8, w), F32)], axis=0).astype(jnp.bfloat16)
     for k in range(nl):
         blocks[k][pl.ds(lights * rows, UNDER), :] = under
-    eh_ref[...] = jnp.zeros_like(eh_ref)
-    at, col = iota((8, w), 0), iota((8, w), 1)
-    pick = (((at == 0) & (col == 0)) | ((at == 1) & (col == w - 1))).astype(jnp.bfloat16)
-    for k in order:
+    for copy in copies:
+        copy.wait()
+    for k in range(nl):
         q = li ^ k
         for l in range(lights):
-            copies[k, l].wait()
             e = lax.dot_general(
                 pick,
                 blocks[k][pl.ds(l * rows, rows), :],
@@ -108,17 +98,31 @@
     for k in range(nl):
         blocks[k][halo, :] = eh_ref[(li ^ k) + 1].astype(jnp.bfloat16)
     blocks[1][pl.ds(lights * rows + UNDER + 2 * lights, 2 * lights), :] = ends.astype(jnp.bfloat16)
-    for copy in edges:
-        copy.wait()
+
+
+def join_body(nl, depth_ref, albedo_ref, valid_ref, block_ref, end_ref, tile_ref, sr_ref, out_ref):
+    rows, w = tile_ref.shape[1:]
+    n = end_ref.shape[0] // 2
+    li = lax.axis_index("light")
+    right = lax.rem(li, 2) == 0
+    other = block_ref[pl.ds(block_ref.shape[0] - 2 * n, 2 * n), :].astype(F32)
+    out_ref[0:n, :] = jnp.where(right, end_ref[0:n, :], end_ref[n:, :])
+    out_ref[n : 2 * n, :] = jnp.where(right, other[0:n], other[n:])
+    out_ref[2 * n :, :] = jnp.zeros((8, rows), F32)
+    sr_ref[...] = jnp.zeros_like(sr_ref)
     lane = iota((rows, w), 1)
-    surf_ref[...] = jnp.zeros_like(surf_ref)
-    sr_ref[...] = jnp.zeros_like(sr_ref)
-    for f in range(3):
-        before, own, after, edge = (mask[s].astype(F32) if f == 2 else near[f, s] for s in range(4))
+
+    def columns(ref, q):
+        return ref[:, pl.ds(pl.multiple_of(q * w, w), w)].astype(F32)
+
+    for f, ref in enumerate((depth_ref, albedo_ref, valid_ref)):
+        own = columns(ref, li)
+        before = columns(ref, jnp.maximum(li - 1, 0))
+        after = columns(ref, jnp.minimum(li + 1, nl - 1))
         tile_ref[f] = own
         inner = jnp.transpose(own)
         outer = jnp.transpose(jnp.where(lane < w // 2, after, before))
-        edge = jnp.transpose(edge)
+        edge = jnp.transpose(columns(ref, jnp.where(right, nl - 1, 0)))
         low = jnp.where(li == 0, 0.0, outer[w - 2 : w])
         high = jnp.where(li == nl - 1, 0.0, outer[0:2])
         if f == 0:
@@ -126,21 +130,13 @@
             sr_ref[2:3, :] = inner[0:1]
             sr_ref[3:4, :] = inner[w - 1 : w]
             sr_ref[4:6, :] = high
-            surf_ref[0:2, :] = jnp.where(right, edge[w - 2 : w], edge[0:2])
+            out_ref[2 * n : 2 * n + 2, :] = jnp.where(right, edge[w - 2 : w], edge[0:2])
         else:
             at = 4 + 2 * f
             sr_ref[at : at + 1, :] = low[1:2]
             sr_ref[at + 1 : at + 2, :] = high[0:1]
-            surf_ref[1 + f : 2 + f, :] = jnp.where(right, edge[w - 1 : w], edge[0:1])
-
-
-def join_body(block_ref, end_ref, surf_ref, out_ref):
-    n = end_ref.shape[0] // 2
-    other = block_ref[pl.ds(block_ref.shape[0] - 2 * n, 2 * n), :].astype(F32)
-    right = lax.rem(lax.axis_index("light"), 2) == 0
-    out_ref[0:n, :] = jnp.where(right, end_ref[0:n, :], end_ref[n:, :])
-    out_ref[n : 2 * n, :] = jnp.where(right, other[0:n], other[n:])
-    out_ref[2 * n :, :] = surf_ref[...]
+            at = 2 * n + 1 + f
+            out_ref[at : at + 1, :] = jnp.where(right, edge[w - 1 : w], edge[0:1])
 
 
 def decode(table):
@@ -516,26 +512,25 @@
 
     hbm = pl.BlockSpec(memory_space=pltpu.HBM)
     field = (rows, w)
-    whole = (observations, light_table.T, depth_start, albedo_start, valid_mask)
-    *blocks, tile, surf, sr, end = call(
+    *blocks, end = call(
         functools.partial(cut_body, nl),
         tuple(shape(block_rows(lights, rows, k), w, dtype=jnp.bfloat16) for k in range(nl))
-        + (shape(3, *field), shape(8, rows), shape(16, rows), shape(2 * lights, rows)),
+        + (shape(2 * lights, rows),),
         [
             pltpu.VMEM((4, lights), jnp.int32),
-            pltpu.VMEM((2, 4, *field), F32),
-            pltpu.VMEM((4, *field), jnp.int32),
             pltpu.VMEM((nl + 2, 2 * lights, rows), F32),
             pltpu.SemaphoreType.DMA((nl * lights,)),
-            pltpu.SemaphoreType.DMA((13,)),
+            pltpu.SemaphoreType.DMA((1,)),
         ],
-        in_specs=[hbm] * 5,
-    )(*(pltpu.with_memory_space_constraint(x, pltpu.HBM) for x in whole))
+        in_specs=[hbm] * 2,
+    )(*(pltpu.with_memory_space_constraint(x, pltpu.HBM) for x in (observations, light_table.T)))
     obs2 = swap(blocks[2], 2)
     obs3 = swap(blocks[3], 3)
     obs1 = swap(blocks[1], 1)
     obs0 = blocks[0]
-    strip = call(join_body, shape(2 * lights + 8, rows))(obs1, end, surf)
+    tile, sr, strip = call(
+        functools.partial(join_body, nl), (shape(3, *field), shape(16, rows), shape(2 * lights + 8, rows))
+    )(depth_start, albedo_start, valid_mask, obs1, end)
     pairs = []
     for i in range(ns - 1):
         pairs += [(2 * ns + i, i + 1), (i, ns + i + 1), (ns + i + 1, 3 * ns + i), (3 * ns + i + 1, 2 * ns + i)]

time: 57.2 us -> 52.9 us (0.925)
  Pallas kernels: 15.7 us -> 11.7 us
    pallas_call x1, Pallas kernels: 6.43 us -> 2.22 us  [program(): call(functools.partial(cut_body, nl), tuple((shape(block_rows(lights, row...]
  transfers between devices with their start and end apart: 9 -> 9, of which waited for: 5 -> 5; matrix products, arithmetic and copies ran while one was open for 0% -> 0% of each run, Pallas kernels for 6% -> 7%
where the time goes in v5:
time: 52.9 us; the launch traced here: 52.7 us
  blocking collectives  15.5 us (29%)
  waiting for transfers between devices  14.6 us (28%)
  Pallas kernels  11.7 us (22%)
  starting transfers between devices  10.2 us (19%)
  between operations  0.74 us (1%)
    all_to_all x1, blocking collectives, program(): recv = lax.all_to_all(pay, AXES, 0, 0, tiled=True)  15.5 us
    all_to_all x1, waiting for transfers between devices, program(): recv = lax.all_to_all(pay, AXES, 0, 0, tiled=True)  6.89 us
    ppermute x7, waiting for transfers between devices, swap(): return lax.ppermute(x, 'light', [(i, i ^ k) for i in range(nl)])  6.28 us
    pallas_call x1, Pallas kernels, program(): call(functools.partial(second_body, nl), (shape(4, *field), shape(nd, 1,...  4.27 us
    ppermute x7, starting transfers between devices, swap(): return lax.ppermute(x, 'light', [(i, i ^ k) for i in range(nl)])  4.03 us
    ppermute x1, starting transfers between devices, program(): direct = lax.ppermute(strip, AXES, pairs)  3.65 us
    all_to_all x1, starting transfers between devices, program(): recv = lax.all_to_all(pay, AXES, 0, 0, tiled=True)  2.54 us
    pallas_call x1, Pallas kernels, program(): call(functools.partial(cut_body, nl), tuple((shape(block_rows(lights, row...  2.22 us
  transfers between devices with their start and end apart: 9, of which 5 were waited for; matrix products, arithmetic and copies ran while one was open for 0% of the time, Pallas kernels for 7%

profile of v5, /device:TPU:0, one launch (start us, length us, event | category | flops | bytes accessed | tf_op | source)
XLA Modules:
  0.0 52.7 jit_solution(8592912690804060476)
XLA Ops:
  0.7 2.2 %shard_map.68 = (bf16[1056,128]{1,0:T(8,128)(2,1)S(1)}, bf16[1072,128]{1,0:T(8,128)(2,1)S(1)}, bf16[1056,128]{1,0:T(8,128)(2,1)S(1)}, bf16[1056,128]{1,0:T(8,128)(2,1)S(1)}, f32[16,128]{1,0:T(8,128)S(1)}) custom-call(bf16[8,128,512]{2,1,0:T(8,128)(2,1)} %obs_ref.1, s32[4,8]{1,0:T(4,128)} %bitcast.1), custom_call_target="tpu_custom_call" | custom-call | tf_op jit(solution)/shard_map/pallas_call | solution.py:515
  2.9 0.6 %collective-permute-start = (bf16[1072,128]{1,0:T(8,128)(2,1)S(1)}, bf16[1072,128]{1,0:T(8,128)(2,1)S(1)}, u32[]{:S(2)}, u32[]{:S(2)}) collective-permute-start(bf16[1072,128]{1,0:T(8,128)(2,1)S(1)} %get-tuple-element.21), channel_id=1, source_target_pairs={{0,8},{8,0},{16,24},{24,16},{1,9},{9,1},{17,25},{25,17},{2,10},{10... | collective-permute-start | bytes 823304 | tf_op jit(solution)/shard_map/ppermute | solution.py:511
  3.4 2.6 %collective-permute-start.2 = (bf16[1056,128]{1,0:T(8,128)(2,1)S(1)}, bf16[1056,128]{1,0:T(8,128)(2,1)S(1)}, u32[]{:S(2)}, u32[]{:S(2)}) collective-permute-start(bf16[1056,128]{1,0:T(8,128)(2,1)S(1)} %get-tuple-element.29), channel_id=1, source_target_pairs={{0,16},{8,24},{16,0},{24,8},{1,17},{9,25},{17,1},{25,9},{2,18},{10... | collective-permute-start | bytes 811016 | tf_op jit(solution)/shard_map/ppermute | solution.py:511
  6.0 0.0 collective-permute-start.3
  6.1 0.2 shard_map.69
  6.3 3.6 %collective-permute-start.1 = (f32[24,128]{1,0:T(8,128)S(1)}, f32[24,128]{1,0:T(8,128)S(1)}, u32[]{:S(2)}, u32[]{:S(2)}) collective-permute-start(f32[24,128]{1,0:T(8,128)S(1)} %get-tuple-element.25), channel_id=1, source_target_pairs={{16,1},{0,9},{9,24},{25,16},{17,2},{1,10},{10,25},{26,17},{18,3},{... | collective-permute-start | bytes 36872 | tf_op jit(solution)/shard_map/ppermute | solution.py:537
  9.9 1.4 %collective-permute-done.1.strip_ref.direct_ref = f32[24,128]{1,0:T(8,128)S(1)} collective-permute-done((f32[24,128]{1,0:T(8,128)S(1)}, f32[24,128]{1,0:T(8,128)S(1)}, u32[]{:S(2)}, u32[]{:S(2)}) %collective-permute-start.1) | collective-permute-done | bytes 12320 | tf_op jit(solution)/shard_map/ppermute | solution.py:537
  11.3 1.6 %shard_map.70 = (f32[4,128,128]{2,1,0:T(8,128)S(1)}, f32[16,128]{1,0:T(8,128)S(1)}, f32[7,128,128]{2,1,0:T(8,128)S(1)}) custom-call(f32[3,128,128]{2,1,0:T(8,128)S(1)} %get-tuple-element.23.tile_ref, f32[16,128]{1,0:T(8,128)S(1)} %get-tuple-element.24.sr_ref, f32[24,128]{1,0:T(8,128)S(1)} %collective-permute-done.1.strip_ref.direct_ref, ...), custom_call_target="tpu_custom_call" | custom-call | tf_op jit(solution)/shard_map/pallas_call | solution.py:541
  13.0 0.4 collective-permute-done.2.obs.rest_2_
  13.3 0.9 %shard_map.71.in_ref = f32[7,128,128]{2,1,0:T(8,128)S(1)} custom-call(f32[4,128,128]{2,1,0:T(8,128)S(1)} %get-tuple-element.27.ctx_ref, f32[7,128,128]{2,1,0:T(8,128)S(1)} %get-tuple-element.28.in_ref, bf16[1056,128]{1,0:T(8,128)(2,1)S(1)} %collective-permute-done.2.obs.rest_2_), custom_call_target="tpu_custom_call" | custom-call | tf_op jit(solution)/shard_map/pallas_call | solution.py:544
  14.2 4.4 %collective-permute-done.3.obs.rest_3_ = bf16[1056,128]{1,0:T(8,128)(2,1)S(1)} collective-permute-done((bf16[1056,128]{1,0:T(8,128)(2,1)S(1)}, bf16[1056,128]{1,0:T(8,128)(2,1)S(1)}, u32[]{:S(2)}, u32[]{:S(2)}) %collective-permute-start.3) | collective-permute-done | bytes 270368 | tf_op jit(solution)/shard_map/ppermute | solution.py:511
  18.6 0.9 %shard_map.72.state_ref = f32[7,128,128]{2,1,0:T(8,128)S(1)} custom-call(f32[4,128,128]{2,1,0:T(8,128)S(1)} %get-tuple-element.27.ctx_ref, f32[7,128,128]{2,1,0:T(8,128)S(1)} %shard_map.71.in_ref, bf16[1056,128]{1,0:T(8,128)(2,1)S(1)} %collective-permute-done.3.obs.rest_3_), custom_call_target="tpu_custom_call" | custom-call | tf_op jit(solution)/shard_map/pallas_call | solution.py:545
  19.5 0.5 %shard_map.73 = (f32[2,128,128]{2,1,0:T(8,128)S(1)}, f32[8,128]{1,0:T(8,128)S(1)}, f32[32,4,128]{2,1,0:T(4,128)S(1)}, f32[3,32,128]{2,1,0:T(8,128)S(1)}) custom-call(f32[4,128,128]{2,1,0:T(8,128)S(1)} %get-tuple-element.27.ctx_ref, f32[3,128,128]{2,1,0:T(8,128)S(1)} %get-tuple-element.23.tile_ref, f32[7,128,128]{2,1,0:T(8,128)S(1)} %shard_map.72.state_ref, ...), custom_call_target="tpu_custom_call" | custom-call | tf_op jit(solution)/shard_map/pallas_call | solution.py:546
  20.1 15.5 %all_to_all.10.recv_ref = f32[32,4,128]{2,1,0:T(4,128)S(1)} all-to-all(f32[32,4,128]{2,1,0:T(4,128)S(1)} %get-tuple-element.32), channel_id=1, replica_groups=mesh['light'=4,'strip'=8] {'light','strip'}, dimensions={0} | all-to-all | bytes 131072 | tf_op jit(solution)/shard_map/all_to_all | solution.py:550
  35.6 4.3 %shard_map.74 = (f32[4,128,128]{2,1,0:T(8,128)S(1)}, f32[32,1,128]{2,1,0:T(1,128)}) custom-call(f32[32,4,128]{2,1,0:T(4,128)S(1)} %all_to_all.10.recv_ref, f32[2,128,128]{2,1,0:T(8,128)S(1)} %get-tuple-element.33.grad_ref, f32[8,128]{1,0:T(8,128)S(1)} %get-tuple-element.34.edge_ref, f32[3,128,128]{2,1,0:T(8,128)S(1)} %get-tuple-element.23.tile_ref, ...), custom_call_target="tpu_custom_call" | custom-call | tf_op jit(solution)/shard_map/pallas_call | solution.py:551
  39.9 0.7 %collective-permute-start.5 = (f32[4,128,128]{2,1,0:T(8,128)S(1)}, f32[4,128,128]{2,1,0:T(8,128)S(1)}, u32[]{:S(2)}, u32[]{:S(2)}) collective-permute-start(f32[4,128,128]{2,1,0:T(8,128)S(1)} %get-tuple-element.37.rest_0_), channel_id=1, source_target_pairs={{0,16},{8,24},{16,0},{24,8},{1,17},{9,25},{17,1},{25,9},{2,18},{10... | collective-permute-start | bytes 786440 | tf_op jit(solution)/shard_map/ppermute | solution.py:511
  40.6 2.5 %all-to-all-start.1 = ((f32[32,1,128]{2,1,0:T(1,128)}), f32[32,1,128]{2,1,0:T(1,128)S(1)}, u32[]{:S(2)}, u32[]{:S(2)}) async-start(f32[32,1,128]{2,1,0:T(1,128)} %get-tuple-element.36), calls=%async_computation.1 | async-start | bytes 32768 | tf_op jit(solution)/shard_map/all_to_all | solution.py:563
  43.1 0.2 collective-permute-start.6
  43.3 6.9 %all-to-all-done.1.recv_ref = f32[32,1,128]{2,1,0:T(1,128)S(1)} async-done(((f32[32,1,128]{2,1,0:T(1,128)}), f32[32,1,128]{2,1,0:T(1,128)S(1)}, u32[]{:S(2)}, u32[]{:S(2)}) %all-to-all-start.1) | async-done | bytes 16416 | tf_op jit(solution)/shard_map/all_to_all | solution.py:563
  50.2 0.0 collective-permute-done.5.rest_2_
  50.2 0.0 collective-permute-start.7
  50.2 0.0 collective-permute-done.6.rest_1_
  50.2 1.5 %collective-permute-done.7.rest_3_ = f32[4,128,128]{2,1,0:T(8,128)S(1)} collective-permute-done((f32[4,128,128]{2,1,0:T(8,128)S(1)}, f32[4,128,128]{2,1,0:T(8,128)S(1)}, u32[]{:S(2)}, u32[]{:S(2)}) %collective-permute-start.7) | collective-permute-done | bytes 262176 | tf_op jit(solution)/shard_map/ppermute | solution.py:511
  51.7 1.0 %shard_map.75 = (f32[128,512]{1,0:T(8,128)}, f32[128,512]{1,0:T(8,128)}) custom-call(f32[32,1,128]{2,1,0:T(1,128)S(1)} %all-to-all-done.1.recv_ref, f32[4,128,128]{2,1,0:T(8,128)S(1)} %get-tuple-element.37.rest_0_, f32[4,128,128]{2,1,0:T(8,128)S(1)} %collective-permute-done.6.rest_1_, f32[4,128,128]{2,1,0:T(8,128)S(1)} %collective-permute-done.5.rest_2_, ...), custom_call_target="tpu_custom_call" | custom-call | tf_op jit(solution)/shard_map/pallas_call | solution.py:567
  (9 shorter events, 0.0 us)
Async XLA Ops:
  0.6 5.4 %copy-start = (f32[128,512]{1,0:T(8,128)S(1)}, f32[128,512]{1,0:T(8,128)}, u32[]{:S(2)}) copy-start(f32[128,512]{1,0:T(8,128)} %depth_ref.1) | copy-start | bytes 786436
  0.6 5.4 %copy-start.1 = (f32[128,512]{1,0:T(8,128)S(1)}, f32[128,512]{1,0:T(8,128)}, u32[]{:S(2)}) copy-start(f32[128,512]{1,0:T(8,128)} %albedo_ref.1) | copy-start | bytes 786436
  0.7 5.4 %copy-start.2 = (s32[128,512]{1,0:T(8,128)S(1)}, s32[128,512]{1,0:T(8,128)}, u32[]{:S(2)}) copy-start(s32[128,512]{1,0:T(8,128)} %valid_ref.1) | copy-start | bytes 786436
  2.9 3.2 %collective-permute-start = (bf16[1072,128]{1,0:T(8,128)(2,1)S(1)}, bf16[1072,128]{1,0:T(8,128)(2,1)S(1)}, u32[]{:S(2)}, u32[]{:S(2)}) collective-permute-start(bf16[1072,128]{1,0:T(8,128)(2,1)S(1)} %get-tuple-element.21), channel_id=1, source_target_pairs={{0,8},{8,0},{16,24},{24,16},{1,9},{9,1},{17,25},{25,17},{2,10},{10... | collective-permute-start | bytes 823304 | tf_op jit(solution)/shard_map/ppermute | solution.py:511
  3.4 9.9 %collective-permute-start.2 = (bf16[1056,128]{1,0:T(8,128)(2,1)S(1)}, bf16[1056,128]{1,0:T(8,128)(2,1)S(1)}, u32[]{:S(2)}, u32[]{:S(2)}) collective-permute-start(bf16[1056,128]{1,0:T(8,128)(2,1)S(1)} %get-tuple-element.29), channel_id=1, source_target_pairs={{0,16},{8,24},{16,0},{24,8},{1,17},{9,25},{17,1},{25,9},{2,18},{10... | collective-permute-start | bytes 811016 | tf_op jit(solution)/shard_map/ppermute | solution.py:511
  6.0 12.6 %collective-permute-start.3 = (bf16[1056,128]{1,0:T(8,128)(2,1)S(1)}, bf16[1056,128]{1,0:T(8,128)(2,1)S(1)}, u32[]{:S(2)}, u32[]{:S(2)}) collective-permute-start(bf16[1056,128]{1,0:T(8,128)(2,1)S(1)} %get-tuple-element.30), channel_id=1, source_target_pairs={{0,24},{8,16},{16,8},{24,0},{1,25},{9,17},{17,9},{25,1},{2,26},{10... | collective-permute-start | bytes 811016 | tf_op jit(solution)/shard_map/ppermute | solution.py:511
  6.3 5.0 %collective-permute-start.1 = (f32[24,128]{1,0:T(8,128)S(1)}, f32[24,128]{1,0:T(8,128)S(1)}, u32[]{:S(2)}, u32[]{:S(2)}) collective-permute-start(f32[24,128]{1,0:T(8,128)S(1)} %get-tuple-element.25), channel_id=1, source_target_pairs={{16,1},{0,9},{9,24},{25,16},{17,2},{1,10},{10,25},{26,17},{18,3},{... | collective-permute-start | bytes 36872 | tf_op jit(solution)/shard_map/ppermute | solution.py:537
  11.3 8.2 %collective-permute-start.4 = (f32[24,128]{1,0:T(8,128)S(1)}, f32[24,128]{1,0:T(8,128)S(1)}, u32[]{:S(2)}, u32[]{:S(2)}) collective-permute-start(f32[24,128]{1,0:T(8,128)S(1)} %collective-permute-done.1.strip_ref.direct_ref), channel_id=1, source_target_pairs={{0,8},{8,0},{16,24},{24,16},{1,9},{9,1},{17,25},{25,17},{2,10},{10... | collective-permute-start | bytes 36872 | tf_op jit(solution)/shard_map/ppermute | solution.py:511
  39.9 10.3 %collective-permute-start.5 = (f32[4,128,128]{2,1,0:T(8,128)S(1)}, f32[4,128,128]{2,1,0:T(8,128)S(1)}, u32[]{:S(2)}, u32[]{:S(2)}) collective-permute-start(f32[4,128,128]{2,1,0:T(8,128)S(1)} %get-tuple-element.37.rest_0_), channel_id=1, source_target_pairs={{0,16},{8,24},{16,0},{24,8},{1,17},{9,25},{17,1},{25,9},{2,18},{10... | collective-permute-start | bytes 786440 | tf_op jit(solution)/shard_map/ppermute | solution.py:511
  40.6 9.6 %all-to-all-start.1 = ((f32[32,1,128]{2,1,0:T(1,128)}), f32[32,1,128]{2,1,0:T(1,128)S(1)}, u32[]{:S(2)}, u32[]{:S(2)}) async-start(f32[32,1,128]{2,1,0:T(1,128)} %get-tuple-element.36), calls=%async_computation.1 | async-start | bytes 32768 | tf_op jit(solution)/shard_map/all_to_all | solution.py:563
  43.1 7.1 %collective-permute-start.6 = (f32[4,128,128]{2,1,0:T(8,128)S(1)}, f32[4,128,128]{2,1,0:T(8,128)S(1)}, u32[]{:S(2)}, u32[]{:S(2)}) collective-permute-start(f32[4,128,128]{2,1,0:T(8,128)S(1)} %get-tuple-element.37.rest_0_), channel_id=1, source_target_pairs={{0,8},{8,0},{16,24},{24,16},{1,9},{9,1},{17,25},{25,17},{2,10},{10... | collective-permute-start | bytes 786440 | tf_op jit(solution)/shard_map/ppermute | solution.py:511
  50.2 1.5 %collective-permute-start.7 = (f32[4,128,128]{2,1,0:T(8,128)S(1)}, f32[4,128,128]{2,1,0:T(8,128)S(1)}, u32[]{:S(2)}, u32[]{:S(2)}) collective-permute-start(f32[4,128,128]{2,1,0:T(8,128)S(1)} %collective-permute-done.5.rest_2_), channel_id=1, source_target_pairs={{0,8},{8,0},{16,24},{24,16},{1,9},{9,1},{17,25},{25,17},{2,10},{10... | collective-permute-start | bytes 786440 | tf_op jit(solution)/shard_map/ppermute | solution.py:511

commit v6 on v5

--- a/solution.py
+++ b/solution.py
@@ -246,7 +246,7 @@
     return (least,) + sums
 
 
-def sweep(ctx_ref, pb_ref, obs_refs, bases, total, load, store):
+def sweep(ctx_ref, params, obs_refs, total, load, store):
     rows, w = ctx_ref.shape[1:]
     lights = lights_of(obs_refs[0], rows)
     split = (TR // 8, 8, w)
@@ -257,7 +257,7 @@
         row = iota(split, 0) * 8 + iota(split, 1) + i * TR
         py = (row.astype(F32) + (0.5 - rows / 2.0)) / total
         state = load(at)
-        for obs_ref, base in zip(obs_refs, bases):
+        for obs_ref, (pb_ref, base) in zip(obs_refs, params):
             obs = [
                 obs_ref[pl.ds(pl.multiple_of(j * rows + i * TR, TR), TR), :].astype(F32).reshape(split)
                 for j in range(lights)
@@ -376,7 +376,7 @@
     n = lights_of(obs0, rows)
     fill_params(pb_ref, 0, obs0, n, rows, w, place, total)
     fill_params(pb_ref, n, obs1, n, rows, w, place, total)
-    sweep(ctx_ref, pb_ref, (obs0, obs1), (0, n), total, lambda at: None, state_store(state_ref, w))
+    sweep(ctx_ref, ((pb_ref, 0), (pb_ref, n)), (obs0, obs1), total, lambda at: None, state_store(state_ref, w))
 
 
 def more_body(ctx_ref, in_ref, obs, state_ref, pb_ref):
@@ -384,7 +384,7 @@
     rows, w = ctx_ref.shape[1:]
     total = w * count
     fill_params(pb_ref, 0, obs, lights_of(obs, rows), rows, w, place, total)
-    sweep(ctx_ref, pb_ref, (obs,), (0,), total, state_load(in_ref, w), state_store(state_ref, w))
+    sweep(ctx_ref, ((pb_ref, 0),), (obs,), total, state_load(in_ref, w), state_store(state_ref, w))
 
 
 def finish(state_ref, ctx_ref, albedo, valid, pack_ref, srow_ref, grad_ref, edge_ref, pay_ref):
@@ -423,7 +423,7 @@
     table = jnp.zeros((4, w), F32)
     for k in range(nl):
         halo = block_refs[k][pl.ds(n * rows + UNDER, 2 * n), :].astype(F32)
-        beyond = (relayed_ref if k < 2 else direct_ref)[(k % 2) * n : (k % 2 + 1) * n, :]
+        beyond = (direct_ref if k < 2 else relayed_ref)[(k % 2) * n : (k % 2 + 1) * n, :]
         pack_ref[0, k * n : (k + 1) * n, :] = jnp.where(li == 0, beyond, halo[0:n])
         pack_ref[1, k * n : (k + 1) * n, :] = jnp.where(li == nl - 1, beyond, halo[n:])
         entries = jnp.concatenate([table_rows(block_refs[k], n, rows)] * 2, axis=0)
@@ -441,8 +441,8 @@
 
 
 def second_body(nl, recv_ref, grad_ref, edge_ref, tile_ref, srow0_ref, pack_ref, *rest):
-    obs_refs = rest[:nl]
-    out_ref, pay_ref, ctx_ref, state_ref, pb_ref, srow_ref = rest[nl:]
+    obs_refs, pb_refs = rest[:nl], rest[nl : 2 * nl - 1]
+    out_ref, pay_ref, ctx_ref, state_ref, srow_ref = rest[2 * nl - 1 :]
     _, _, place, count = position()
     rows, w = ctx_ref.shape[1:]
     total = w * count
@@ -475,10 +475,8 @@
     srow_ref[8:16, :] = srow0_ref[8:16, :]
     fill_context(ctx_ref, surface, albedo, srow_ref[1:2, :], srow_ref[4:5, :])
     n = lights_of(obs_refs[0], rows)
-    bases = tuple(k * n for k in range(nl))
-    for k in range(nl):
-        fill_params(pb_ref, bases[k], obs_refs[k], n, rows, w, place, total)
-    sweep(ctx_ref, pb_ref, obs_refs, bases, total, lambda at: None, state_store(state_ref, w))
+    params = ((pb_refs[0], 0), (pb_refs[0], n)) + tuple((ref, 0) for ref in pb_refs[1:])
+    sweep(ctx_ref, params, obs_refs, total, lambda at: None, state_store(state_ref, w))
     depth, grad_albedo = finish(
         state_ref, ctx_ref, albedo, tile_ref[2], pack_ref, srow_ref, None, None, pay_ref
     )
@@ -533,16 +531,21 @@
     )(depth_start, albedo_start, valid_mask, obs1, end)
     pairs = []
     for i in range(ns - 1):
-        pairs += [(2 * ns + i, i + 1), (i, ns + i + 1), (ns + i + 1, 3 * ns + i), (3 * ns + i + 1, 2 * ns + i)]
+        for l in range(nl):
+            source, target = (i, i + 1) if l % 2 == 0 else (i + 1, i)
+            pairs.append((l * ns + source, l * ns + target))
     direct = lax.ppermute(strip, AXES, pairs)
-    relayed = swap(direct, 1)
-
-    pb = pltpu.VMEM((2 * lights, 5, 8, w), F32)
-    ctx, srow, state = call(
-        functools.partial(first_body, nl), (shape(4, *field), shape(16, rows), shape(7, *field)), [pb]
+    relayed = swap(direct, 2)
+
+    def tiles(n):
+        return shape(n, 5, 8, w)
+
+    ctx, srow, state, pb0 = call(
+        functools.partial(first_body, nl), (shape(4, *field), shape(16, rows), shape(7, *field), tiles(2 * lights))
     )(tile, sr, direct, obs0, obs1)
-    state = call(more_body, shape(7, *field), [pb])(ctx, state, obs2)
-    state = call(more_body, shape(7, *field), [pb])(ctx, state, obs3)
+    more = (shape(7, *field), tiles(lights))
+    state, pb2 = call(more_body, more)(ctx, state, obs2)
+    state, pb3 = call(more_body, more)(ctx, state, obs3)
     grad, edge, pay, pack = call(
         functools.partial(last_body, nl),
         (shape(2, *field), shape(8, rows), shape(nd, 4, rows), shape(3, nl * lights, rows)),
@@ -554,10 +557,9 @@
         [
             pltpu.VMEM((4, *field), F32),
             pltpu.VMEM((7, *field), F32),
-            pltpu.VMEM((nl * lights, 5, 8, w), F32),
             pltpu.VMEM((16, rows), F32),
         ],
-    )(recv, grad, edge, tile, srow, pack, obs0, obs1, obs2, obs3)
+    )(recv, grad, edge, tile, srow, pack, obs0, obs1, obs2, obs3, pb0, pb2, pb3)
     part2 = swap(own, 2)
     part1 = swap(own, 1)
     recv = lax.all_to_all(pay, AXES, 0, 0, tiled=True)

time: 52.9 us -> 50.3 us (0.951)
  blocking collectives: 15.5 us -> 13 us
  waiting for transfers between devices: 14.6 us -> 13 us
  starting transfers between devices: 10.2 us -> 11.7 us
    all_to_all x1, blocking collectives: 15.5 us -> 13 us  [program(): recv = lax.all_to_all(pay, AXES, 0, 0, tiled=True)]
    ppermute x7, waiting for transfers between devices: 6.28 us -> 4.75 us  [swap(): return lax.ppermute(x, 'light', [(i, i ^ k) for i in range(nl)])]
    ppermute x7, starting transfers between devices: 4.03 us -> 5.52 us  [swap(): return lax.ppermute(x, 'light', [(i, i ^ k) for i in range(nl)])]
  transfers between devices with their start and end apart: 9 -> 9, of which waited for: 5 -> 4; matrix products, arithmetic and copies ran while one was open for 0% -> 0% of each run, Pallas kernels for 7% -> 7%
where the time goes in v6:
time: 50.3 us; the launch traced here: 50.1 us
  waiting for transfers between devices  13 us (26%)
  blocking collectives  13 us (26%)
  starting transfers between devices  11.7 us (23%)
  Pallas kernels  11.6 us (23%)
  between operations  0.74 us (1%)
    all_to_all x1, blocking collectives, program(): recv = lax.all_to_all(pay, AXES, 0, 0, tiled=True)  13 us
    all_to_all x1, waiting for transfers between devices, program(): recv = lax.all_to_all(pay, AXES, 0, 0, tiled=True)  6.89 us
    ppermute x7, starting transfers between devices, swap(): return lax.ppermute(x, 'light', [(i, i ^ k) for i in range(nl)])  5.52 us
    ppermute x7, waiting for transfers between devices, swap(): return lax.ppermute(x, 'light', [(i, i ^ k) for i in range(nl)])  4.75 us
    pallas_call x1, Pallas kernels, program(): call(functools.partial(second_body, nl), (shape(4, *field), shape(nd, 1,...  4.17 us
    ppermute x1, starting transfers between devices, program(): direct = lax.ppermute(strip, AXES, pairs)  3.68 us
    all_to_all x1, starting transfers between devices, program(): recv = lax.all_to_all(pay, AXES, 0, 0, tiled=True)  2.54 us
    pallas_call x1, Pallas kernels, program(): call(functools.partial(cut_body, nl), tuple((shape(block_rows(lights, row...  2.22 us
  transfers between devices with their start and end apart: 9, of which 4 were waited for; matrix products, arithmetic and copies ran while one was open for 0% of the time, Pallas kernels for 7%

profile of v6, /device:TPU:0, one launch (start us, length us, event | category | flops | bytes accessed | tf_op | source)
XLA Modules:
  0.0 50.1 jit_solution(10928511590596686271)
XLA Ops:
  0.7 2.2 %shard_map.68 = (bf16[1056,128]{1,0:T(8,128)(2,1)S(1)}, bf16[1072,128]{1,0:T(8,128)(2,1)S(1)}, bf16[1056,128]{1,0:T(8,128)(2,1)S(1)}, bf16[1056,128]{1,0:T(8,128)(2,1)S(1)}, f32[16,128]{1,0:T(8,128)S(1)}) custom-call(bf16[8,128,512]{2,1,0:T(8,128)(2,1)} %obs_ref.1, s32[4,8]{1,0:T(4,128)} %bitcast.1), custom_call_target="tpu_custom_call" | custom-call | tf_op jit(solution)/shard_map/pallas_call | solution.py:513
  2.9 0.6 %collective-permute-start = (bf16[1072,128]{1,0:T(8,128)(2,1)S(1)}, bf16[1072,128]{1,0:T(8,128)(2,1)S(1)}, u32[]{:S(2)}, u32[]{:S(2)}) collective-permute-start(bf16[1072,128]{1,0:T(8,128)(2,1)S(1)} %get-tuple-element.26), channel_id=1, source_target_pairs={{0,8},{8,0},{16,24},{24,16},{1,9},{9,1},{17,25},{25,17},{2,10},{10... | collective-permute-start | bytes 823304 | tf_op jit(solution)/shard_map/ppermute | solution.py:509
  3.4 2.6 %collective-permute-start.2 = (bf16[1056,128]{1,0:T(8,128)(2,1)S(1)}, bf16[1056,128]{1,0:T(8,128)(2,1)S(1)}, u32[]{:S(2)}, u32[]{:S(2)}) collective-permute-start(bf16[1056,128]{1,0:T(8,128)(2,1)S(1)} %get-tuple-element.34), channel_id=1, source_target_pairs={{0,16},{8,24},{16,0},{24,8},{1,17},{9,25},{17,1},{25,9},{2,18},{10... | collective-permute-start | bytes 811016 | tf_op jit(solution)/shard_map/ppermute | solution.py:509
  6.0 0.0 collective-permute-start.3
  6.0 0.0 collective-permute-done.block_ref.obs1.rest_1_
  6.1 0.2 shard_map.69
  6.3 3.7 %collective-permute-start.1 = (f32[24,128]{1,0:T(8,128)S(1)}, f32[24,128]{1,0:T(8,128)S(1)}, u32[]{:S(2)}, u32[]{:S(2)}) collective-permute-start(f32[24,128]{1,0:T(8,128)S(1)} %get-tuple-element.30), channel_id=1, source_target_pairs={{0,1},{9,8},{16,17},{25,24},{1,2},{10,9},{17,18},{26,25},{2,3},{11... | collective-permute-start | bytes 36872 | tf_op jit(solution)/shard_map/ppermute | solution.py:537
  10.0 1.4 %collective-permute-done.1.strip_ref.direct_ref = f32[24,128]{1,0:T(8,128)S(1)} collective-permute-done((f32[24,128]{1,0:T(8,128)S(1)}, f32[24,128]{1,0:T(8,128)S(1)}, u32[]{:S(2)}, u32[]{:S(2)}) %collective-permute-start.1) | collective-permute-done | bytes 12320 | tf_op jit(solution)/shard_map/ppermute | solution.py:537
  11.4 1.5 %collective-permute-start.4 = (f32[24,128]{1,0:T(8,128)S(1)}, f32[24,128]{1,0:T(8,128)S(1)}, u32[]{:S(2)}, u32[]{:S(2)}) collective-permute-start(f32[24,128]{1,0:T(8,128)S(1)} %collective-permute-done.1.strip_ref.direct_ref), channel_id=1, source_target_pairs={{0,16},{8,24},{16,0},{24,8},{1,17},{9,25},{17,1},{25,9},{2,18},{10... | collective-permute-start | bytes 36872 | tf_op jit(solution)/shard_map/ppermute | solution.py:509
  12.9 1.6 %shard_map.70 = (f32[4,128,128]{2,1,0:T(8,128)S(1)}, f32[16,128]{1,0:T(8,128)S(1)}, f32[7,128,128]{2,1,0:T(8,128)S(1)}, f32[16,5,8,128]{3,2,1,0:T(8,128)S(1)}) custom-call(f32[3,128,128]{2,1,0:T(8,128)S(1)} %get-tuple-element.28.tile_ref, f32[16,128]{1,0:T(8,128)S(1)} %get-tuple-element.29.sr_ref, f32[24,128]{1,0:T(8,128)S(1)} %collective-permute-done.1.strip_ref.direct_ref, ...), custom_call_target="tpu_custom_call" | custom-call | tf_op jit(solution)/shard_map/pallas_call | solution.py:543
  14.5 0.0 collective-permute-done.2.obs.rest_2_
  14.5 0.9 %shard_map.71 = (f32[7,128,128]{2,1,0:T(8,128)S(1)}, f32[8,5,8,128]{3,2,1,0:T(8,128)S(1)}) custom-call(f32[4,128,128]{2,1,0:T(8,128)S(1)} %get-tuple-element.32.ctx_ref, f32[7,128,128]{2,1,0:T(8,128)S(1)} %get-tuple-element.33.in_ref, bf16[1056,128]{1,0:T(8,128)(2,1)S(1)} %collective-permute-done.2.obs.rest_2_), custom_call_target="tpu_custom_call" | custom-call | tf_op jit(solution)/shard_map/pallas_call | solution.py:547
  15.4 3.2 %collective-permute-done.3.obs.rest_3_ = bf16[1056,128]{1,0:T(8,128)(2,1)S(1)} collective-permute-done((bf16[1056,128]{1,0:T(8,128)(2,1)S(1)}, bf16[1056,128]{1,0:T(8,128)(2,1)S(1)}, u32[]{:S(2)}, u32[]{:S(2)}) %collective-permute-start.3) | collective-permute-done | bytes 270368 | tf_op jit(solution)/shard_map/ppermute | solution.py:509
  18.6 0.9 %shard_map.72 = (f32[7,128,128]{2,1,0:T(8,128)S(1)}, f32[8,5,8,128]{3,2,1,0:T(8,128)S(1)}) custom-call(f32[4,128,128]{2,1,0:T(8,128)S(1)} %get-tuple-element.32.ctx_ref, f32[7,128,128]{2,1,0:T(8,128)S(1)} %get-tuple-element.35.in_ref, bf16[1056,128]{1,0:T(8,128)(2,1)S(1)} %collective-permute-done.3.obs.rest_3_), custom_call_target="tpu_custom_call" | custom-call | tf_op jit(solution)/shard_map/pallas_call | solution.py:548
  19.5 0.0 collective-permute-done.4.relayed_ref
  19.5 0.5 %shard_map.73 = (f32[2,128,128]{2,1,0:T(8,128)S(1)}, f32[8,128]{1,0:T(8,128)S(1)}, f32[32,4,128]{2,1,0:T(4,128)S(1)}, f32[3,32,128]{2,1,0:T(8,128)S(1)}) custom-call(f32[4,128,128]{2,1,0:T(8,128)S(1)} %get-tuple-element.32.ctx_ref, f32[3,128,128]{2,1,0:T(8,128)S(1)} %get-tuple-element.28.tile_ref, f32[7,128,128]{2,1,0:T(8,128)S(1)} %get-tuple-element.37.state_ref, ...), custom_call_target="tpu_custom_call" | custom-call | tf_op jit(solution)/shard_map/pallas_call | solution.py:549
  20.1 13.0 %all_to_all.10.recv_ref = f32[32,4,128]{2,1,0:T(4,128)S(1)} all-to-all(f32[32,4,128]{2,1,0:T(4,128)S(1)} %get-tuple-element.39), channel_id=1, replica_groups=mesh['light'=4,'strip'=8] {'light','strip'}, dimensions={0} | all-to-all | bytes 131072 | tf_op jit(solution)/shard_map/all_to_all | solution.py:553
  33.1 4.2 %shard_map.74 = (f32[4,128,128]{2,1,0:T(8,128)S(1)}, f32[32,1,128]{2,1,0:T(1,128)}) custom-call(f32[32,4,128]{2,1,0:T(4,128)S(1)} %all_to_all.10.recv_ref, f32[2,128,128]{2,1,0:T(8,128)S(1)} %get-tuple-element.40.grad_ref, f32[8,128]{1,0:T(8,128)S(1)} %get-tuple-element.41.edge_ref, f32[3,128,128]{2,1,0:T(8,128)S(1)} %get-tuple-element.28.tile_ref, ...), custom_call_target="tpu_custom_call" | custom-call | tf_op jit(solution)/shard_map/pallas_call | solution.py:554
  37.2 0.7 %collective-permute-start.5 = (f32[4,128,128]{2,1,0:T(8,128)S(1)}, f32[4,128,128]{2,1,0:T(8,128)S(1)}, u32[]{:S(2)}, u32[]{:S(2)}) collective-permute-start(f32[4,128,128]{2,1,0:T(8,128)S(1)} %get-tuple-element.47.rest_0_), channel_id=1, source_target_pairs={{0,16},{8,24},{16,0},{24,8},{1,17},{9,25},{17,1},{25,9},{2,18},{10... | collective-permute-start | bytes 786440 | tf_op jit(solution)/shard_map/ppermute | solution.py:509
  37.9 2.5 %all-to-all-start.1 = ((f32[32,1,128]{2,1,0:T(1,128)}), f32[32,1,128]{2,1,0:T(1,128)S(1)}, u32[]{:S(2)}, u32[]{:S(2)}) async-start(f32[32,1,128]{2,1,0:T(1,128)} %get-tuple-element.46), calls=%async_computation.1 | async-start | bytes 32768 | tf_op jit(solution)/shard_map/all_to_all | solution.py:565
  40.5 0.2 collective-permute-start.6
  40.7 6.9 %all-to-all-done.1.recv_ref = f32[32,1,128]{2,1,0:T(1,128)S(1)} async-done(((f32[32,1,128]{2,1,0:T(1,128)}), f32[32,1,128]{2,1,0:T(1,128)S(1)}, u32[]{:S(2)}, u32[]{:S(2)}) %all-to-all-start.1) | async-done | bytes 16416 | tf_op jit(solution)/shard_map/all_to_all | solution.py:565
  47.6 1.5 %collective-permute-done.7.rest_3_ = f32[4,128,128]{2,1,0:T(8,128)S(1)} collective-permute-done((f32[4,128,128]{2,1,0:T(8,128)S(1)}, f32[4,128,128]{2,1,0:T(8,128)S(1)}, u32[]{:S(2)}, u32[]{:S(2)}) %collective-permute-start.7) | collective-permute-done | bytes 262176 | tf_op jit(solution)/shard_map/ppermute | solution.py:509
  49.1 1.0 %shard_map.75 = (f32[128,512]{1,0:T(8,128)}, f32[128,512]{1,0:T(8,128)}) custom-call(f32[32,1,128]{2,1,0:T(1,128)S(1)} %all-to-all-done.1.recv_ref, f32[4,128,128]{2,1,0:T(8,128)S(1)} %get-tuple-element.47.rest_0_, f32[4,128,128]{2,1,0:T(8,128)S(1)} %collective-permute-done.6.rest_1_, f32[4,128,128]{2,1,0:T(8,128)S(1)} %collective-permute-done.5.rest_2_, ...), custom_call_target="tpu_custom_call" | custom-call | tf_op jit(solution)/shard_map/pallas_call | solution.py:569
  (9 shorter events, 0.0 us)
Async XLA Ops:
  0.6 5.4 %copy-start = (f32[128,512]{1,0:T(8,128)S(1)}, f32[128,512]{1,0:T(8,128)}, u32[]{:S(2)}) copy-start(f32[128,512]{1,0:T(8,128)} %depth_ref.1) | copy-start | bytes 786436
  0.6 5.4 %copy-start.1 = (f32[128,512]{1,0:T(8,128)S(1)}, f32[128,512]{1,0:T(8,128)}, u32[]{:S(2)}) copy-start(f32[128,512]{1,0:T(8,128)} %albedo_ref.1) | copy-start | bytes 786436
  0.7 5.4 %copy-start.2 = (s32[128,512]{1,0:T(8,128)S(1)}, s32[128,512]{1,0:T(8,128)}, u32[]{:S(2)}) copy-start(s32[128,512]{1,0:T(8,128)} %valid_ref.1) | copy-start | bytes 786436
  2.9 3.2 %collective-permute-start = (bf16[1072,128]{1,0:T(8,128)(2,1)S(1)}, bf16[1072,128]{1,0:T(8,128)(2,1)S(1)}, u32[]{:S(2)}, u32[]{:S(2)}) collective-permute-start(bf16[1072,128]{1,0:T(8,128)(2,1)S(1)} %get-tuple-element.26), channel_id=1, source_target_pairs={{0,8},{8,0},{16,24},{24,16},{1,9},{9,1},{17,25},{25,17},{2,10},{10... | collective-permute-start | bytes 823304 | tf_op jit(solution)/shard_map/ppermute | solution.py:509
  3.4 11.0 %collective-permute-start.2 = (bf16[1056,128]{1,0:T(8,128)(2,1)S(1)}, bf16[1056,128]{1,0:T(8,128)(2,1)S(1)}, u32[]{:S(2)}, u32[]{:S(2)}) collective-permute-start(bf16[1056,128]{1,0:T(8,128)(2,1)S(1)} %get-tuple-element.34), channel_id=1, source_target_pairs={{0,16},{8,24},{16,0},{24,8},{1,17},{9,25},{17,1},{25,9},{2,18},{10... | collective-permute-start | bytes 811016 | tf_op jit(solution)/shard_map/ppermute | solution.py:509
  6.0 12.6 %collective-permute-start.3 = (bf16[1056,128]{1,0:T(8,128)(2,1)S(1)}, bf16[1056,128]{1,0:T(8,128)(2,1)S(1)}, u32[]{:S(2)}, u32[]{:S(2)}) collective-permute-start(bf16[1056,128]{1,0:T(8,128)(2,1)S(1)} %get-tuple-element.36), channel_id=1, source_target_pairs={{0,24},{8,16},{16,8},{24,0},{1,25},{9,17},{17,9},{25,1},{2,26},{10... | collective-permute-start | bytes 811016 | tf_op jit(solution)/shard_map/ppermute | solution.py:509
  6.3 5.1 %collective-permute-start.1 = (f32[24,128]{1,0:T(8,128)S(1)}, f32[24,128]{1,0:T(8,128)S(1)}, u32[]{:S(2)}, u32[]{:S(2)}) collective-permute-start(f32[24,128]{1,0:T(8,128)S(1)} %get-tuple-element.30), channel_id=1, source_target_pairs={{0,1},{9,8},{16,17},{25,24},{1,2},{10,9},{17,18},{26,25},{2,3},{11... | collective-permute-start | bytes 36872 | tf_op jit(solution)/shard_map/ppermute | solution.py:537
  11.4 8.2 %collective-permute-start.4 = (f32[24,128]{1,0:T(8,128)S(1)}, f32[24,128]{1,0:T(8,128)S(1)}, u32[]{:S(2)}, u32[]{:S(2)}) collective-permute-start(f32[24,128]{1,0:T(8,128)S(1)} %collective-permute-done.1.strip_ref.direct_ref), channel_id=1, source_target_pairs={{0,16},{8,24},{16,0},{24,8},{1,17},{9,25},{17,1},{25,9},{2,18},{10... | collective-permute-start | bytes 36872 | tf_op jit(solution)/shard_map/ppermute | solution.py:509
  37.2 10.3 %collective-permute-start.5 = (f32[4,128,128]{2,1,0:T(8,128)S(1)}, f32[4,128,128]{2,1,0:T(8,128)S(1)}, u32[]{:S(2)}, u32[]{:S(2)}) collective-permute-start(f32[4,128,128]{2,1,0:T(8,128)S(1)} %get-tuple-element.47.rest_0_), channel_id=1, source_target_pairs={{0,16},{8,24},{16,0},{24,8},{1,17},{9,25},{17,1},{25,9},{2,18},{10... | collective-permute-start | bytes 786440 | tf_op jit(solution)/shard_map/ppermute | solution.py:509
  37.9 9.6 %all-to-all-start.1 = ((f32[32,1,128]{2,1,0:T(1,128)}), f32[32,1,128]{2,1,0:T(1,128)S(1)}, u32[]{:S(2)}, u32[]{:S(2)}) async-start(f32[32,1,128]{2,1,0:T(1,128)} %get-tuple-element.46), calls=%async_computation.1 | async-start | bytes 32768 | tf_op jit(solution)/shard_map/all_to_all | solution.py:565
  40.5 7.1 %collective-permute-start.6 = (f32[4,128,128]{2,1,0:T(8,128)S(1)}, f32[4,128,128]{2,1,0:T(8,128)S(1)}, u32[]{:S(2)}, u32[]{:S(2)}) collective-permute-start(f32[4,128,128]{2,1,0:T(8,128)S(1)} %get-tuple-element.47.rest_0_), channel_id=1, source_target_pairs={{0,8},{8,0},{16,24},{24,16},{1,9},{9,1},{17,25},{25,17},{2,10},{10... | collective-permute-start | bytes 786440 | tf_op jit(solution)/shard_map/ppermute | solution.py:509
  47.6 1.5 %collective-permute-start.7 = (f32[4,128,128]{2,1,0:T(8,128)S(1)}, f32[4,128,128]{2,1,0:T(8,128)S(1)}, u32[]{:S(2)}, u32[]{:S(2)}) collective-permute-start(f32[4,128,128]{2,1,0:T(8,128)S(1)} %collective-permute-done.5.rest_2_), channel_id=1, source_target_pairs={{0,8},{8,0},{16,24},{24,16},{1,9},{9,1},{17,25},{25,17},{2,10},{10... | collective-permute-start | bytes 786440 | tf_op jit(solution)/shard_map/ppermute | solution.py:509

commit v7 on v6

--- a/solution.py
+++ b/solution.py
@@ -45,26 +45,31 @@
 
 
 UNDER = 16
-
-
-def block_rows(lights, rows, k):
-    return lights * rows + UNDER + 2 * lights + (2 * lights if k == 1 else 0)
+LATE = 2
+
+
+def block_rows(lights, rows, k, nl):
+    here = lights - LATE if k == nl - 1 else lights
+    return here * rows + UNDER + 2 * lights + (2 * lights if k == 1 else 0)
 
 
 def cut_body(nl, obs_ref, table_ref, *rest):
-    blocks, (end_ref, table, eh_ref, sems, extra) = rest[:nl], rest[nl:]
+    blocks, (late_ref, end_ref, table, eh_ref, sems, extra) = rest[:nl], rest[nl:]
     lights, rows, cols = obs_ref.shape
     w = cols // nl
     li = lax.axis_index("light")
+    here = [lights_of(block, rows) for block in blocks]
+
+    def slot(k, l):
+        if l < here[k]:
+            return blocks[k].at[pl.ds(l * rows, rows)]
+        return late_ref.at[pl.ds((l - here[k]) * rows, rows)]
+
     copies = []
     for k in (2, 3, 1, 0):
         for l in range(lights):
             at = pl.ds(pl.multiple_of((li ^ k) * w, w), w)
-            copies.append(
-                pltpu.make_async_copy(
-                    obs_ref.at[l, :, at], blocks[k].at[pl.ds(l * rows, rows)], sems.at[k * lights + l]
-                )
-            )
+            copies.append(pltpu.make_async_copy(obs_ref.at[l, :, at], slot(k, l), sems.at[k * lights + l]))
             copies[-1].start()
     fetch = pltpu.make_async_copy(table_ref, table, extra.at[0])
     fetch.start()
@@ -78,7 +83,7 @@
     wide = jnp.concatenate([both, jnp.zeros((8, w - lights), F32)], axis=1)
     under = jnp.concatenate([wide, jnp.zeros((UNDER - 8, w), F32)], axis=0).astype(jnp.bfloat16)
     for k in range(nl):
-        blocks[k][pl.ds(lights * rows, UNDER), :] = under
+        blocks[k][pl.ds(here[k] * rows, UNDER), :] = under
     for copy in copies:
         copy.wait()
     for k in range(nl):
@@ -86,7 +91,7 @@
         for l in range(lights):
             e = lax.dot_general(
                 pick,
-                blocks[k][pl.ds(l * rows, rows), :],
+                slot(k, l)[...],
                 (((1,), (1,)), ((), ())),
                 preferred_element_type=F32,
             )
@@ -94,8 +99,8 @@
             eh_ref[q + 2, l : l + 1, :] = e[1:2]
     ends = jnp.concatenate([eh_ref[nl + 1, 0:lights, :], eh_ref[0, lights:, :]], axis=0)
     end_ref[...] = ends
-    halo = pl.ds(lights * rows + UNDER, 2 * lights)
     for k in range(nl):
+        halo = pl.ds(here[k] * rows + UNDER, 2 * lights)
         blocks[k][halo, :] = eh_ref[(li ^ k) + 1].astype(jnp.bfloat16)
     blocks[1][pl.ds(lights * rows + UNDER + 2 * lights, 2 * lights), :] = ends.astype(jnp.bfloat16)
 
@@ -195,13 +200,13 @@
     return block_ref.shape[0] // rows
 
 
-def table_rows(block_ref, n, rows):
-    under = block_ref[pl.ds(n * rows, UNDER), :].astype(F32)
+def table_rows(block_ref, rows):
+    under = block_ref[pl.ds(lights_of(block_ref, rows) * rows, UNDER), :].astype(F32)
     return under[0:4] * 32.0 + under[4:8]
 
 
 def fill_params(pb_ref, base, block_ref, n, rows, w, place, total):
-    lx, ly, lz, le = decode_rows(table_rows(block_ref, n, rows))
+    lx, ly, lz, le = decode_rows(table_rows(block_ref, rows))
     col = iota((8, w), 1) + place * w
     px = (col.astype(F32) + 0.5) / total - 0.5
     for j in range(n):
@@ -213,20 +218,24 @@
         pb_ref[base + j, 4] = jnp.broadcast_to(le[:, j : j + 1], (8, w))
 
 
-def accumulate(state, tile, py, obs, pb_ref, base):
+def accumulate(state, tile, py, lights):
     surface, sx, sy, scaled = tile
     kept = []
     least = None
-    for j in range(len(obs)):
-        dx, dx2 = pb_ref[base + j, 0], pb_ref[base + j, 1]
-        dy = pb_ref[base + j, 2] - py
-        dz = pb_ref[base + j, 3] - surface
-        dist = (dx2 + dy * dy) + dz * dz
+    for obs, pb, across in lights:
+        dx = pb(0)
+        dy = pb(2) - py
+        dz = pb(3) - surface
+        flat = across(None)
+        if flat is None:
+            flat = pb(1) + dy * dy
+            across(flat)
+        dist = flat + dz * dz
         facing = dz - (sx * dx + sy * dy)
         r = lax.rsqrt(dist)
         r2 = r * r
-        g = (r2 * r) * pb_ref[base + j, 4]
-        residual = scaled * (g * facing) - obs[j]
+        g = (r2 * r) * pb(4)
+        residual = scaled * (g * facing) - obs
         square = residual * residual
         least = square if least is None else jnp.minimum(least, square)
         kept.append((square, residual * g, facing, dz * r2, dx, dy))
@@ -246,9 +255,8 @@
     return (least,) + sums
 
 
-def sweep(ctx_ref, params, obs_refs, total, load, store):
+def sweep(ctx_ref, chunks, total, load, store, known):
     rows, w = ctx_ref.shape[1:]
-    lights = lights_of(obs_refs[0], rows)
     split = (TR // 8, 8, w)
 
     def step(i, carry):
@@ -256,17 +264,31 @@
         tile = tuple(ctx_ref[f, at, :].reshape(split) for f in range(4))
         row = iota(split, 0) * 8 + iota(split, 1) + i * TR
         py = (row.astype(F32) + (0.5 - rows / 2.0)) / total
+
+        def light(entry):
+            (obs_ref, j), (pb_ref, p), (flat_ref, f) = entry
+            obs = obs_ref[pl.ds(pl.multiple_of(j * rows + i * TR, TR), TR), :].astype(F32).reshape(split)
+
+            def across(value):
+                if known:
+                    return flat_ref[f, at, :].reshape(split)
+                if value is not None:
+                    flat_ref[f, at, :] = value.reshape(TR, w)
+                return None
+
+            return obs, lambda field: pb_ref[p, field], across
+
         state = load(at)
-        for obs_ref, (pb_ref, base) in zip(obs_refs, params):
-            obs = [
-                obs_ref[pl.ds(pl.multiple_of(j * rows + i * TR, TR), TR), :].astype(F32).reshape(split)
-                for j in range(lights)
-            ]
-            state = accumulate(state, tile, py, obs, pb_ref, base)
+        for chunk in chunks:
+            state = accumulate(state, tile, py, [light(entry) for entry in chunk])
         store(at, state)
         return carry
 
     lax.fori_loop(0, rows // TR, step, 0)
+
+
+def chunk_of(obs_ref, pb_ref, flat_ref, count, pb_at=0, flat_at=0):
+    return [((obs_ref, j), (pb_ref, pb_at + j), (flat_ref, flat_at + j)) for j in range(count)]
 
 
 def state_load(state_ref, w):
@@ -353,7 +375,7 @@
     return lax.rsqrt(d / count + EPS), lax.rsqrt(a / count + EPS)
 
 
-def first_body(nl, tile_ref, sr_ref, strip_ref, obs0, obs1, ctx_ref, srow_ref, state_ref, pb_ref):
+def first_body(nl, tile_ref, sr_ref, strip_ref, obs0, obs1, ctx_ref, srow_ref, state_ref, pb_ref, flat_ref):
     li, _, place, count = position()
     rows, w = ctx_ref.shape[1:]
     srow_ref[...] = sr_ref[...]
@@ -376,23 +398,38 @@
     n = lights_of(obs0, rows)
     fill_params(pb_ref, 0, obs0, n, rows, w, place, total)
     fill_params(pb_ref, n, obs1, n, rows, w, place, total)
-    sweep(ctx_ref, ((pb_ref, 0), (pb_ref, n)), (obs0, obs1), total, lambda at: None, state_store(state_ref, w))
-
-
-def more_body(ctx_ref, in_ref, obs, state_ref, pb_ref):
+    chunks = [chunk_of(obs0, pb_ref, flat_ref, n), chunk_of(obs1, pb_ref, flat_ref, n, n, n)]
+    sweep(ctx_ref, chunks, total, lambda at: None, state_store(state_ref, w), False)
+
+
+def more_body(ctx_ref, in_ref, obs, state_ref, pb_ref, flat_ref):
     _, _, place, count = position()
     rows, w = ctx_ref.shape[1:]
     total = w * count
-    fill_params(pb_ref, 0, obs, lights_of(obs, rows), rows, w, place, total)
-    sweep(ctx_ref, ((pb_ref, 0),), (obs,), total, state_load(in_ref, w), state_store(state_ref, w))
-
-
-def finish(state_ref, ctx_ref, albedo, valid, pack_ref, srow_ref, grad_ref, edge_ref, pay_ref):
+    fill_params(pb_ref, 0, obs, pb_ref.shape[0], rows, w, place, total)
+    chunks = [chunk_of(obs, pb_ref, flat_ref, lights_of(obs, rows))]
+    sweep(ctx_ref, chunks, total, state_load(in_ref, w), state_store(state_ref, w), False)
+
+
+def late_body(ctx_ref, in_ref, obs, pb_ref, state_ref, flat_ref):
+    _, _, _, count = position()
+    rows, w = ctx_ref.shape[1:]
+    n = lights_of(obs, rows)
+    chunks = [chunk_of(obs, pb_ref, flat_ref, n, pb_ref.shape[0] - n)]
+    sweep(ctx_ref, chunks, w * count, state_load(in_ref, w), state_store(state_ref, w), False)
+
+
+def halo_slopes(pack_ref, srow_ref, rows, w):
     _, _, place, count = position()
-    rows, w = ctx_ref.shape[1:]
     total = w * count
     low = halo_slope(place * w - 1, 0, pack_ref, srow_ref, rows, total)
     high = halo_slope(place * w + w, 1, pack_ref, srow_ref, rows, total)
+    return low, high
+
+
+def finish(state_ref, ctx_ref, albedo, valid, low, high, grad_ref, edge_ref, pay_ref):
+    _, _, place, count = position()
+    rows, w = ctx_ref.shape[1:]
     depth, grad_albedo = gradients(state_ref, ctx_ref, albedo, valid, low, high)
     sums = partial_sums(depth, grad_albedo)
     if edge_ref is None:
@@ -417,32 +454,35 @@
     return depth, grad_albedo
 
 
-def fill_pack(nl, pack_ref, block_refs, direct_ref, relayed_ref, rows, w):
+def sides_body(nl, srow_ref, direct_ref, relayed_ref, *rest):
+    block_refs, (pack_ref, slope_ref) = rest[:nl], rest[nl:]
     li = lax.axis_index("light")
-    n = lights_of(block_refs[0], rows)
+    w = block_refs[0].shape[1]
+    rows = srow_ref.shape[1]
+    n = (direct_ref.shape[0] - 8) // 2
     table = jnp.zeros((4, w), F32)
     for k in range(nl):
-        halo = block_refs[k][pl.ds(n * rows + UNDER, 2 * n), :].astype(F32)
+        halo = block_refs[k][pl.ds(lights_of(block_refs[k], rows) * rows + UNDER, 2 * n), :].astype(F32)
         beyond = (direct_ref if k < 2 else relayed_ref)[(k % 2) * n : (k % 2 + 1) * n, :]
         pack_ref[0, k * n : (k + 1) * n, :] = jnp.where(li == 0, beyond, halo[0:n])
         pack_ref[1, k * n : (k + 1) * n, :] = jnp.where(li == nl - 1, beyond, halo[n:])
-        entries = jnp.concatenate([table_rows(block_refs[k], n, rows)] * 2, axis=0)
+        entries = jnp.concatenate([table_rows(block_refs[k], rows)] * 2, axis=0)
         table = table + (pltpu.roll(entries, k * n, 1) if k else entries)[0:4]
     tall = jnp.concatenate([table, jnp.zeros((w - 4, w), F32)], axis=0)
     pack_ref[2] = jnp.transpose(tall)[0 : nl * n]
-
-
-def last_body(nl, ctx_ref, tile_ref, state_ref, srow_ref, direct_ref, relayed_ref, *rest):
-    block_refs, (grad_ref, edge_ref, pay_ref, pack_ref) = rest[:nl], rest[nl:]
-    rows, w = ctx_ref.shape[1:]
-    fill_pack(nl, pack_ref, block_refs, direct_ref, relayed_ref, rows, w)
+    slope_ref[0:1, :], slope_ref[1:2, :] = halo_slopes(pack_ref, srow_ref, rows, w)
+
+
+def last_body(ctx_ref, tile_ref, state_ref, slope_ref, grad_ref, edge_ref, pay_ref):
     edge_ref[...] = jnp.zeros_like(edge_ref)
-    finish(state_ref, ctx_ref, tile_ref[1], tile_ref[2], pack_ref, srow_ref, grad_ref, edge_ref, pay_ref)
+    finish(
+        state_ref, ctx_ref, tile_ref[1], tile_ref[2], slope_ref[0:1, :], slope_ref[1:2, :], grad_ref, edge_ref, pay_ref
+    )
 
 
 def second_body(nl, recv_ref, grad_ref, edge_ref, tile_ref, srow0_ref, pack_ref, *rest):
-    obs_refs, pb_refs = rest[:nl], rest[nl : 2 * nl - 1]
-    out_ref, pay_ref, ctx_ref, state_ref, srow_ref = rest[2 * nl - 1 :]
+    obs_refs, pb_refs, flat_refs = rest[: nl + 1], rest[nl + 1 : 2 * nl], rest[2 * nl : 3 * nl]
+    out_ref, pay_ref, ctx_ref, state_ref, srow_ref = rest[3 * nl :]
     _, _, place, count = position()
     rows, w = ctx_ref.shape[1:]
     total = w * count
@@ -475,11 +515,19 @@
     srow_ref[8:16, :] = srow0_ref[8:16, :]
     fill_context(ctx_ref, surface, albedo, srow_ref[1:2, :], srow_ref[4:5, :])
     n = lights_of(obs_refs[0], rows)
-    params = ((pb_refs[0], 0), (pb_refs[0], n)) + tuple((ref, 0) for ref in pb_refs[1:])
-    sweep(ctx_ref, params, obs_refs, total, lambda at: None, state_store(state_ref, w))
-    depth, grad_albedo = finish(
-        state_ref, ctx_ref, albedo, tile_ref[2], pack_ref, srow_ref, None, None, pay_ref
-    )
+    chunks = [
+        chunk_of(obs_refs[0], pb_refs[0], flat_refs[0], n),
+        chunk_of(obs_refs[1], pb_refs[0], flat_refs[0], n, n, n),
+    ]
+    chunks += [chunk_of(obs_refs[k], pb_refs[k - 1], flat_refs[k - 1], n) for k in range(2, nl - 1)]
+    late = lights_of(obs_refs[nl], rows)
+    chunks.append(
+        chunk_of(obs_refs[nl - 1], pb_refs[-1], flat_refs[-2], n - late)
+        + chunk_of(obs_refs[nl], pb_refs[-1], flat_refs[-1], late, n - late)
+    )
+    sweep(ctx_ref, chunks, total, lambda at: None, state_store(state_ref, w), True)
+    low, high = halo_slopes(pack_ref, srow_ref, rows, w)
+    depth, grad_albedo = finish(state_ref, ctx_ref, albedo, tile_ref[2], low, high, None, None, pay_ref)
     out_ref[2] = depth
     out_ref[3] = grad_albedo
 
@@ -510,10 +558,10 @@
 
     hbm = pl.BlockSpec(memory_space=pltpu.HBM)
     field = (rows, w)
-    *blocks, end = call(
+    *blocks, late, end = call(
         functools.partial(cut_body, nl),
-        tuple(shape(block_rows(lights, rows, k), w, dtype=jnp.bfloat16) for k in range(nl))
-        + (shape(2 * lights, rows),),
+        tuple(shape(block_rows(lights, rows, k, nl), w, dtype=jnp.bfloat16) for k in range(nl))
+        + (shape(LATE * rows, w, dtype=jnp.bfloat16), shape(2 * lights, rows)),
         [
             pltpu.VMEM((4, lights), jnp.int32),
             pltpu.VMEM((nl + 2, 2 * lights, rows), F32),
@@ -536,20 +584,23 @@
             pairs.append((l * ns + source, l * ns + target))
     direct = lax.ppermute(strip, AXES, pairs)
     relayed = swap(direct, 2)
+    late = swap(late, 3)
 
     def tiles(n):
         return shape(n, 5, 8, w)
 
-    ctx, srow, state, pb0 = call(
-        functools.partial(first_body, nl), (shape(4, *field), shape(16, rows), shape(7, *field), tiles(2 * lights))
+    ctx, srow, state, pb0, flat0 = call(
+        functools.partial(first_body, nl),
+        (shape(4, *field), shape(16, rows), shape(7, *field), tiles(2 * lights), shape(2 * lights, *field)),
     )(tile, sr, direct, obs0, obs1)
-    more = (shape(7, *field), tiles(lights))
-    state, pb2 = call(more_body, more)(ctx, state, obs2)
-    state, pb3 = call(more_body, more)(ctx, state, obs3)
-    grad, edge, pay, pack = call(
-        functools.partial(last_body, nl),
-        (shape(2, *field), shape(8, rows), shape(nd, 4, rows), shape(3, nl * lights, rows)),
-    )(ctx, tile, state, srow, direct, relayed, obs0, obs1, obs2, obs3)
+    early = lights - LATE
+    state, pb2, flat2 = call(more_body, (shape(7, *field), tiles(lights), shape(lights, *field)))(ctx, state, obs2)
+    state, pb3, flat3 = call(more_body, (shape(7, *field), tiles(lights), shape(early, *field)))(ctx, state, obs3)
+    pack, slope = call(
+        functools.partial(sides_body, nl), (shape(3, nl * lights, rows), shape(8, rows))
+    )(srow, direct, relayed, obs0, obs1, obs2, obs3)
+    state, flat4 = call(late_body, (shape(7, *field), shape(LATE, *field)))(ctx, state, late, pb3)
+    grad, edge, pay = call(last_body, (shape(2, *field), shape(8, rows), shape(nd, 4, rows)))(ctx, tile, state, slope)
     recv = lax.all_to_all(pay, AXES, 0, 0, tiled=True)
     own, pay = call(
         functools.partial(second_body, nl),
@@ -559,7 +610,7 @@
             pltpu.VMEM((7, *field), F32),
             pltpu.VMEM((16, rows), F32),
         ],
-    )(recv, grad, edge, tile, srow, pack, obs0, obs1, obs2, obs3, pb0, pb2, pb3)
+    )(recv, grad, edge, tile, srow, pack, obs0, obs1, obs2, obs3, late, pb0, pb2, pb3, flat0, flat2, flat3, flat4)
     part2 = swap(own, 2)
     part1 = swap(own, 1)
     recv = lax.all_to_all(pay, AXES, 0, 0, tiled=True)

time: 50.3 us -> 50 us (level)
  waiting for transfers between devices: 13 us -> 11.9 us
    ppermute x7 -> x8, waiting for transfers between devices: 4.75 us -> 3.65 us  [swap(): return lax.ppermute(x, 'light', [(i, i ^ k) for i in range(nl)])]
    ppermute x7 -> x8, starting transfers between devices: 5.52 us -> 6.27 us  [swap(): return lax.ppermute(x, 'light', [(i, i ^ k) for i in range(nl)])]
    pallas_call x3 -> x5, Pallas kernels: 2.36 us -> 2.61 us  [the longest x1 0.92 us: program(): call(more_body, (shape(7, *field), tiles(lights), shape(lights, *field)))]
  transfers between devices with their start and end apart: 9 -> 10, of which waited for: 4 -> 6; matrix products, arithmetic and copies ran while one was open for 0% -> 0% of each run, Pallas kernels for 7% -> 8%
where the time goes in v7:
time: 50 us; the launch traced here: 49.8 us
  blocking collectives  13.2 us (26%)
  starting transfers between devices  12.2 us (24%)
  waiting for transfers between devices  11.9 us (24%)
  Pallas kernels  11.7 us (23%)
  between operations  0.75 us (2%)
    all_to_all x1, blocking collectives, program(): recv = lax.all_to_all(pay, AXES, 0, 0, tiled=True)  13.2 us
    all_to_all x1, waiting for transfers between devices, program(): recv = lax.all_to_all(pay, AXES, 0, 0, tiled=True)  6.89 us
    ppermute x8, starting transfers between devices, swap(): return lax.ppermute(x, 'light', [(i, i ^ k) for i in range(nl)])  6.27 us
    pallas_call x1, Pallas kernels, program(): call(functools.partial(second_body, nl), (shape(4, *field), shape(nd, 1,...  4.01 us
    ppermute x8, waiting for transfers between devices, swap(): return lax.ppermute(x, 'light', [(i, i ^ k) for i in range(nl)])  3.65 us
    ppermute x1, starting transfers between devices, program(): direct = lax.ppermute(strip, AXES, pairs)  3.43 us
    all_to_all x1, starting transfers between devices, program(): recv = lax.all_to_all(pay, AXES, 0, 0, tiled=True)  2.54 us
    pallas_call x1, Pallas kernels, program(): call(functools.partial(cut_body, nl), tuple((shape(block_rows(lights, row...  2.22 us
  transfers between devices with their start and end apart: 10, of which 6 were waited for; matrix products, arithmetic and copies ran while one was open for 0% of the time, Pallas kernels for 8%

profile of v7, /device:TPU:0, one launch (start us, length us, event | category | flops | bytes accessed | tf_op | source)
XLA Modules:
  0.0 49.8 jit_solution(6414732577989715651)
XLA Ops:
  0.7 2.2 %shard_map.68 = (bf16[1056,128]{1,0:T(8,128)(2,1)S(1)}, bf16[1072,128]{1,0:T(8,128)(2,1)S(1)}, bf16[1056,128]{1,0:T(8,128)(2,1)S(1)}, bf16[800,128]{1,0:T(8,128)...) custom-call(bf16[8,128,512]{2,1,0:T(8,128)(2,1)} %obs_ref.1, s32[4,8]{1,0:T(4,128)} %bitcast.1), custom_call_target="tpu_custom_call" | custom-call | tf_op jit(solution)/shard_map/pallas_call | solution.py:561
  2.9 0.6 %collective-permute-start = (bf16[1072,128]{1,0:T(8,128)(2,1)S(1)}, bf16[1072,128]{1,0:T(8,128)(2,1)S(1)}, u32[]{:S(2)}, u32[]{:S(2)}) collective-permute-start(bf16[1072,128]{1,0:T(8,128)(2,1)S(1)} %get-tuple-element.33), channel_id=1, source_target_pairs={{0,8},{8,0},{16,24},{24,16},{1,9},{9,1},{17,25},{25,17},{2,10},{10... | collective-permute-start | bytes 823304 | tf_op jit(solution)/shard_map/ppermute | solution.py:557
  3.4 2.6 %collective-permute-start.2 = (bf16[1056,128]{1,0:T(8,128)(2,1)S(1)}, bf16[1056,128]{1,0:T(8,128)(2,1)S(1)}, u32[]{:S(2)}, u32[]{:S(2)}) collective-permute-start(bf16[1056,128]{1,0:T(8,128)(2,1)S(1)} %get-tuple-element.41), channel_id=1, source_target_pairs={{0,16},{8,24},{16,0},{24,8},{1,17},{9,25},{17,1},{25,9},{2,18},{10... | collective-permute-start | bytes 811016 | tf_op jit(solution)/shard_map/ppermute | solution.py:557
  6.0 1.7 %collective-permute-start.4 = (bf16[256,128]{1,0:T(8,128)(2,1)S(1)}, bf16[256,128]{1,0:T(8,128)(2,1)S(1)}, u32[]{:S(2)}, u32[]{:S(2)}) collective-permute-start(bf16[256,128]{1,0:T(8,128)(2,1)S(1)} %get-tuple-element.45), channel_id=1, source_target_pairs={{0,24},{8,16},{16,8},{24,0},{1,25},{9,17},{17,9},{25,1},{2,26},{10... | collective-permute-start | bytes 196616 | tf_op jit(solution)/shard_map/ppermute | solution.py:557
  7.8 0.2 shard_map.69
  8.0 3.4 %collective-permute-start.1 = (f32[24,128]{1,0:T(8,128)S(1)}, f32[24,128]{1,0:T(8,128)S(1)}, u32[]{:S(2)}, u32[]{:S(2)}) collective-permute-start(f32[24,128]{1,0:T(8,128)S(1)} %get-tuple-element.37), channel_id=1, source_target_pairs={{0,1},{9,8},{16,17},{25,24},{1,2},{10,9},{17,18},{26,25},{2,3},{11... | collective-permute-start | bytes 36872 | tf_op jit(solution)/shard_map/ppermute | solution.py:585
  11.4 1.4 %collective-permute-done.1.strip_ref.direct_ref = f32[24,128]{1,0:T(8,128)S(1)} collective-permute-done((f32[24,128]{1,0:T(8,128)S(1)}, f32[24,128]{1,0:T(8,128)S(1)}, u32[]{:S(2)}, u32[]{:S(2)}) %collective-permute-start.1) | collective-permute-done | bytes 12320 | tf_op jit(solution)/shard_map/ppermute | solution.py:585
  12.8 0.5 %collective-permute-start.5 = (f32[24,128]{1,0:T(8,128)S(1)}, f32[24,128]{1,0:T(8,128)S(1)}, u32[]{:S(2)}, u32[]{:S(2)}) collective-permute-start(f32[24,128]{1,0:T(8,128)S(1)} %collective-permute-done.1.strip_ref.direct_ref), channel_id=1, source_target_pairs={{0,16},{8,24},{16,0},{24,8},{1,17},{9,25},{17,1},{25,9},{2,18},{10... | collective-permute-start | bytes 36872 | tf_op jit(solution)/shard_map/ppermute | solution.py:557
  13.4 1.6 %shard_map.70 = (f32[4,128,128]{2,1,0:T(8,128)S(1)}, f32[16,128]{1,0:T(8,128)S(1)}, f32[7,128,128]{2,1,0:T(8,128)S(1)}, f32[16,5,8,128]{3,2,1,0:T(8,128)S(1)}, f32[16,128,128]{2,1,0:T(8,128)S(1)}) custom-call(f32[3,128,128]{2,1,0:T(8,128)S(1)} %get-tuple-element.35.tile_ref, f32[16,128]{1,0:T(8,128)S(1)} %get-tuple-element.36.sr_ref, ...), custom_call_target="tpu_custom_call" | custom-call | tf_op jit(solution)/shard_map/pallas_call | solution.py:592
  15.0 0.9 %shard_map.71 = (f32[7,128,128]{2,1,0:T(8,128)S(1)}, f32[8,5,8,128]{3,2,1,0:T(8,128)S(1)}, f32[8,128,128]{2,1,0:T(8,128)S(1)}) custom-call(f32[4,128,128]{2,1,0:T(8,128)S(1)} %get-tuple-element.39.ctx_ref, f32[7,128,128]{2,1,0:T(8,128)S(1)} %get-tuple-element.40.in_ref, bf16[1056,128]{1,0:T(8,128)(2,1)S(1)} %collective-permute-done.2.obs.rest_2_), custom_call_target="tpu_custom_call" | custom-call | tf_op jit(solution)/shard_map/pallas_call | solution.py:597
  15.9 1.4 %collective-permute-done.3.obs.rest_3_ = bf16[800,128]{1,0:T(8,128)(2,1)S(1)} collective-permute-done((bf16[800,128]{1,0:T(8,128)(2,1)S(1)}, bf16[800,128]{1,0:T(8,128)(2,1)S(1)}, u32[]{:S(2)}, u32[]{:S(2)}) %collective-permute-start.3) | collective-permute-done | bytes 204832 | tf_op jit(solution)/shard_map/ppermute | solution.py:557
  17.3 0.8 %shard_map.72 = (f32[7,128,128]{2,1,0:T(8,128)S(1)}, f32[8,5,8,128]{3,2,1,0:T(8,128)S(1)}, f32[6,128,128]{2,1,0:T(8,128)S(1)}) custom-call(f32[4,128,128]{2,1,0:T(8,128)S(1)} %get-tuple-element.39.ctx_ref, f32[7,128,128]{2,1,0:T(8,128)S(1)} %get-tuple-element.42.in_ref, bf16[800,128]{1,0:T(8,128)(2,1)S(1)} %collective-permute-done.3.obs.rest_3_), custom_call_target="tpu_custom_call" | custom-call | tf_op jit(solution)/shard_map/pallas_call | solution.py:598
  18.0 0.6 %collective-permute-done.4.obs.rest_4_ = bf16[256,128]{1,0:T(8,128)(2,1)S(1)} collective-permute-done((bf16[256,128]{1,0:T(8,128)(2,1)S(1)}, bf16[256,128]{1,0:T(8,128)(2,1)S(1)}, u32[]{:S(2)}, u32[]{:S(2)}) %collective-permute-start.4) | collective-permute-done | bytes 65568 | tf_op jit(solution)/shard_map/ppermute | solution.py:557
  18.6 0.4 shard_map.73
  19.1 0.3 shard_map.74
  19.4 0.3 shard_map.75
  19.7 13.2 %all_to_all.10.recv_ref = f32[32,4,128]{2,1,0:T(4,128)S(1)} all-to-all(f32[32,4,128]{2,1,0:T(4,128)S(1)} %get-tuple-element.50), channel_id=1, replica_groups=mesh['light'=4,'strip'=8] {'light','strip'}, dimensions={0} | all-to-all | bytes 131072 | tf_op jit(solution)/shard_map/all_to_all | solution.py:604
  32.9 4.0 %shard_map.76 = (f32[4,128,128]{2,1,0:T(8,128)S(1)}, f32[32,1,128]{2,1,0:T(1,128)}) custom-call(f32[32,4,128]{2,1,0:T(4,128)S(1)} %all_to_all.10.recv_ref, f32[2,128,128]{2,1,0:T(8,128)S(1)} %get-tuple-element.51.grad_ref, f32[8,128]{1,0:T(8,128)S(1)} %get-tuple-element.52.edge_ref, f32[3,128,128]{2,1,0:T(8,128)S(1)} %get-tuple-element.35.tile_ref, ...), custom_call_target="tpu_custom_call" | custom-call | tf_op jit(solution)/shard_map/pallas_call | solution.py:605
  36.9 0.7 %collective-permute-start.6 = (f32[4,128,128]{2,1,0:T(8,128)S(1)}, f32[4,128,128]{2,1,0:T(8,128)S(1)}, u32[]{:S(2)}, u32[]{:S(2)}) collective-permute-start(f32[4,128,128]{2,1,0:T(8,128)S(1)} %get-tuple-element.61.rest_0_), channel_id=1, source_target_pairs={{0,16},{8,24},{16,0},{24,8},{1,17},{9,25},{17,1},{25,9},{2,18},{10... | collective-permute-start | bytes 786440 | tf_op jit(solution)/shard_map/ppermute | solution.py:557
  37.6 2.5 %all-to-all-start.1 = ((f32[32,1,128]{2,1,0:T(1,128)}), f32[32,1,128]{2,1,0:T(1,128)S(1)}, u32[]{:S(2)}, u32[]{:S(2)}) async-start(f32[32,1,128]{2,1,0:T(1,128)} %get-tuple-element.60), calls=%async_computation.1 | async-start | bytes 32768 | tf_op jit(solution)/shard_map/all_to_all | solution.py:616
  40.2 0.2 collective-permute-start.7
  40.3 6.9 %all-to-all-done.1.recv_ref = f32[32,1,128]{2,1,0:T(1,128)S(1)} async-done(((f32[32,1,128]{2,1,0:T(1,128)}), f32[32,1,128]{2,1,0:T(1,128)S(1)}, u32[]{:S(2)}, u32[]{:S(2)}) %all-to-all-start.1) | async-done | bytes 16416 | tf_op jit(solution)/shard_map/all_to_all | solution.py:616
  47.2 1.5 %collective-permute-done.8.rest_3_ = f32[4,128,128]{2,1,0:T(8,128)S(1)} collective-permute-done((f32[4,128,128]{2,1,0:T(8,128)S(1)}, f32[4,128,128]{2,1,0:T(8,128)S(1)}, u32[]{:S(2)}, u32[]{:S(2)}) %collective-permute-start.8) | collective-permute-done | bytes 262176 | tf_op jit(solution)/shard_map/ppermute | solution.py:557
  48.8 1.0 %shard_map.77 = (f32[128,512]{1,0:T(8,128)}, f32[128,512]{1,0:T(8,128)}) custom-call(f32[32,1,128]{2,1,0:T(1,128)S(1)} %all-to-all-done.1.recv_ref, f32[4,128,128]{2,1,0:T(8,128)S(1)} %get-tuple-element.61.rest_0_, f32[4,128,128]{2,1,0:T(8,128)S(1)} %collective-permute-done.7.rest_1_, f32[4,128,128]{2,1,0:T(8,128)S(1)} %collective-permute-done.6.rest_2_, ...), custom_call_target="tpu_custom_call" | custom-call | tf_op jit(solution)/shard_map/pallas_call | solution.py:620
  (13 shorter events, 0.2 us)
Async XLA Ops:
  0.6 7.1 %copy-start = (f32[128,512]{1,0:T(8,128)S(1)}, f32[128,512]{1,0:T(8,128)}, u32[]{:S(2)}) copy-start(f32[128,512]{1,0:T(8,128)} %depth_ref.1) | copy-start | bytes 786436
  0.6 7.1 %copy-start.1 = (f32[128,512]{1,0:T(8,128)S(1)}, f32[128,512]{1,0:T(8,128)}, u32[]{:S(2)}) copy-start(f32[128,512]{1,0:T(8,128)} %albedo_ref.1) | copy-start | bytes 786436
  0.7 7.1 %copy-start.2 = (s32[128,512]{1,0:T(8,128)S(1)}, s32[128,512]{1,0:T(8,128)}, u32[]{:S(2)}) copy-start(s32[128,512]{1,0:T(8,128)} %valid_ref.1) | copy-start | bytes 786436
  2.9 4.9 %collective-permute-start = (bf16[1072,128]{1,0:T(8,128)(2,1)S(1)}, bf16[1072,128]{1,0:T(8,128)(2,1)S(1)}, u32[]{:S(2)}, u32[]{:S(2)}) collective-permute-start(bf16[1072,128]{1,0:T(8,128)(2,1)S(1)} %get-tuple-element.33), channel_id=1, source_target_pairs={{0,8},{8,0},{16,24},{24,16},{1,9},{9,1},{17,25},{25,17},{2,10},{10... | collective-permute-start | bytes 823304 | tf_op jit(solution)/shard_map/ppermute | solution.py:557
  3.4 11.5 %collective-permute-start.2 = (bf16[1056,128]{1,0:T(8,128)(2,1)S(1)}, bf16[1056,128]{1,0:T(8,128)(2,1)S(1)}, u32[]{:S(2)}, u32[]{:S(2)}) collective-permute-start(bf16[1056,128]{1,0:T(8,128)(2,1)S(1)} %get-tuple-element.41), channel_id=1, source_target_pairs={{0,16},{8,24},{16,0},{24,8},{1,17},{9,25},{17,1},{25,9},{2,18},{10... | collective-permute-start | bytes 811016 | tf_op jit(solution)/shard_map/ppermute | solution.py:557
  6.0 11.3 %collective-permute-start.3 = (bf16[800,128]{1,0:T(8,128)(2,1)S(1)}, bf16[800,128]{1,0:T(8,128)(2,1)S(1)}, u32[]{:S(2)}, u32[]{:S(2)}) collective-permute-start(bf16[800,128]{1,0:T(8,128)(2,1)S(1)} %get-tuple-element.43), channel_id=1, source_target_pairs={{0,24},{8,16},{16,8},{24,0},{1,25},{9,17},{17,9},{25,1},{2,26},{10... | collective-permute-start | bytes 614408 | tf_op jit(solution)/shard_map/ppermute | solution.py:557
  6.0 12.6 %collective-permute-start.4 = (bf16[256,128]{1,0:T(8,128)(2,1)S(1)}, bf16[256,128]{1,0:T(8,128)(2,1)S(1)}, u32[]{:S(2)}, u32[]{:S(2)}) collective-permute-start(bf16[256,128]{1,0:T(8,128)(2,1)S(1)} %get-tuple-element.45), channel_id=1, source_target_pairs={{0,24},{8,16},{16,8},{24,0},{1,25},{9,17},{17,9},{25,1},{2,26},{10... | collective-permute-start | bytes 196616 | tf_op jit(solution)/shard_map/ppermute | solution.py:557
  8.0 4.8 %collective-permute-start.1 = (f32[24,128]{1,0:T(8,128)S(1)}, f32[24,128]{1,0:T(8,128)S(1)}, u32[]{:S(2)}, u32[]{:S(2)}) collective-permute-start(f32[24,128]{1,0:T(8,128)S(1)} %get-tuple-element.37), channel_id=1, source_target_pairs={{0,1},{9,8},{16,17},{25,24},{1,2},{10,9},{17,18},{26,25},{2,3},{11... | collective-permute-start | bytes 36872 | tf_op jit(solution)/shard_map/ppermute | solution.py:585
  12.8 6.3 %collective-permute-start.5 = (f32[24,128]{1,0:T(8,128)S(1)}, f32[24,128]{1,0:T(8,128)S(1)}, u32[]{:S(2)}, u32[]{:S(2)}) collective-permute-start(f32[24,128]{1,0:T(8,128)S(1)} %collective-permute-done.1.strip_ref.direct_ref), channel_id=1, source_target_pairs={{0,16},{8,24},{16,0},{24,8},{1,17},{9,25},{17,1},{25,9},{2,18},{10... | collective-permute-start | bytes 36872 | tf_op jit(solution)/shard_map/ppermute | solution.py:557
  36.9 10.3 %collective-permute-start.6 = (f32[4,128,128]{2,1,0:T(8,128)S(1)}, f32[4,128,128]{2,1,0:T(8,128)S(1)}, u32[]{:S(2)}, u32[]{:S(2)}) collective-permute-start(f32[4,128,128]{2,1,0:T(8,128)S(1)} %get-tuple-element.61.rest_0_), channel_id=1, source_target_pairs={{0,16},{8,24},{16,0},{24,8},{1,17},{9,25},{17,1},{25,9},{2,18},{10... | collective-permute-start | bytes 786440 | tf_op jit(solution)/shard_map/ppermute | solution.py:557
  37.6 9.6 %all-to-all-start.1 = ((f32[32,1,128]{2,1,0:T(1,128)}), f32[32,1,128]{2,1,0:T(1,128)S(1)}, u32[]{:S(2)}, u32[]{:S(2)}) async-start(f32[32,1,128]{2,1,0:T(1,128)} %get-tuple-element.60), calls=%async_computation.1 | async-start | bytes 32768 | tf_op jit(solution)/shard_map/all_to_all | solution.py:616
  40.2 7.1 %collective-permute-start.7 = (f32[4,128,128]{2,1,0:T(8,128)S(1)}, f32[4,128,128]{2,1,0:T(8,128)S(1)}, u32[]{:S(2)}, u32[]{:S(2)}) collective-permute-start(f32[4,128,128]{2,1,0:T(8,128)S(1)} %get-tuple-element.61.rest_0_), channel_id=1, source_target_pairs={{0,8},{8,0},{16,24},{24,16},{1,9},{9,1},{17,25},{25,17},{2,10},{10... | collective-permute-start | bytes 786440 | tf_op jit(solution)/shard_map/ppermute | solution.py:557
  47.2 1.5 %collective-permute-start.8 = (f32[4,128,128]{2,1,0:T(8,128)S(1)}, f32[4,128,128]{2,1,0:T(8,128)S(1)}, u32[]{:S(2)}, u32[]{:S(2)}) collective-permute-start(f32[4,128,128]{2,1,0:T(8,128)S(1)} %collective-permute-done.6.rest_2_), channel_id=1, source_target_pairs={{0,8},{8,0},{16,24},{24,16},{1,9},{9,1},{17,25},{25,17},{2,10},{10... | collective-permute-start | bytes 786440 | tf_op jit(solution)/shard_map/ppermute | solution.py:557

commit v8 on v7

--- a/solution.py
+++ b/solution.py
@@ -45,7 +45,7 @@
 
 
 UNDER = 16
-LATE = 2
+LATE = 3
 
 
 def block_rows(lights, rows, k, nl):
@@ -532,6 +532,10 @@
     out_ref[3] = grad_albedo
 
 
+def hop_body(in_ref, out_ref):
+    out_ref[...] = in_ref[...]
+
+
 def final_body(nl, recv_ref, *rest):
     parts, (depth_ref, albedo_ref) = rest[:nl], rest[nl:]
     li, _, _, count = position()
@@ -614,8 +618,7 @@
     part2 = swap(own, 2)
     part1 = swap(own, 1)
     recv = lax.all_to_all(pay, AXES, 0, 0, tiled=True)
-    recv, part2 = lax.optimization_barrier((recv, part2))
-    part3 = swap(part2, 1)
+    part3 = swap(call(hop_body, shape(4, *field))(part2), 1)
     return tuple(
         call(functools.partial(final_body, nl), (shape(rows, cols), shape(rows, cols)))(recv, own, part1, part2, part3)
     )

time: 50 us -> 54.9 us (1.098)
  blocking collectives: 13.2 us -> 22 us
  starting transfers between devices: 12.2 us -> 9.66 us
  waiting for transfers between devices: 11.9 us -> 11.2 us
  Pallas kernels: 11.7 us -> 11.1 us
    all_to_all x1 -> x2, blocking collectives: 13.2 us -> 22 us  [program(): recv = lax.all_to_all(pay, AXES, 0, 0, tiled=True)]
    all_to_all x1 -> x0, waiting for transfers between devices: 6.89 us -> none  [program(): recv = lax.all_to_all(pay, AXES, 0, 0, tiled=True)]
    ppermute x8, waiting for transfers between devices: 3.65 us -> 9.79 us  [swap(): return lax.ppermute(x, 'light', [(i, i ^ k) for i in range(nl)])]
    all_to_all x1 -> x0, starting transfers between devices: 2.54 us -> none  [program(): recv = lax.all_to_all(pay, AXES, 0, 0, tiled=True)]
    pallas_call x1, Pallas kernels: 4.01 us -> 3.44 us  [program(): call(functools.partial(second_body, nl), (shape(4, *field), shape(nd, 1,...]
  transfers between devices with their start and end apart: 10 -> 9, of which waited for: 6 -> 5; matrix products, arithmetic and copies ran while one was open for 0% -> 0% of each run, Pallas kernels for 8% -> 7%
where the time goes in v8:
time: 54.9 us; the launch traced here: 54.7 us
  blocking collectives  22 us (40%)
  waiting for transfers between devices  11.2 us (20%)
  Pallas kernels  11.1 us (20%)
  starting transfers between devices  9.66 us (18%)
  between operations  0.76 us (1%)
    all_to_all x2, blocking collectives, program(): recv = lax.all_to_all(pay, AXES, 0, 0, tiled=True)  22 us
    ppermute x8, waiting for transfers between devices, swap(): return lax.ppermute(x, 'light', [(i, i ^ k) for i in range(nl)])  9.79 us
    ppermute x8, starting transfers between devices, swap(): return lax.ppermute(x, 'light', [(i, i ^ k) for i in range(nl)])  6.23 us
    pallas_call x1, Pallas kernels, program(): call(functools.partial(second_body, nl), (shape(4, *field), shape(nd, 1,...  3.44 us
    ppermute x1, starting transfers between devices, program(): direct = lax.ppermute(strip, AXES, pairs)  3.43 us
    pallas_call x1, Pallas kernels, program(): call(functools.partial(cut_body, nl), tuple((shape(block_rows(lights, row...  2.22 us
    pallas_call x1, Pallas kernels, program(): call(functools.partial(first_body, nl), (shape(4, *field), shape(16, rows...  1.61 us
    ppermute x1, waiting for transfers between devices, program(): direct = lax.ppermute(strip, AXES, pairs)  1.39 us
  transfers between devices with their start and end apart: 9, of which 5 were waited for; matrix products, arithmetic and copies ran while one was open for 0% of the time, Pallas kernels for 7%

profile of v8, /device:TPU:0, one launch (start us, length us, event | category | flops | bytes accessed | tf_op | source)
XLA Modules:
  0.0 54.7 jit_solution(2879025762595452352)
XLA Ops:
  0.7 2.2 %shard_map.68 = (bf16[1056,128]{1,0:T(8,128)(2,1)S(1)}, bf16[1072,128]{1,0:T(8,128)(2,1)S(1)}, bf16[1056,128]{1,0:T(8,128)(2,1)S(1)}, bf16[672,128]{1,0:T(8,128)...) custom-call(bf16[8,128,512]{2,1,0:T(8,128)(2,1)} %obs_ref.1, s32[4,8]{1,0:T(4,128)} %bitcast.1), custom_call_target="tpu_custom_call" | custom-call | tf_op jit(solution)/shard_map/pallas_call | solution.py:565
  2.9 0.6 %collective-permute-start = (bf16[1072,128]{1,0:T(8,128)(2,1)S(1)}, bf16[1072,128]{1,0:T(8,128)(2,1)S(1)}, u32[]{:S(2)}, u32[]{:S(2)}) collective-permute-start(bf16[1072,128]{1,0:T(8,128)(2,1)S(1)} %get-tuple-element.31), channel_id=1, source_target_pairs={{0,8},{8,0},{16,24},{24,16},{1,9},{9,1},{17,25},{25,17},{2,10},{10... | collective-permute-start | bytes 823304 | tf_op jit(solution)/shard_map/ppermute | solution.py:561
  3.4 2.6 %collective-permute-start.2 = (bf16[1056,128]{1,0:T(8,128)(2,1)S(1)}, bf16[1056,128]{1,0:T(8,128)(2,1)S(1)}, u32[]{:S(2)}, u32[]{:S(2)}) collective-permute-start(bf16[1056,128]{1,0:T(8,128)(2,1)S(1)} %get-tuple-element.39), channel_id=1, source_target_pairs={{0,16},{8,24},{16,0},{24,8},{1,17},{9,25},{17,1},{25,9},{2,18},{10... | collective-permute-start | bytes 811016 | tf_op jit(solution)/shard_map/ppermute | solution.py:561
  6.0 1.7 %collective-permute-start.4 = (bf16[384,128]{1,0:T(8,128)(2,1)S(1)}, bf16[384,128]{1,0:T(8,128)(2,1)S(1)}, u32[]{:S(2)}, u32[]{:S(2)}) collective-permute-start(bf16[384,128]{1,0:T(8,128)(2,1)S(1)} %get-tuple-element.43), channel_id=1, source_target_pairs={{0,24},{8,16},{16,8},{24,0},{1,25},{9,17},{17,9},{25,1},{2,26},{10... | collective-permute-start | bytes 294920 | tf_op jit(solution)/shard_map/ppermute | solution.py:561
  7.8 0.2 shard_map.69
  8.0 3.4 %collective-permute-start.1 = (f32[24,128]{1,0:T(8,128)S(1)}, f32[24,128]{1,0:T(8,128)S(1)}, u32[]{:S(2)}, u32[]{:S(2)}) collective-permute-start(f32[24,128]{1,0:T(8,128)S(1)} %get-tuple-element.35), channel_id=1, source_target_pairs={{0,1},{9,8},{16,17},{25,24},{1,2},{10,9},{17,18},{26,25},{2,3},{11... | collective-permute-start | bytes 36872 | tf_op jit(solution)/shard_map/ppermute | solution.py:589
  11.4 1.4 %collective-permute-done.1.strip_ref.direct_ref = f32[24,128]{1,0:T(8,128)S(1)} collective-permute-done((f32[24,128]{1,0:T(8,128)S(1)}, f32[24,128]{1,0:T(8,128)S(1)}, u32[]{:S(2)}, u32[]{:S(2)}) %collective-permute-start.1) | collective-permute-done | bytes 12320 | tf_op jit(solution)/shard_map/ppermute | solution.py:589
  12.8 0.5 collective-permute-start.5
  13.4 1.6 %shard_map.70 = (f32[4,128,128]{2,1,0:T(8,128)S(1)}, f32[16,128]{1,0:T(8,128)S(1)}, f32[7,128,128]{2,1,0:T(8,128)S(1)}, f32[16,5,8,128]{3,2,1,0:T(8,128)S(1)}, f32[16,128,128]{2,1,0:T(8,128)S(1)}) custom-call(f32[3,128,128]{2,1,0:T(8,128)S(1)} %get-tuple-element.33.tile_ref, f32[16,128]{1,0:T(8,128)S(1)} %get-tuple-element.34.sr_ref, ...), custom_call_target="tpu_custom_call" | custom-call | tf_op jit(solution)/shard_map/pallas_call | solution.py:596
  15.0 0.9 %shard_map.71 = (f32[7,128,128]{2,1,0:T(8,128)S(1)}, f32[8,5,8,128]{3,2,1,0:T(8,128)S(1)}, f32[8,128,128]{2,1,0:T(8,128)S(1)}) custom-call(f32[4,128,128]{2,1,0:T(8,128)S(1)} %get-tuple-element.37.ctx_ref, f32[7,128,128]{2,1,0:T(8,128)S(1)} %get-tuple-element.38.in_ref, bf16[1056,128]{1,0:T(8,128)(2,1)S(1)} %collective-permute-done.2.obs.rest_2_), custom_call_target="tpu_custom_call" | custom-call | tf_op jit(solution)/shard_map/pallas_call | solution.py:601
  15.9 0.7 %collective-permute-done.3.obs.rest_3_ = bf16[672,128]{1,0:T(8,128)(2,1)S(1)} collective-permute-done((bf16[672,128]{1,0:T(8,128)(2,1)S(1)}, bf16[672,128]{1,0:T(8,128)(2,1)S(1)}, u32[]{:S(2)}, u32[]{:S(2)}) %collective-permute-start.3) | collective-permute-done | bytes 172064 | tf_op jit(solution)/shard_map/ppermute | solution.py:561
  16.6 0.7 %shard_map.72 = (f32[7,128,128]{2,1,0:T(8,128)S(1)}, f32[8,5,8,128]{3,2,1,0:T(8,128)S(1)}, f32[5,128,128]{2,1,0:T(8,128)S(1)}) custom-call(f32[4,128,128]{2,1,0:T(8,128)S(1)} %get-tuple-element.37.ctx_ref, f32[7,128,128]{2,1,0:T(8,128)S(1)} %get-tuple-element.40.in_ref, bf16[672,128]{1,0:T(8,128)(2,1)S(1)} %collective-permute-done.3.obs.rest_3_), custom_call_target="tpu_custom_call" | custom-call | tf_op jit(solution)/shard_map/pallas_call | solution.py:602
  17.2 1.4 %collective-permute-done.4.obs.rest_4_ = bf16[384,128]{1,0:T(8,128)(2,1)S(1)} collective-permute-done((bf16[384,128]{1,0:T(8,128)(2,1)S(1)}, bf16[384,128]{1,0:T(8,128)(2,1)S(1)}, u32[]{:S(2)}, u32[]{:S(2)}) %collective-permute-start.4) | collective-permute-done | bytes 98336 | tf_op jit(solution)/shard_map/ppermute | solution.py:561
  18.6 0.4 shard_map.73
  19.0 0.1 collective-permute-done.5.relayed_ref
  19.1 0.3 shard_map.74
  19.4 0.3 shard_map.75
  19.7 13.2 %all_to_all.10.recv_ref = f32[32,4,128]{2,1,0:T(4,128)S(1)} all-to-all(f32[32,4,128]{2,1,0:T(4,128)S(1)} %get-tuple-element.48), channel_id=1, replica_groups=mesh['light'=4,'strip'=8] {'light','strip'}, dimensions={0} | all-to-all | bytes 131072 | tf_op jit(solution)/shard_map/all_to_all | solution.py:608
  32.9 3.4 %shard_map.76 = (f32[4,128,128]{2,1,0:T(8,128)S(1)}, f32[32,1,128]{2,1,0:T(1,128)S(1)}) custom-call(f32[32,4,128]{2,1,0:T(4,128)S(1)} %all_to_all.10.recv_ref, f32[2,128,128]{2,1,0:T(8,128)S(1)} %get-tuple-element.49.grad_ref, f32[8,128]{1,0:T(8,128)S(1)} %get-tuple-element.50.edge_ref, f32[3,128,128]{2,1,0:T(8,128)S(1)} %get-tuple-element.33.tile_ref, ...), custom_call_target="tpu_custom_call" | custom-call | tf_op jit(solution)/shard_map/pallas_call | solution.py:609
  36.3 0.8 %collective-permute-start.7 = (f32[4,128,128]{2,1,0:T(8,128)S(1)}, f32[4,128,128]{2,1,0:T(8,128)S(1)}, u32[]{:S(2)}, u32[]{:S(2)}) collective-permute-start(f32[4,128,128]{2,1,0:T(8,128)S(1)} %get-tuple-element.59.rest_0_), channel_id=1, source_target_pairs={{0,16},{8,24},{16,0},{24,8},{1,17},{9,25},{17,1},{25,9},{2,18},{10... | collective-permute-start | bytes 786440 | tf_op jit(solution)/shard_map/ppermute | solution.py:561
  37.1 7.6 %collective-permute-done.7.in_ref.rest_2_ = f32[4,128,128]{2,1,0:T(8,128)S(1)} collective-permute-done((f32[4,128,128]{2,1,0:T(8,128)S(1)}, f32[4,128,128]{2,1,0:T(8,128)S(1)}, u32[]{:S(2)}, u32[]{:S(2)}) %collective-permute-start.7) | collective-permute-done | bytes 262176 | tf_op jit(solution)/shard_map/ppermute | solution.py:561
  44.8 0.1 collective-permute-start.8
  44.8 8.8 %all_to_all.11.recv_ref = f32[32,1,128]{2,1,0:T(1,128)S(1)} all-to-all(f32[32,1,128]{2,1,0:T(1,128)S(1)} %get-tuple-element.58), channel_id=1, replica_groups=mesh['light'=4,'strip'=8] {'light','strip'}, dimensions={0} | all-to-all | bytes 32768 | tf_op jit(solution)/shard_map/all_to_all | solution.py:620
  53.7 1.0 %shard_map.78 = (f32[128,512]{1,0:T(8,128)}, f32[128,512]{1,0:T(8,128)}) custom-call(f32[32,1,128]{2,1,0:T(1,128)S(1)} %all_to_all.11.recv_ref, f32[4,128,128]{2,1,0:T(8,128)S(1)} %get-tuple-element.59.rest_0_, f32[4,128,128]{2,1,0:T(8,128)S(1)} %collective-permute-done.6.rest_1_, f32[4,128,128]{2,1,0:T(8,128)S(1)} %collective-permute-done.7.in_ref.rest_2_, ...), custom_call_target="tpu_custom_call" | custom-call | tf_op jit(solution)/shard_map/pallas_call | solution.py:623
  (13 shorter events, 0.1 us)
Async XLA Ops:
  0.6 7.1 %copy-start = (f32[128,512]{1,0:T(8,128)S(1)}, f32[128,512]{1,0:T(8,128)}, u32[]{:S(2)}) copy-start(f32[128,512]{1,0:T(8,128)} %depth_ref.1) | copy-start | bytes 786436
  0.6 7.1 %copy-start.1 = (f32[128,512]{1,0:T(8,128)S(1)}, f32[128,512]{1,0:T(8,128)}, u32[]{:S(2)}) copy-start(f32[128,512]{1,0:T(8,128)} %albedo_ref.1) | copy-start | bytes 786436
  0.7 7.1 %copy-start.2 = (s32[128,512]{1,0:T(8,128)S(1)}, s32[128,512]{1,0:T(8,128)}, u32[]{:S(2)}) copy-start(s32[128,512]{1,0:T(8,128)} %valid_ref.1) | copy-start | bytes 786436
  2.9 4.9 %collective-permute-start = (bf16[1072,128]{1,0:T(8,128)(2,1)S(1)}, bf16[1072,128]{1,0:T(8,128)(2,1)S(1)}, u32[]{:S(2)}, u32[]{:S(2)}) collective-permute-start(bf16[1072,128]{1,0:T(8,128)(2,1)S(1)} %get-tuple-element.31), channel_id=1, source_target_pairs={{0,8},{8,0},{16,24},{24,16},{1,9},{9,1},{17,25},{25,17},{2,10},{10... | collective-permute-start | bytes 823304 | tf_op jit(solution)/shard_map/ppermute | solution.py:561
  3.4 11.5 %collective-permute-start.2 = (bf16[1056,128]{1,0:T(8,128)(2,1)S(1)}, bf16[1056,128]{1,0:T(8,128)(2,1)S(1)}, u32[]{:S(2)}, u32[]{:S(2)}) collective-permute-start(bf16[1056,128]{1,0:T(8,128)(2,1)S(1)} %get-tuple-element.39), channel_id=1, source_target_pairs={{0,16},{8,24},{16,0},{24,8},{1,17},{9,25},{17,1},{25,9},{2,18},{10... | collective-permute-start | bytes 811016 | tf_op jit(solution)/shard_map/ppermute | solution.py:561
  6.0 10.6 %collective-permute-start.3 = (bf16[672,128]{1,0:T(8,128)(2,1)S(1)}, bf16[672,128]{1,0:T(8,128)(2,1)S(1)}, u32[]{:S(2)}, u32[]{:S(2)}) collective-permute-start(bf16[672,128]{1,0:T(8,128)(2,1)S(1)} %get-tuple-element.41), channel_id=1, source_target_pairs={{0,24},{8,16},{16,8},{24,0},{1,25},{9,17},{17,9},{25,1},{2,26},{10... | collective-permute-start | bytes 516104 | tf_op jit(solution)/shard_map/ppermute | solution.py:561
  6.0 12.6 %collective-permute-start.4 = (bf16[384,128]{1,0:T(8,128)(2,1)S(1)}, bf16[384,128]{1,0:T(8,128)(2,1)S(1)}, u32[]{:S(2)}, u32[]{:S(2)}) collective-permute-start(bf16[384,128]{1,0:T(8,128)(2,1)S(1)} %get-tuple-element.43), channel_id=1, source_target_pairs={{0,24},{8,16},{16,8},{24,0},{1,25},{9,17},{17,9},{25,1},{2,26},{10... | collective-permute-start | bytes 294920 | tf_op jit(solution)/shard_map/ppermute | solution.py:561
  8.0 4.8 %collective-permute-start.1 = (f32[24,128]{1,0:T(8,128)S(1)}, f32[24,128]{1,0:T(8,128)S(1)}, u32[]{:S(2)}, u32[]{:S(2)}) collective-permute-start(f32[24,128]{1,0:T(8,128)S(1)} %get-tuple-element.35), channel_id=1, source_target_pairs={{0,1},{9,8},{16,17},{25,24},{1,2},{10,9},{17,18},{26,25},{2,3},{11... | collective-permute-start | bytes 36872 | tf_op jit(solution)/shard_map/ppermute | solution.py:589
  12.8 6.3 %collective-permute-start.5 = (f32[24,128]{1,0:T(8,128)S(1)}, f32[24,128]{1,0:T(8,128)S(1)}, u32[]{:S(2)}, u32[]{:S(2)}) collective-permute-start(f32[24,128]{1,0:T(8,128)S(1)} %collective-permute-done.1.strip_ref.direct_ref), channel_id=1, source_target_pairs={{0,16},{8,24},{16,0},{24,8},{1,17},{9,25},{17,1},{25,9},{2,18},{10... | collective-permute-start | bytes 36872 | tf_op jit(solution)/shard_map/ppermute | solution.py:561
  36.3 8.4 %collective-permute-start.7 = (f32[4,128,128]{2,1,0:T(8,128)S(1)}, f32[4,128,128]{2,1,0:T(8,128)S(1)}, u32[]{:S(2)}, u32[]{:S(2)}) collective-permute-start(f32[4,128,128]{2,1,0:T(8,128)S(1)} %get-tuple-element.59.rest_0_), channel_id=1, source_target_pairs={{0,16},{8,24},{16,0},{24,8},{1,17},{9,25},{17,1},{25,9},{2,18},{10... | collective-permute-start | bytes 786440 | tf_op jit(solution)/shard_map/ppermute | solution.py:561
  37.1 16.6 %collective-permute-start.6 = (f32[4,128,128]{2,1,0:T(8,128)S(1)}, f32[4,128,128]{2,1,0:T(8,128)S(1)}, u32[]{:S(2)}, u32[]{:S(2)}) collective-permute-start(f32[4,128,128]{2,1,0:T(8,128)S(1)} %get-tuple-element.59.rest_0_), channel_id=1, source_target_pairs={{0,8},{8,0},{16,24},{24,16},{1,9},{9,1},{17,25},{25,17},{2,10},{10... | collective-permute-start | bytes 786440 | tf_op jit(solution)/shard_map/ppermute | solution.py:561
  44.8 8.9 %collective-permute-start.8 = (f32[4,128,128]{2,1,0:T(8,128)S(1)}, f32[4,128,128]{2,1,0:T(8,128)S(1)}, u32[]{:S(2)}, u32[]{:S(2)}) collective-permute-start(f32[4,128,128]{2,1,0:T(8,128)S(1)} %shard_map.77), channel_id=1, source_target_pairs={{0,8},{8,0},{16,24},{24,16},{1,9},{9,1},{17,25},{25,17},{2,10},{10... | collective-permute-start | bytes 786440 | tf_op jit(solution)/shard_map/ppermute | solution.py:561

commit v9 on v8

--- a/solution.py
+++ b/solution.py
@@ -60,22 +60,23 @@
     li = lax.axis_index("light")
     here = [lights_of(block, rows) for block in blocks]
 
-    def slot(k, l):
-        if l < here[k]:
-            return blocks[k].at[pl.ds(l * rows, rows)]
-        return late_ref.at[pl.ds((l - here[k]) * rows, rows)]
-
     copies = []
     for k in (2, 3, 1, 0):
-        for l in range(lights):
-            at = pl.ds(pl.multiple_of((li ^ k) * w, w), w)
-            copies.append(pltpu.make_async_copy(obs_ref.at[l, :, at], slot(k, l), sems.at[k * lights + l]))
+        at = pl.ds(pl.multiple_of((li ^ k) * w, w), w)
+        groups = [(0, here[k], blocks[k])]
+        if here[k] < lights:
+            groups.append((here[k], lights - here[k], late_ref))
+        for start, size, ref in groups:
+            target = ref.at[pl.ds(0, size * rows)].reshape(size, rows, w)
+            copies.append(
+                pltpu.make_async_copy(obs_ref.at[pl.ds(start, size), :, at], target, sems.at[len(copies)])
+            )
             copies[-1].start()
     fetch = pltpu.make_async_copy(table_ref, table, extra.at[0])
     fetch.start()
     eh_ref[...] = jnp.zeros_like(eh_ref)
-    at, col = iota((8, w), 0), iota((8, w), 1)
-    pick = (((at == 0) & (col == 0)) | ((at == 1) & (col == w - 1))).astype(jnp.bfloat16)
+    at, col = iota((2 * lights, lights * w), 0), iota((2 * lights, lights * w), 1)
+    pick = (col == jnp.where(at < lights, at * w + w - 1, (at - lights) * w)).astype(jnp.bfloat16)
     fetch.wait()
     entries = table[...]
     high = lax.shift_right_logical(entries, 5)
@@ -88,15 +89,16 @@
         copy.wait()
     for k in range(nl):
         q = li ^ k
-        for l in range(lights):
-            e = lax.dot_general(
-                pick,
-                slot(k, l)[...],
-                (((1,), (1,)), ((), ())),
-                preferred_element_type=F32,
-            )
-            eh_ref[q, lights + l : lights + l + 1, :] = e[0:1]
-            eh_ref[q + 2, l : l + 1, :] = e[1:2]
+        side_by_side = [blocks[k][pl.ds(l * rows, rows), :] for l in range(here[k])]
+        side_by_side += [late_ref[pl.ds(l * rows, rows), :] for l in range(lights - here[k])]
+        e = lax.dot_general(
+            pick,
+            jnp.concatenate(side_by_side, axis=1),
+            (((1,), (1,)), ((), ())),
+            preferred_element_type=F32,
+        )
+        eh_ref[q, lights:, :] = e[lights:]
+        eh_ref[q + 2, 0:lights, :] = e[0:lights]
     ends = jnp.concatenate([eh_ref[nl + 1, 0:lights, :], eh_ref[0, lights:, :]], axis=0)
     end_ref[...] = ends
     for k in range(nl):
@@ -569,7 +571,7 @@
         [
             pltpu.VMEM((4, lights), jnp.int32),
             pltpu.VMEM((nl + 2, 2 * lights, rows), F32),
-            pltpu.SemaphoreType.DMA((nl * lights,)),
+            pltpu.SemaphoreType.DMA((nl + 1,)),
             pltpu.SemaphoreType.DMA((1,)),
         ],
         in_specs=[hbm] * 2,

time: 54.9 us -> 54.5 us (level)
  no operation moved by 1% of the time
where the time goes in v9:
time: 54.5 us; the launch traced here: 54.3 us
  blocking collectives  22 us (40%)
  waiting for transfers between devices  11.2 us (21%)
  Pallas kernels  10.6 us (19%)
  starting transfers between devices  9.66 us (18%)
  between operations  0.76 us (1%)
    all_to_all x2, blocking collectives, program(): recv = lax.all_to_all(pay, AXES, 0, 0, tiled=True)  22 us
    ppermute x8, waiting for transfers between devices, swap(): return lax.ppermute(x, 'light', [(i, i ^ k) for i in range(nl)])  9.79 us
    ppermute x8, starting transfers between devices, swap(): return lax.ppermute(x, 'light', [(i, i ^ k) for i in range(nl)])  6.23 us
    pallas_call x1, Pallas kernels, program(): call(functools.partial(second_body, nl), (shape(4, *field), shape(nd, 1,...  3.44 us
    ppermute x1, starting transfers between devices, program(): direct = lax.ppermute(strip, AXES, pairs)  3.43 us
    pallas_call x1, Pallas kernels, program(): call(functools.partial(cut_body, nl), tuple((shape(block_rows(lights, row...  1.8 us
    pallas_call x1, Pallas kernels, program(): call(functools.partial(first_body, nl), (shape(4, *field), shape(16, rows...  1.61 us
    ppermute x1, waiting for transfers between devices, program(): direct = lax.ppermute(strip, AXES, pairs)  1.39 us
  transfers between devices with their start and end apart: 9, of which 5 were waited for; matrix products, arithmetic and copies ran while one was open for 0% of the time, Pallas kernels for 7%

profile of v9, /device:TPU:0, one launch (start us, length us, event | category | flops | bytes accessed | tf_op | source)
XLA Modules:
  0.0 54.3 jit_solution(1269481519969383238)
XLA Ops:
  0.7 1.8 %shard_map.68 = (bf16[1056,128]{1,0:T(8,128)(2,1)S(1)}, bf16[1072,128]{1,0:T(8,128)(2,1)S(1)}, bf16[1056,128]{1,0:T(8,128)(2,1)S(1)}, bf16[672,128]{1,0:T(8,128)...) custom-call(bf16[8,128,512]{2,1,0:T(8,128)(2,1)} %obs_ref.1, s32[4,8]{1,0:T(4,128)} %bitcast.1), custom_call_target="tpu_custom_call" | custom-call | tf_op jit(solution)/shard_map/pallas_call | solution.py:567
  2.5 0.6 %collective-permute-start = (bf16[1072,128]{1,0:T(8,128)(2,1)S(1)}, bf16[1072,128]{1,0:T(8,128)(2,1)S(1)}, u32[]{:S(2)}, u32[]{:S(2)}) collective-permute-start(bf16[1072,128]{1,0:T(8,128)(2,1)S(1)} %get-tuple-element.31), channel_id=1, source_target_pairs={{0,8},{8,0},{16,24},{24,16},{1,9},{9,1},{17,25},{25,17},{2,10},{10... | collective-permute-start | bytes 823304 | tf_op jit(solution)/shard_map/ppermute | solution.py:563
  3.0 2.6 %collective-permute-start.2 = (bf16[1056,128]{1,0:T(8,128)(2,1)S(1)}, bf16[1056,128]{1,0:T(8,128)(2,1)S(1)}, u32[]{:S(2)}, u32[]{:S(2)}) collective-permute-start(bf16[1056,128]{1,0:T(8,128)(2,1)S(1)} %get-tuple-element.39), channel_id=1, source_target_pairs={{0,16},{8,24},{16,0},{24,8},{1,17},{9,25},{17,1},{25,9},{2,18},{10... | collective-permute-start | bytes 811016 | tf_op jit(solution)/shard_map/ppermute | solution.py:563
  5.6 1.7 %collective-permute-start.4 = (bf16[384,128]{1,0:T(8,128)(2,1)S(1)}, bf16[384,128]{1,0:T(8,128)(2,1)S(1)}, u32[]{:S(2)}, u32[]{:S(2)}) collective-permute-start(bf16[384,128]{1,0:T(8,128)(2,1)S(1)} %get-tuple-element.43), channel_id=1, source_target_pairs={{0,24},{8,16},{16,8},{24,0},{1,25},{9,17},{17,9},{25,1},{2,26},{10... | collective-permute-start | bytes 294920 | tf_op jit(solution)/shard_map/ppermute | solution.py:563
  7.3 0.2 shard_map.69
  7.6 3.4 %collective-permute-start.1 = (f32[24,128]{1,0:T(8,128)S(1)}, f32[24,128]{1,0:T(8,128)S(1)}, u32[]{:S(2)}, u32[]{:S(2)}) collective-permute-start(f32[24,128]{1,0:T(8,128)S(1)} %get-tuple-element.35), channel_id=1, source_target_pairs={{0,1},{9,8},{16,17},{25,24},{1,2},{10,9},{17,18},{26,25},{2,3},{11... | collective-permute-start | bytes 36872 | tf_op jit(solution)/shard_map/ppermute | solution.py:591
  11.0 1.4 %collective-permute-done.1.strip_ref.direct_ref = f32[24,128]{1,0:T(8,128)S(1)} collective-permute-done((f32[24,128]{1,0:T(8,128)S(1)}, f32[24,128]{1,0:T(8,128)S(1)}, u32[]{:S(2)}, u32[]{:S(2)}) %collective-permute-start.1) | collective-permute-done | bytes 12320 | tf_op jit(solution)/shard_map/ppermute | solution.py:591
  12.4 0.5 collective-permute-start.5
  12.9 1.6 %shard_map.70 = (f32[4,128,128]{2,1,0:T(8,128)S(1)}, f32[16,128]{1,0:T(8,128)S(1)}, f32[7,128,128]{2,1,0:T(8,128)S(1)}, f32[16,5,8,128]{3,2,1,0:T(8,128)S(1)}, f32[16,128,128]{2,1,0:T(8,128)S(1)}) custom-call(f32[3,128,128]{2,1,0:T(8,128)S(1)} %get-tuple-element.33.tile_ref, f32[16,128]{1,0:T(8,128)S(1)} %get-tuple-element.34.sr_ref, ...), custom_call_target="tpu_custom_call" | custom-call | tf_op jit(solution)/shard_map/pallas_call | solution.py:598
  14.6 0.9 %shard_map.71 = (f32[7,128,128]{2,1,0:T(8,128)S(1)}, f32[8,5,8,128]{3,2,1,0:T(8,128)S(1)}, f32[8,128,128]{2,1,0:T(8,128)S(1)}) custom-call(f32[4,128,128]{2,1,0:T(8,128)S(1)} %get-tuple-element.37.ctx_ref, f32[7,128,128]{2,1,0:T(8,128)S(1)} %get-tuple-element.38.in_ref, bf16[1056,128]{1,0:T(8,128)(2,1)S(1)} %collective-permute-done.2.obs.rest_2_), custom_call_target="tpu_custom_call" | custom-call | tf_op jit(solution)/shard_map/pallas_call | solution.py:603
  15.5 0.7 %collective-permute-done.3.obs.rest_3_ = bf16[672,128]{1,0:T(8,128)(2,1)S(1)} collective-permute-done((bf16[672,128]{1,0:T(8,128)(2,1)S(1)}, bf16[672,128]{1,0:T(8,128)(2,1)S(1)}, u32[]{:S(2)}, u32[]{:S(2)}) %collective-permute-start.3) | collective-permute-done | bytes 172064 | tf_op jit(solution)/shard_map/ppermute | solution.py:563
  16.1 0.7 %shard_map.72 = (f32[7,128,128]{2,1,0:T(8,128)S(1)}, f32[8,5,8,128]{3,2,1,0:T(8,128)S(1)}, f32[5,128,128]{2,1,0:T(8,128)S(1)}) custom-call(f32[4,128,128]{2,1,0:T(8,128)S(1)} %get-tuple-element.37.ctx_ref, f32[7,128,128]{2,1,0:T(8,128)S(1)} %get-tuple-element.40.in_ref, bf16[672,128]{1,0:T(8,128)(2,1)S(1)} %collective-permute-done.3.obs.rest_3_), custom_call_target="tpu_custom_call" | custom-call | tf_op jit(solution)/shard_map/pallas_call | solution.py:604
  16.8 1.4 %collective-permute-done.4.obs.rest_4_ = bf16[384,128]{1,0:T(8,128)(2,1)S(1)} collective-permute-done((bf16[384,128]{1,0:T(8,128)(2,1)S(1)}, bf16[384,128]{1,0:T(8,128)(2,1)S(1)}, u32[]{:S(2)}, u32[]{:S(2)}) %collective-permute-start.4) | collective-permute-done | bytes 98336 | tf_op jit(solution)/shard_map/ppermute | solution.py:563
  18.2 0.4 shard_map.73
  18.6 0.1 collective-permute-done.5.relayed_ref
  18.7 0.3 shard_map.74
  19.0 0.3 shard_map.75
  19.3 13.2 %all_to_all.10.recv_ref = f32[32,4,128]{2,1,0:T(4,128)S(1)} all-to-all(f32[32,4,128]{2,1,0:T(4,128)S(1)} %get-tuple-element.48), channel_id=1, replica_groups=mesh['light'=4,'strip'=8] {'light','strip'}, dimensions={0} | all-to-all | bytes 131072 | tf_op jit(solution)/shard_map/all_to_all | solution.py:610
  32.5 3.4 %shard_map.76 = (f32[4,128,128]{2,1,0:T(8,128)S(1)}, f32[32,1,128]{2,1,0:T(1,128)S(1)}) custom-call(f32[32,4,128]{2,1,0:T(4,128)S(1)} %all_to_all.10.recv_ref, f32[2,128,128]{2,1,0:T(8,128)S(1)} %get-tuple-element.49.grad_ref, f32[8,128]{1,0:T(8,128)S(1)} %get-tuple-element.50.edge_ref, f32[3,128,128]{2,1,0:T(8,128)S(1)} %get-tuple-element.33.tile_ref, ...), custom_call_target="tpu_custom_call" | custom-call | tf_op jit(solution)/shard_map/pallas_call | solution.py:611
  35.9 0.8 %collective-permute-start.7 = (f32[4,128,128]{2,1,0:T(8,128)S(1)}, f32[4,128,128]{2,1,0:T(8,128)S(1)}, u32[]{:S(2)}, u32[]{:S(2)}) collective-permute-start(f32[4,128,128]{2,1,0:T(8,128)S(1)} %get-tuple-element.59.rest_0_), channel_id=1, source_target_pairs={{0,16},{8,24},{16,0},{24,8},{1,17},{9,25},{17,1},{25,9},{2,18},{10... | collective-permute-start | bytes 786440 | tf_op jit(solution)/shard_map/ppermute | solution.py:563
  36.7 7.6 %collective-permute-done.7.in_ref.rest_2_ = f32[4,128,128]{2,1,0:T(8,128)S(1)} collective-permute-done((f32[4,128,128]{2,1,0:T(8,128)S(1)}, f32[4,128,128]{2,1,0:T(8,128)S(1)}, u32[]{:S(2)}, u32[]{:S(2)}) %collective-permute-start.7) | collective-permute-done | bytes 262176 | tf_op jit(solution)/shard_map/ppermute | solution.py:563
  44.3 0.1 collective-permute-start.8
  44.4 8.8 %all_to_all.11.recv_ref = f32[32,1,128]{2,1,0:T(1,128)S(1)} all-to-all(f32[32,1,128]{2,1,0:T(1,128)S(1)} %get-tuple-element.58), channel_id=1, replica_groups=mesh['light'=4,'strip'=8] {'light','strip'}, dimensions={0} | all-to-all | bytes 32768 | tf_op jit(solution)/shard_map/all_to_all | solution.py:622
  53.3 1.0 %shard_map.78 = (f32[128,512]{1,0:T(8,128)}, f32[128,512]{1,0:T(8,128)}) custom-call(f32[32,1,128]{2,1,0:T(1,128)S(1)} %all_to_all.11.recv_ref, f32[4,128,128]{2,1,0:T(8,128)S(1)} %get-tuple-element.59.rest_0_, f32[4,128,128]{2,1,0:T(8,128)S(1)} %collective-permute-done.6.rest_1_, f32[4,128,128]{2,1,0:T(8,128)S(1)} %collective-permute-done.7.in_ref.rest_2_, ...), custom_call_target="tpu_custom_call" | custom-call | tf_op jit(solution)/shard_map/pallas_call | solution.py:625
  (13 shorter events, 0.1 us)
Async XLA Ops:
  0.6 6.7 %copy-start = (f32[128,512]{1,0:T(8,128)S(1)}, f32[128,512]{1,0:T(8,128)}, u32[]{:S(2)}) copy-start(f32[128,512]{1,0:T(8,128)} %depth_ref.1) | copy-start | bytes 786436
  0.6 6.7 %copy-start.1 = (f32[128,512]{1,0:T(8,128)S(1)}, f32[128,512]{1,0:T(8,128)}, u32[]{:S(2)}) copy-start(f32[128,512]{1,0:T(8,128)} %albedo_ref.1) | copy-start | bytes 786436
  0.7 6.7 %copy-start.2 = (s32[128,512]{1,0:T(8,128)S(1)}, s32[128,512]{1,0:T(8,128)}, u32[]{:S(2)}) copy-start(s32[128,512]{1,0:T(8,128)} %valid_ref.1) | copy-start | bytes 786436
  2.5 4.9 %collective-permute-start = (bf16[1072,128]{1,0:T(8,128)(2,1)S(1)}, bf16[1072,128]{1,0:T(8,128)(2,1)S(1)}, u32[]{:S(2)}, u32[]{:S(2)}) collective-permute-start(bf16[1072,128]{1,0:T(8,128)(2,1)S(1)} %get-tuple-element.31), channel_id=1, source_target_pairs={{0,8},{8,0},{16,24},{24,16},{1,9},{9,1},{17,25},{25,17},{2,10},{10... | collective-permute-start | bytes 823304 | tf_op jit(solution)/shard_map/ppermute | solution.py:563
  3.0 11.5 %collective-permute-start.2 = (bf16[1056,128]{1,0:T(8,128)(2,1)S(1)}, bf16[1056,128]{1,0:T(8,128)(2,1)S(1)}, u32[]{:S(2)}, u32[]{:S(2)}) collective-permute-start(bf16[1056,128]{1,0:T(8,128)(2,1)S(1)} %get-tuple-element.39), channel_id=1, source_target_pairs={{0,16},{8,24},{16,0},{24,8},{1,17},{9,25},{17,1},{25,9},{2,18},{10... | collective-permute-start | bytes 811016 | tf_op jit(solution)/shard_map/ppermute | solution.py:563
  5.6 10.6 %collective-permute-start.3 = (bf16[672,128]{1,0:T(8,128)(2,1)S(1)}, bf16[672,128]{1,0:T(8,128)(2,1)S(1)}, u32[]{:S(2)}, u32[]{:S(2)}) collective-permute-start(bf16[672,128]{1,0:T(8,128)(2,1)S(1)} %get-tuple-element.41), channel_id=1, source_target_pairs={{0,24},{8,16},{16,8},{24,0},{1,25},{9,17},{17,9},{25,1},{2,26},{10... | collective-permute-start | bytes 516104 | tf_op jit(solution)/shard_map/ppermute | solution.py:563
  5.6 12.6 %collective-permute-start.4 = (bf16[384,128]{1,0:T(8,128)(2,1)S(1)}, bf16[384,128]{1,0:T(8,128)(2,1)S(1)}, u32[]{:S(2)}, u32[]{:S(2)}) collective-permute-start(bf16[384,128]{1,0:T(8,128)(2,1)S(1)} %get-tuple-element.43), channel_id=1, source_target_pairs={{0,24},{8,16},{16,8},{24,0},{1,25},{9,17},{17,9},{25,1},{2,26},{10... | collective-permute-start | bytes 294920 | tf_op jit(solution)/shard_map/ppermute | solution.py:563
  7.6 4.8 %collective-permute-start.1 = (f32[24,128]{1,0:T(8,128)S(1)}, f32[24,128]{1,0:T(8,128)S(1)}, u32[]{:S(2)}, u32[]{:S(2)}) collective-permute-start(f32[24,128]{1,0:T(8,128)S(1)} %get-tuple-element.35), channel_id=1, source_target_pairs={{0,1},{9,8},{16,17},{25,24},{1,2},{10,9},{17,18},{26,25},{2,3},{11... | collective-permute-start | bytes 36872 | tf_op jit(solution)/shard_map/ppermute | solution.py:591
  12.4 6.3 %collective-permute-start.5 = (f32[24,128]{1,0:T(8,128)S(1)}, f32[24,128]{1,0:T(8,128)S(1)}, u32[]{:S(2)}, u32[]{:S(2)}) collective-permute-start(f32[24,128]{1,0:T(8,128)S(1)} %collective-permute-done.1.strip_ref.direct_ref), channel_id=1, source_target_pairs={{0,16},{8,24},{16,0},{24,8},{1,17},{9,25},{17,1},{25,9},{2,18},{10... | collective-permute-start | bytes 36872 | tf_op jit(solution)/shard_map/ppermute | solution.py:563
  35.9 8.4 %collective-permute-start.7 = (f32[4,128,128]{2,1,0:T(8,128)S(1)}, f32[4,128,128]{2,1,0:T(8,128)S(1)}, u32[]{:S(2)}, u32[]{:S(2)}) collective-permute-start(f32[4,128,128]{2,1,0:T(8,128)S(1)} %get-tuple-element.59.rest_0_), channel_id=1, source_target_pairs={{0,16},{8,24},{16,0},{24,8},{1,17},{9,25},{17,1},{25,9},{2,18},{10... | collective-permute-start | bytes 786440 | tf_op jit(solution)/shard_map/ppermute | solution.py:563
  36.7 16.6 %collective-permute-start.6 = (f32[4,128,128]{2,1,0:T(8,128)S(1)}, f32[4,128,128]{2,1,0:T(8,128)S(1)}, u32[]{:S(2)}, u32[]{:S(2)}) collective-permute-start(f32[4,128,128]{2,1,0:T(8,128)S(1)} %get-tuple-element.59.rest_0_), channel_id=1, source_target_pairs={{0,8},{8,0},{16,24},{24,16},{1,9},{9,1},{17,25},{25,17},{2,10},{10... | collective-permute-start | bytes 786440 | tf_op jit(solution)/shard_map/ppermute | solution.py:563
  44.3 8.9 %collective-permute-start.8 = (f32[4,128,128]{2,1,0:T(8,128)S(1)}, f32[4,128,128]{2,1,0:T(8,128)S(1)}, u32[]{:S(2)}, u32[]{:S(2)}) collective-permute-start(f32[4,128,128]{2,1,0:T(8,128)S(1)} %shard_map.77), channel_id=1, source_target_pairs={{0,8},{8,0},{16,24},{24,16},{1,9},{9,1},{17,25},{25,17},{2,10},{10... | collective-permute-start | bytes 786440 | tf_op jit(solution)/shard_map/ppermute | solution.py:563

commit v10 on v9

--- a/solution.py
+++ b/solution.py
@@ -341,7 +341,7 @@
     return -(valid * albedo * rn / total_w) * (px_sum + (sx * rn * rn) * pf_sum)
 
 
-def gradients(state_ref, ctx_ref, albedo, valid, slope_low, slope_high):
+def gradients(state_ref, ctx_ref, albedo, valid, ends):
     sx, sy = ctx_ref[1], ctx_ref[2]
     rn = lax.rsqrt(1.0 + sx * sx + sy * sy)
     inverse = valid * rn / state_ref[1]
@@ -352,7 +352,7 @@
     direct = factor * (3.0 * state_ref[6] - state_ref[2])
     grad_x = -factor * (state_ref[3] + sx * rn2pf)
     grad_y = -factor * (state_ref[4] + sy * rn2pf)
-    before, after = shifts_cols(grad_x, columns_from(slope_low, slope_high, grad_x.shape))
+    before, after = shifts_cols(grad_x, ends)
     above, below = shifts_rows(grad_y)
     return direct + 0.5 * (before - after) + 0.5 * (above - below), grad_albedo
 
@@ -413,26 +413,18 @@
     sweep(ctx_ref, chunks, total, state_load(in_ref, w), state_store(state_ref, w), False)
 
 
-def late_body(ctx_ref, in_ref, obs, pb_ref, state_ref, flat_ref):
-    _, _, _, count = position()
-    rows, w = ctx_ref.shape[1:]
-    n = lights_of(obs, rows)
-    chunks = [chunk_of(obs, pb_ref, flat_ref, n, pb_ref.shape[0] - n)]
-    sweep(ctx_ref, chunks, w * count, state_load(in_ref, w), state_store(state_ref, w), False)
-
-
 def halo_slopes(pack_ref, srow_ref, rows, w):
     _, _, place, count = position()
     total = w * count
     low = halo_slope(place * w - 1, 0, pack_ref, srow_ref, rows, total)
     high = halo_slope(place * w + w, 1, pack_ref, srow_ref, rows, total)
-    return low, high
-
-
-def finish(state_ref, ctx_ref, albedo, valid, low, high, grad_ref, edge_ref, pay_ref):
+    return columns_from(low, high, (rows, w))
+
+
+def finish(state_ref, ctx_ref, albedo, valid, ends, grad_ref, edge_ref, pay_ref):
     _, _, place, count = position()
     rows, w = ctx_ref.shape[1:]
-    depth, grad_albedo = gradients(state_ref, ctx_ref, albedo, valid, low, high)
+    depth, grad_albedo = gradients(state_ref, ctx_ref, albedo, valid, ends)
     sums = partial_sums(depth, grad_albedo)
     if edge_ref is None:
         pay_ref[...] = jnp.broadcast_to(sums[None], pay_ref.shape)
@@ -457,7 +449,7 @@
 
 
 def sides_body(nl, srow_ref, direct_ref, relayed_ref, *rest):
-    block_refs, (pack_ref, slope_ref) = rest[:nl], rest[nl:]
+    block_refs, (pack_ref, ends_ref) = rest[:nl], rest[nl:]
     li = lax.axis_index("light")
     w = block_refs[0].shape[1]
     rows = srow_ref.shape[1]
@@ -472,19 +464,22 @@
         table = table + (pltpu.roll(entries, k * n, 1) if k else entries)[0:4]
     tall = jnp.concatenate([table, jnp.zeros((w - 4, w), F32)], axis=0)
     pack_ref[2] = jnp.transpose(tall)[0 : nl * n]
-    slope_ref[0:1, :], slope_ref[1:2, :] = halo_slopes(pack_ref, srow_ref, rows, w)
-
-
-def last_body(ctx_ref, tile_ref, state_ref, slope_ref, grad_ref, edge_ref, pay_ref):
+    ends_ref[...] = halo_slopes(pack_ref, srow_ref, rows, w)
+
+
+def last_body(ctx_ref, in_ref, obs, pb_ref, tile_ref, ends_ref, grad_ref, edge_ref, pay_ref, flat_ref, state_ref):
+    _, _, _, count = position()
+    rows, w = ctx_ref.shape[1:]
+    n = lights_of(obs, rows)
     edge_ref[...] = jnp.zeros_like(edge_ref)
-    finish(
-        state_ref, ctx_ref, tile_ref[1], tile_ref[2], slope_ref[0:1, :], slope_ref[1:2, :], grad_ref, edge_ref, pay_ref
-    )
+    chunks = [chunk_of(obs, pb_ref, flat_ref, n, pb_ref.shape[0] - n)]
+    sweep(ctx_ref, chunks, w * count, state_load(in_ref, w), state_store(state_ref, w), False)
+    finish(state_ref, ctx_ref, tile_ref[1], tile_ref[2], ends_ref[...], grad_ref, edge_ref, pay_ref)
 
 
 def second_body(nl, recv_ref, grad_ref, edge_ref, tile_ref, srow0_ref, pack_ref, *rest):
     obs_refs, pb_refs, flat_refs = rest[: nl + 1], rest[nl + 1 : 2 * nl], rest[2 * nl : 3 * nl]
-    out_ref, pay_ref, ctx_ref, state_ref, srow_ref = rest[3 * nl :]
+    out_ref, pay_ref, ctx_ref, state_ref, srow_ref, ends_ref = rest[3 * nl :]
     _, _, place, count = position()
     rows, w = ctx_ref.shape[1:]
     total = w * count
@@ -527,9 +522,11 @@
         chunk_of(obs_refs[nl - 1], pb_refs[-1], flat_refs[-2], n - late)
         + chunk_of(obs_refs[nl], pb_refs[-1], flat_refs[-1], late, n - late)
     )
+    ends_ref[...] = halo_slopes(pack_ref, srow_ref, rows, w)
     sweep(ctx_ref, chunks, total, lambda at: None, state_store(state_ref, w), True)
-    low, high = halo_slopes(pack_ref, srow_ref, rows, w)
-    depth, grad_albedo = finish(state_ref, ctx_ref, albedo, tile_ref[2], low, high, None, None, pay_ref)
+    depth, grad_albedo = finish(
+        state_ref, ctx_ref, out_ref[1], tile_ref[2], ends_ref[...], None, None, pay_ref
+    )
     out_ref[2] = depth
     out_ref[3] = grad_albedo
 
@@ -602,11 +599,14 @@
     early = lights - LATE
     state, pb2, flat2 = call(more_body, (shape(7, *field), tiles(lights), shape(lights, *field)))(ctx, state, obs2)
     state, pb3, flat3 = call(more_body, (shape(7, *field), tiles(lights), shape(early, *field)))(ctx, state, obs3)
-    pack, slope = call(
-        functools.partial(sides_body, nl), (shape(3, nl * lights, rows), shape(8, rows))
+    pack, ends = call(
+        functools.partial(sides_body, nl), (shape(3, nl * lights, rows), shape(*field))
     )(srow, direct, relayed, obs0, obs1, obs2, obs3)
-    state, flat4 = call(late_body, (shape(7, *field), shape(LATE, *field)))(ctx, state, late, pb3)
-    grad, edge, pay = call(last_body, (shape(2, *field), shape(8, rows), shape(nd, 4, rows)))(ctx, tile, state, slope)
+    grad, edge, pay, flat4 = call(
+        last_body,
+        (shape(2, *field), shape(8, rows), shape(nd, 4, rows), shape(LATE, *field)),
+        [pltpu.VMEM((7, *field), F32)],
+    )(ctx, state, late, pb3, tile, ends)
     recv = lax.all_to_all(pay, AXES, 0, 0, tiled=True)
     own, pay = call(
         functools.partial(second_body, nl),
@@ -615,6 +615,7 @@
             pltpu.VMEM((4, *field), F32),
             pltpu.VMEM((7, *field), F32),
             pltpu.VMEM((16, rows), F32),
+            pltpu.VMEM(field, F32),
         ],
     )(recv, grad, edge, tile, srow, pack, obs0, obs1, obs2, obs3, late, pb0, pb2, pb3, flat0, flat2, flat3, flat4)
     part2 = swap(own, 2)

time: 54.5 us -> 54.9 us (level)
  transfers between devices with their start and end apart: 9 -> 9, of which waited for: 5 -> 4; matrix products, arithmetic and copies ran while one was open for 0% -> 0% of each run, Pallas kernels for 7% -> 7%
where the time goes in v10:
time: 54.9 us; the launch traced here: 54.7 us
  blocking collectives  22 us (40%)
  waiting for transfers between devices  11.6 us (21%)
  Pallas kernels  10.7 us (19%)
  starting transfers between devices  9.66 us (18%)
  between operations  0.76 us (1%)
    all_to_all x2, blocking collectives, program(): recv = lax.all_to_all(pay, AXES, 0, 0, tiled=True)  22 us
    ppermute x8, waiting for transfers between devices, swap(): return lax.ppermute(x, 'light', [(i, i ^ k) for i in range(nl)])  10.2 us
    ppermute x8, starting transfers between devices, swap(): return lax.ppermute(x, 'light', [(i, i ^ k) for i in range(nl)])  6.23 us
    ppermute x1, starting transfers between devices, program(): direct = lax.ppermute(strip, AXES, pairs)  3.43 us
    pallas_call x1, Pallas kernels, program(): call(functools.partial(second_body, nl), (shape(4, *field), shape(nd, 1,...  3.4 us
    pallas_call x1, Pallas kernels, program(): call(functools.partial(cut_body, nl), tuple((shape(block_rows(lights, row...  1.8 us
    pallas_call x1, Pallas kernels, program(): call(functools.partial(first_body, nl), (shape(4, *field), shape(16, rows...  1.61 us
    ppermute x1, waiting for transfers between devices, program(): direct = lax.ppermute(strip, AXES, pairs)  1.39 us
  transfers between devices with their start and end apart: 9, of which 4 were waited for; matrix products, arithmetic and copies ran while one was open for 0% of the time, Pallas kernels for 7%

profile of v10, /device:TPU:0, one launch (start us, length us, event | category | flops | bytes accessed | tf_op | source)
XLA Modules:
  0.0 54.7 jit_solution(2312597703142477613)
XLA Ops:
  0.7 1.8 %shard_map.68 = (bf16[1056,128]{1,0:T(8,128)(2,1)S(1)}, bf16[1072,128]{1,0:T(8,128)(2,1)S(1)}, bf16[1056,128]{1,0:T(8,128)(2,1)S(1)}, bf16[672,128]{1,0:T(8,128)...) custom-call(bf16[8,128,512]{2,1,0:T(8,128)(2,1)} %obs_ref.1, s32[4,8]{1,0:T(4,128)} %bitcast.1), custom_call_target="tpu_custom_call" | custom-call | tf_op jit(solution)/shard_map/pallas_call | solution.py:564
  2.5 0.6 %collective-permute-start = (bf16[1072,128]{1,0:T(8,128)(2,1)S(1)}, bf16[1072,128]{1,0:T(8,128)(2,1)S(1)}, u32[]{:S(2)}, u32[]{:S(2)}) collective-permute-start(bf16[1072,128]{1,0:T(8,128)(2,1)S(1)} %get-tuple-element.30), channel_id=1, source_target_pairs={{0,8},{8,0},{16,24},{24,16},{1,9},{9,1},{17,25},{25,17},{2,10},{10... | collective-permute-start | bytes 823304 | tf_op jit(solution)/shard_map/ppermute | solution.py:560
  3.0 2.6 %collective-permute-start.2 = (bf16[1056,128]{1,0:T(8,128)(2,1)S(1)}, bf16[1056,128]{1,0:T(8,128)(2,1)S(1)}, u32[]{:S(2)}, u32[]{:S(2)}) collective-permute-start(bf16[1056,128]{1,0:T(8,128)(2,1)S(1)} %get-tuple-element.38), channel_id=1, source_target_pairs={{0,16},{8,24},{16,0},{24,8},{1,17},{9,25},{17,1},{25,9},{2,18},{10... | collective-permute-start | bytes 811016 | tf_op jit(solution)/shard_map/ppermute | solution.py:560
  5.6 0.0 collective-permute-start.3
  5.6 1.7 %collective-permute-start.4 = (bf16[384,128]{1,0:T(8,128)(2,1)S(1)}, bf16[384,128]{1,0:T(8,128)(2,1)S(1)}, u32[]{:S(2)}, u32[]{:S(2)}) collective-permute-start(bf16[384,128]{1,0:T(8,128)(2,1)S(1)} %get-tuple-element.42), channel_id=1, source_target_pairs={{0,24},{8,16},{16,8},{24,0},{1,25},{9,17},{17,9},{25,1},{2,26},{10... | collective-permute-start | bytes 294920 | tf_op jit(solution)/shard_map/ppermute | solution.py:560
  7.3 0.2 shard_map.69
  7.6 3.4 %collective-permute-start.1 = (f32[24,128]{1,0:T(8,128)S(1)}, f32[24,128]{1,0:T(8,128)S(1)}, u32[]{:S(2)}, u32[]{:S(2)}) collective-permute-start(f32[24,128]{1,0:T(8,128)S(1)} %get-tuple-element.34), channel_id=1, source_target_pairs={{0,1},{9,8},{16,17},{25,24},{1,2},{10,9},{17,18},{26,25},{2,3},{11... | collective-permute-start | bytes 36872 | tf_op jit(solution)/shard_map/ppermute | solution.py:588
  11.0 1.4 %collective-permute-done.1.strip_ref.direct_ref = f32[24,128]{1,0:T(8,128)S(1)} collective-permute-done((f32[24,128]{1,0:T(8,128)S(1)}, f32[24,128]{1,0:T(8,128)S(1)}, u32[]{:S(2)}, u32[]{:S(2)}) %collective-permute-start.1) | collective-permute-done | bytes 12320 | tf_op jit(solution)/shard_map/ppermute | solution.py:588
  12.4 0.5 collective-permute-start.5
  12.9 1.6 %shard_map.70 = (f32[4,128,128]{2,1,0:T(8,128)S(1)}, f32[16,128]{1,0:T(8,128)S(1)}, f32[7,128,128]{2,1,0:T(8,128)S(1)}, f32[16,5,8,128]{3,2,1,0:T(8,128)S(1)}, f32[16,128,128]{2,1,0:T(8,128)S(1)}) custom-call(f32[3,128,128]{2,1,0:T(8,128)S(1)} %get-tuple-element.32.tile_ref, f32[16,128]{1,0:T(8,128)S(1)} %get-tuple-element.33.sr_ref, ...), custom_call_target="tpu_custom_call" | custom-call | tf_op jit(solution)/shard_map/pallas_call | solution.py:595
  14.6 0.9 %shard_map.71 = (f32[7,128,128]{2,1,0:T(8,128)S(1)}, f32[8,5,8,128]{3,2,1,0:T(8,128)S(1)}, f32[8,128,128]{2,1,0:T(8,128)S(1)}) custom-call(f32[4,128,128]{2,1,0:T(8,128)S(1)} %get-tuple-element.36.ctx_ref, f32[7,128,128]{2,1,0:T(8,128)S(1)} %get-tuple-element.37.in_ref, bf16[1056,128]{1,0:T(8,128)(2,1)S(1)} %collective-permute-done.2.obs.rest_2_), custom_call_target="tpu_custom_call" | custom-call | tf_op jit(solution)/shard_map/pallas_call | solution.py:600
  15.5 0.7 %collective-permute-done.3.obs.rest_3_ = bf16[672,128]{1,0:T(8,128)(2,1)S(1)} collective-permute-done((bf16[672,128]{1,0:T(8,128)(2,1)S(1)}, bf16[672,128]{1,0:T(8,128)(2,1)S(1)}, u32[]{:S(2)}, u32[]{:S(2)}) %collective-permute-start.3) | collective-permute-done | bytes 172064 | tf_op jit(solution)/shard_map/ppermute | solution.py:560
  16.1 0.7 %shard_map.72 = (f32[7,128,128]{2,1,0:T(8,128)S(1)}, f32[8,5,8,128]{3,2,1,0:T(8,128)S(1)}, f32[5,128,128]{2,1,0:T(8,128)S(1)}) custom-call(f32[4,128,128]{2,1,0:T(8,128)S(1)} %get-tuple-element.36.ctx_ref, f32[7,128,128]{2,1,0:T(8,128)S(1)} %get-tuple-element.39.in_ref, bf16[672,128]{1,0:T(8,128)(2,1)S(1)} %collective-permute-done.3.obs.rest_3_), custom_call_target="tpu_custom_call" | custom-call | tf_op jit(solution)/shard_map/pallas_call | solution.py:601
  16.8 1.9 %collective-permute-done.5.relayed_ref = f32[24,128]{1,0:T(8,128)S(1)} collective-permute-done((f32[24,128]{1,0:T(8,128)S(1)}, f32[24,128]{1,0:T(8,128)S(1)}, u32[]{:S(2)}, u32[]{:S(2)}) %collective-permute-start.5) | collective-permute-done | bytes 12320 | tf_op jit(solution)/shard_map/ppermute | solution.py:560
  18.7 0.4 shard_map.73
  19.1 0.0 collective-permute-done.4.obs.rest_4_
  19.1 0.6 %shard_map.74 = (f32[2,128,128]{2,1,0:T(8,128)S(1)}, f32[8,128]{1,0:T(8,128)S(1)}, f32[32,4,128]{2,1,0:T(4,128)S(1)}, f32[3,128,128]{2,1,0:T(8,128)S(1)}) custom-call(f32[4,128,128]{2,1,0:T(8,128)S(1)} %get-tuple-element.36.ctx_ref, f32[7,128,128]{2,1,0:T(8,128)S(1)} %get-tuple-element.41.in_ref, bf16[384,128]{1,0:T(8,128)(2,1)S(1)} %collective-permute-done.4.obs.rest_4_, ...), custom_call_target="tpu_custom_call" | custom-call | tf_op jit(solution)/shard_map/pallas_call | solution.py:605
  19.8 13.2 %all_to_all.10.recv_ref = f32[32,4,128]{2,1,0:T(4,128)S(1)} all-to-all(f32[32,4,128]{2,1,0:T(4,128)S(1)} %get-tuple-element.46), channel_id=1, replica_groups=mesh['light'=4,'strip'=8] {'light','strip'}, dimensions={0} | all-to-all | bytes 131072 | tf_op jit(solution)/shard_map/all_to_all | solution.py:610
  33.0 3.4 %shard_map.75 = (f32[4,128,128]{2,1,0:T(8,128)S(1)}, f32[32,1,128]{2,1,0:T(1,128)S(1)}) custom-call(f32[32,4,128]{2,1,0:T(4,128)S(1)} %all_to_all.10.recv_ref, f32[2,128,128]{2,1,0:T(8,128)S(1)} %get-tuple-element.47.grad_ref, f32[8,128]{1,0:T(8,128)S(1)} %get-tuple-element.48.edge_ref, f32[3,128,128]{2,1,0:T(8,128)S(1)} %get-tuple-element.32.tile_ref, ...), custom_call_target="tpu_custom_call" | custom-call | tf_op jit(solution)/shard_map/pallas_call | solution.py:611
  36.4 0.8 %collective-permute-start.7 = (f32[4,128,128]{2,1,0:T(8,128)S(1)}, f32[4,128,128]{2,1,0:T(8,128)S(1)}, u32[]{:S(2)}, u32[]{:S(2)}) collective-permute-start(f32[4,128,128]{2,1,0:T(8,128)S(1)} %get-tuple-element.57.rest_0_), channel_id=1, source_target_pairs={{0,16},{8,24},{16,0},{24,8},{1,17},{9,25},{17,1},{25,9},{2,18},{10... | collective-permute-start | bytes 786440 | tf_op jit(solution)/shard_map/ppermute | solution.py:560
  37.1 7.6 %collective-permute-done.7.in_ref.rest_2_ = f32[4,128,128]{2,1,0:T(8,128)S(1)} collective-permute-done((f32[4,128,128]{2,1,0:T(8,128)S(1)}, f32[4,128,128]{2,1,0:T(8,128)S(1)}, u32[]{:S(2)}, u32[]{:S(2)}) %collective-permute-start.7) | collective-permute-done | bytes 262176 | tf_op jit(solution)/shard_map/ppermute | solution.py:560
  44.8 0.1 collective-permute-start.8
  44.9 8.8 %all_to_all.11.recv_ref = f32[32,1,128]{2,1,0:T(1,128)S(1)} all-to-all(f32[32,1,128]{2,1,0:T(1,128)S(1)} %get-tuple-element.56), channel_id=1, replica_groups=mesh['light'=4,'strip'=8] {'light','strip'}, dimensions={0} | all-to-all | bytes 32768 | tf_op jit(solution)/shard_map/all_to_all | solution.py:623
  53.7 1.0 %shard_map.77 = (f32[128,512]{1,0:T(8,128)}, f32[128,512]{1,0:T(8,128)}) custom-call(f32[32,1,128]{2,1,0:T(1,128)S(1)} %all_to_all.11.recv_ref, f32[4,128,128]{2,1,0:T(8,128)S(1)} %get-tuple-element.57.rest_0_, f32[4,128,128]{2,1,0:T(8,128)S(1)} %collective-permute-done.6.rest_1_, f32[4,128,128]{2,1,0:T(8,128)S(1)} %collective-permute-done.7.in_ref.rest_2_, ...), custom_call_target="tpu_custom_call" | custom-call | tf_op jit(solution)/shard_map/pallas_call | solution.py:626
  (12 shorter events, 0.0 us)
Async XLA Ops:
  0.6 6.7 %copy-start = (f32[128,512]{1,0:T(8,128)S(1)}, f32[128,512]{1,0:T(8,128)}, u32[]{:S(2)}) copy-start(f32[128,512]{1,0:T(8,128)} %depth_ref.1) | copy-start | bytes 786436
  0.6 6.7 %copy-start.1 = (f32[128,512]{1,0:T(8,128)S(1)}, f32[128,512]{1,0:T(8,128)}, u32[]{:S(2)}) copy-start(f32[128,512]{1,0:T(8,128)} %albedo_ref.1) | copy-start | bytes 786436
  0.7 6.7 %copy-start.2 = (s32[128,512]{1,0:T(8,128)S(1)}, s32[128,512]{1,0:T(8,128)}, u32[]{:S(2)}) copy-start(s32[128,512]{1,0:T(8,128)} %valid_ref.1) | copy-start | bytes 786436
  2.5 4.9 %collective-permute-start = (bf16[1072,128]{1,0:T(8,128)(2,1)S(1)}, bf16[1072,128]{1,0:T(8,128)(2,1)S(1)}, u32[]{:S(2)}, u32[]{:S(2)}) collective-permute-start(bf16[1072,128]{1,0:T(8,128)(2,1)S(1)} %get-tuple-element.30), channel_id=1, source_target_pairs={{0,8},{8,0},{16,24},{24,16},{1,9},{9,1},{17,25},{25,17},{2,10},{10... | collective-permute-start | bytes 823304 | tf_op jit(solution)/shard_map/ppermute | solution.py:560
  3.0 11.5 %collective-permute-start.2 = (bf16[1056,128]{1,0:T(8,128)(2,1)S(1)}, bf16[1056,128]{1,0:T(8,128)(2,1)S(1)}, u32[]{:S(2)}, u32[]{:S(2)}) collective-permute-start(bf16[1056,128]{1,0:T(8,128)(2,1)S(1)} %get-tuple-element.38), channel_id=1, source_target_pairs={{0,16},{8,24},{16,0},{24,8},{1,17},{9,25},{17,1},{25,9},{2,18},{10... | collective-permute-start | bytes 811016 | tf_op jit(solution)/shard_map/ppermute | solution.py:560
  5.6 10.6 %collective-permute-start.3 = (bf16[672,128]{1,0:T(8,128)(2,1)S(1)}, bf16[672,128]{1,0:T(8,128)(2,1)S(1)}, u32[]{:S(2)}, u32[]{:S(2)}) collective-permute-start(bf16[672,128]{1,0:T(8,128)(2,1)S(1)} %get-tuple-element.40), channel_id=1, source_target_pairs={{0,24},{8,16},{16,8},{24,0},{1,25},{9,17},{17,9},{25,1},{2,26},{10... | collective-permute-start | bytes 516104 | tf_op jit(solution)/shard_map/ppermute | solution.py:560
  5.6 13.5 %collective-permute-start.4 = (bf16[384,128]{1,0:T(8,128)(2,1)S(1)}, bf16[384,128]{1,0:T(8,128)(2,1)S(1)}, u32[]{:S(2)}, u32[]{:S(2)}) collective-permute-start(bf16[384,128]{1,0:T(8,128)(2,1)S(1)} %get-tuple-element.42), channel_id=1, source_target_pairs={{0,24},{8,16},{16,8},{24,0},{1,25},{9,17},{17,9},{25,1},{2,26},{10... | collective-permute-start | bytes 294920 | tf_op jit(solution)/shard_map/ppermute | solution.py:560
  7.6 4.8 %collective-permute-start.1 = (f32[24,128]{1,0:T(8,128)S(1)}, f32[24,128]{1,0:T(8,128)S(1)}, u32[]{:S(2)}, u32[]{:S(2)}) collective-permute-start(f32[24,128]{1,0:T(8,128)S(1)} %get-tuple-element.34), channel_id=1, source_target_pairs={{0,1},{9,8},{16,17},{25,24},{1,2},{10,9},{17,18},{26,25},{2,3},{11... | collective-permute-start | bytes 36872 | tf_op jit(solution)/shard_map/ppermute | solution.py:588
  12.4 6.3 %collective-permute-start.5 = (f32[24,128]{1,0:T(8,128)S(1)}, f32[24,128]{1,0:T(8,128)S(1)}, u32[]{:S(2)}, u32[]{:S(2)}) collective-permute-start(f32[24,128]{1,0:T(8,128)S(1)} %collective-permute-done.1.strip_ref.direct_ref), channel_id=1, source_target_pairs={{0,16},{8,24},{16,0},{24,8},{1,17},{9,25},{17,1},{25,9},{2,18},{10... | collective-permute-start | bytes 36872 | tf_op jit(solution)/shard_map/ppermute | solution.py:560
  36.4 8.4 %collective-permute-start.7 = (f32[4,128,128]{2,1,0:T(8,128)S(1)}, f32[4,128,128]{2,1,0:T(8,128)S(1)}, u32[]{:S(2)}, u32[]{:S(2)}) collective-permute-start(f32[4,128,128]{2,1,0:T(8,128)S(1)} %get-tuple-element.57.rest_0_), channel_id=1, source_target_pairs={{0,16},{8,24},{16,0},{24,8},{1,17},{9,25},{17,1},{25,9},{2,18},{10... | collective-permute-start | bytes 786440 | tf_op jit(solution)/shard_map/ppermute | solution.py:560
  37.1 16.6 %collective-permute-start.6 = (f32[4,128,128]{2,1,0:T(8,128)S(1)}, f32[4,128,128]{2,1,0:T(8,128)S(1)}, u32[]{:S(2)}, u32[]{:S(2)}) collective-permute-start(f32[4,128,128]{2,1,0:T(8,128)S(1)} %get-tuple-element.57.rest_0_), channel_id=1, source_target_pairs={{0,8},{8,0},{16,24},{24,16},{1,9},{9,1},{17,25},{25,17},{2,10},{10... | collective-permute-start | bytes 786440 | tf_op jit(solution)/shard_map/ppermute | solution.py:560
  44.8 8.9 %collective-permute-start.8 = (f32[4,128,128]{2,1,0:T(8,128)S(1)}, f32[4,128,128]{2,1,0:T(8,128)S(1)}, u32[]{:S(2)}, u32[]{:S(2)}) collective-permute-start(f32[4,128,128]{2,1,0:T(8,128)S(1)} %shard_map.76), channel_id=1, source_target_pairs={{0,8},{8,0},{16,24},{24,16},{1,9},{9,1},{17,25},{25,17},{2,10},{10... | collective-permute-start | bytes 786440 | tf_op jit(solution)/shard_map/ppermute | solution.py:560

commit v11 on v10

--- a/solution.py
+++ b/solution.py
@@ -45,7 +45,7 @@
 
 
 UNDER = 16
-LATE = 3
+LATE = 2
 
 
 def block_rows(lights, rows, k, nl):
@@ -107,7 +107,14 @@
     blocks[1][pl.ds(lights * rows + UNDER + 2 * lights, 2 * lights), :] = ends.astype(jnp.bfloat16)
 
 
-def join_body(nl, depth_ref, albedo_ref, valid_ref, block_ref, end_ref, tile_ref, sr_ref, out_ref):
+def join_body(
+    nl, depth_from, albedo_from, valid_from, block_ref, end_ref, tile_ref, sr_ref, out_ref, fields, valid_ref, sems
+):
+    depth_ref, albedo_ref = fields.at[0], fields.at[1]
+    copies = []
+    for source, target in ((depth_from, depth_ref), (albedo_from, albedo_ref), (valid_from, valid_ref)):
+        copies.append(pltpu.make_async_copy(source, target, sems.at[len(copies)]))
+        copies[-1].start()
     rows, w = tile_ref.shape[1:]
     n = end_ref.shape[0] // 2
     li = lax.axis_index("light")
@@ -118,6 +125,8 @@
     out_ref[2 * n :, :] = jnp.zeros((8, rows), F32)
     sr_ref[...] = jnp.zeros_like(sr_ref)
     lane = iota((rows, w), 1)
+    for copy in copies:
+        copy.wait()
 
     def columns(ref, q):
         return ref[:, pl.ds(pl.multiple_of(q * w, w), w)].astype(F32)
@@ -546,6 +555,10 @@
         albedo_ref[:, at] = parts[k][1] - STEP_ALBEDO * jnp.tanh(parts[k][3] * inv_albedo)
 
 
+def in_hbm(x):
+    return pltpu.with_memory_space_constraint(x, pltpu.HBM)
+
+
 def shape(*dims, dtype=F32):
     return jax.ShapeDtypeStruct(dims, dtype)
 
@@ -572,14 +585,21 @@
             pltpu.SemaphoreType.DMA((1,)),
         ],
         in_specs=[hbm] * 2,
-    )(*(pltpu.with_memory_space_constraint(x, pltpu.HBM) for x in (observations, light_table.T)))
+    )(in_hbm(observations), in_hbm(light_table.T))
     obs2 = swap(blocks[2], 2)
     obs3 = swap(blocks[3], 3)
     obs1 = swap(blocks[1], 1)
     obs0 = blocks[0]
     tile, sr, strip = call(
-        functools.partial(join_body, nl), (shape(3, *field), shape(16, rows), shape(2 * lights + 8, rows))
-    )(depth_start, albedo_start, valid_mask, obs1, end)
+        functools.partial(join_body, nl),
+        (shape(3, *field), shape(16, rows), shape(2 * lights + 8, rows)),
+        [
+            pltpu.VMEM((2, rows, cols), F32),
+            pltpu.VMEM((rows, cols), jnp.int32),
+            pltpu.SemaphoreType.DMA((3,)),
+        ],
+        in_specs=[hbm] * 3 + [pl.BlockSpec(memory_space=pltpu.VMEM)] * 2,
+    )(*(in_hbm(x) for x in (depth_start, albedo_start, valid_mask)), obs1, end)
     pairs = []
     for i in range(ns - 1):
         for l in range(nl):

time: 54.9 us -> 54.8 us (level)
  waiting for transfers between devices: 11.6 us -> 10.4 us
  Pallas kernels: 10.7 us -> 11.8 us
    ppermute x8, waiting for transfers between devices: 10.2 us -> 9 us  [swap(): return lax.ppermute(x, 'light', [(i, i ^ k) for i in range(nl)])]
    pallas_call x1, Pallas kernels: 0.22 us -> 1.36 us  [program(): call(functools.partial(join_body, nl), (shape(3, *field), shape(16, rows)...]
  transfers between devices with their start and end apart: 9 -> 9, of which waited for: 4 -> 4; matrix products, arithmetic and copies ran while one was open for 0% -> 0% of each run, Pallas kernels for 7% -> 9%
where the time goes in v11:
time: 54.8 us; the launch traced here: 54.6 us
  blocking collectives  22 us (40%)
  Pallas kernels  11.8 us (22%)
  waiting for transfers between devices  10.4 us (19%)
  starting transfers between devices  9.65 us (18%)
  between operations  0.72 us (1%)
    all_to_all x2, blocking collectives, program(): recv = lax.all_to_all(pay, AXES, 0, 0, tiled=True)  22 us
    ppermute x8, waiting for transfers between devices, swap(): return lax.ppermute(x, 'light', [(i, i ^ k) for i in range(nl)])  9 us
    ppermute x8, starting transfers between devices, swap(): return lax.ppermute(x, 'light', [(i, i ^ k) for i in range(nl)])  6.23 us
    ppermute x1, starting transfers between devices, program(): direct = lax.ppermute(strip, AXES, pairs)  3.42 us
    pallas_call x1, Pallas kernels, program(): call(functools.partial(second_body, nl), (shape(4, *field), shape(nd, 1,...  3.38 us
    pallas_call x1, Pallas kernels, program(): call(functools.partial(cut_body, nl), tuple((shape(block_rows(lights, row...  1.73 us
    pallas_call x1, Pallas kernels, program(): call(functools.partial(first_body, nl), (shape(4, *field), shape(16, rows...  1.59 us
    ppermute x1, waiting for transfers between devices, program(): direct = lax.ppermute(strip, AXES, pairs)  1.39 us
  transfers between devices with their start and end apart: 9, of which 4 were waited for; matrix products, arithmetic and copies ran while one was open for 0% of the time, Pallas kernels for 9%

profile of v11, /device:TPU:0, one launch (start us, length us, event | category | flops | bytes accessed | tf_op | source)
XLA Modules:
  0.0 54.6 jit_solution(18009361690600810340)
XLA Ops:
  0.6 1.7 %shard_map.68 = (bf16[1056,128]{1,0:T(8,128)(2,1)S(1)}, bf16[1072,128]{1,0:T(8,128)(2,1)S(1)}, bf16[1056,128]{1,0:T(8,128)(2,1)S(1)}, bf16[800,128]{1,0:T(8,128)...) custom-call(bf16[8,128,512]{2,1,0:T(8,128)(2,1)} %obs_ref.1, s32[4,8]{1,0:T(4,128)} %bitcast.1), custom_call_target="tpu_custom_call" | custom-call | tf_op jit(solution)/shard_map/pallas_call | solution.py:577
  2.4 0.6 %collective-permute-start = (bf16[1072,128]{1,0:T(8,128)(2,1)S(1)}, bf16[1072,128]{1,0:T(8,128)(2,1)S(1)}, u32[]{:S(2)}, u32[]{:S(2)}) collective-permute-start(bf16[1072,128]{1,0:T(8,128)(2,1)S(1)} %get-tuple-element.30), channel_id=1, source_target_pairs={{0,8},{8,0},{16,24},{24,16},{1,9},{9,1},{17,25},{25,17},{2,10},{10... | collective-permute-start | bytes 823304 | tf_op jit(solution)/shard_map/ppermute | solution.py:573
  2.9 2.6 %collective-permute-start.2 = (bf16[1056,128]{1,0:T(8,128)(2,1)S(1)}, bf16[1056,128]{1,0:T(8,128)(2,1)S(1)}, u32[]{:S(2)}, u32[]{:S(2)}) collective-permute-start(bf16[1056,128]{1,0:T(8,128)(2,1)S(1)} %get-tuple-element.38), channel_id=1, source_target_pairs={{0,16},{8,24},{16,0},{24,8},{1,17},{9,25},{17,1},{25,9},{2,18},{10... | collective-permute-start | bytes 811016 | tf_op jit(solution)/shard_map/ppermute | solution.py:573
  5.5 0.0 collective-permute-start.3
  5.5 1.7 %collective-permute-start.4 = (bf16[256,128]{1,0:T(8,128)(2,1)S(1)}, bf16[256,128]{1,0:T(8,128)(2,1)S(1)}, u32[]{:S(2)}, u32[]{:S(2)}) collective-permute-start(bf16[256,128]{1,0:T(8,128)(2,1)S(1)} %get-tuple-element.42), channel_id=1, source_target_pairs={{0,24},{8,16},{16,8},{24,0},{1,25},{9,17},{17,9},{25,1},{2,26},{10... | collective-permute-start | bytes 196616 | tf_op jit(solution)/shard_map/ppermute | solution.py:573
  7.2 0.0 collective-permute-done.block_ref.obs1.rest_1_
  7.2 1.4 %shard_map.69 = (f32[3,128,128]{2,1,0:T(8,128)S(1)}, f32[16,128]{1,0:T(8,128)S(1)}, f32[24,128]{1,0:T(8,128)S(1)}) custom-call(f32[128,512]{1,0:T(8,128)} %depth_from.1, f32[128,512]{1,0:T(8,128)} %albedo_from.1, s32[128,512]{1,0:T(8,128)} %valid_from.1, bf16[1072,128]{1,0:T(8,128)(2,1)S(1)} %collective-permute-done.block_ref.obs1.rest_1_, ...), custom_call_target="tpu_custom_call" | custom-call | tf_op jit(solution)/shard_map/pallas_call | solution.py:593
  8.6 3.4 %collective-permute-start.1 = (f32[24,128]{1,0:T(8,128)S(1)}, f32[24,128]{1,0:T(8,128)S(1)}, u32[]{:S(2)}, u32[]{:S(2)}) collective-permute-start(f32[24,128]{1,0:T(8,128)S(1)} %get-tuple-element.34), channel_id=1, source_target_pairs={{0,1},{9,8},{16,17},{25,24},{1,2},{10,9},{17,18},{26,25},{2,3},{11... | collective-permute-start | bytes 36872 | tf_op jit(solution)/shard_map/ppermute | solution.py:608
  12.0 1.4 %collective-permute-done.1.strip_ref.direct_ref = f32[24,128]{1,0:T(8,128)S(1)} collective-permute-done((f32[24,128]{1,0:T(8,128)S(1)}, f32[24,128]{1,0:T(8,128)S(1)}, u32[]{:S(2)}, u32[]{:S(2)}) %collective-permute-start.1) | collective-permute-done | bytes 12320 | tf_op jit(solution)/shard_map/ppermute | solution.py:608
  13.4 0.5 collective-permute-start.5
  14.0 1.6 %shard_map.70 = (f32[4,128,128]{2,1,0:T(8,128)S(1)}, f32[16,128]{1,0:T(8,128)S(1)}, f32[7,128,128]{2,1,0:T(8,128)S(1)}, f32[16,5,8,128]{3,2,1,0:T(8,128)S(1)}, f32[16,128,128]{2,1,0:T(8,128)S(1)}) custom-call(f32[3,128,128]{2,1,0:T(8,128)S(1)} %get-tuple-element.32.tile_ref, f32[16,128]{1,0:T(8,128)S(1)} %get-tuple-element.33.sr_ref, ...), custom_call_target="tpu_custom_call" | custom-call | tf_op jit(solution)/shard_map/pallas_call | solution.py:615
  15.6 0.9 %shard_map.71 = (f32[7,128,128]{2,1,0:T(8,128)S(1)}, f32[8,5,8,128]{3,2,1,0:T(8,128)S(1)}, f32[8,128,128]{2,1,0:T(8,128)S(1)}) custom-call(f32[4,128,128]{2,1,0:T(8,128)S(1)} %get-tuple-element.36.ctx_ref, f32[7,128,128]{2,1,0:T(8,128)S(1)} %get-tuple-element.37.in_ref, bf16[1056,128]{1,0:T(8,128)(2,1)S(1)} %collective-permute-done.2.obs.rest_2_), custom_call_target="tpu_custom_call" | custom-call | tf_op jit(solution)/shard_map/pallas_call | solution.py:620
  16.5 0.3 collective-permute-done.3.obs.rest_3_
  16.7 0.8 %shard_map.72 = (f32[7,128,128]{2,1,0:T(8,128)S(1)}, f32[8,5,8,128]{3,2,1,0:T(8,128)S(1)}, f32[6,128,128]{2,1,0:T(8,128)S(1)}) custom-call(f32[4,128,128]{2,1,0:T(8,128)S(1)} %get-tuple-element.36.ctx_ref, f32[7,128,128]{2,1,0:T(8,128)S(1)} %get-tuple-element.39.in_ref, bf16[800,128]{1,0:T(8,128)(2,1)S(1)} %collective-permute-done.3.obs.rest_3_), custom_call_target="tpu_custom_call" | custom-call | tf_op jit(solution)/shard_map/pallas_call | solution.py:621
  17.5 1.1 %collective-permute-done.5.relayed_ref = f32[24,128]{1,0:T(8,128)S(1)} collective-permute-done((f32[24,128]{1,0:T(8,128)S(1)}, f32[24,128]{1,0:T(8,128)S(1)}, u32[]{:S(2)}, u32[]{:S(2)}) %collective-permute-start.5) | collective-permute-done | bytes 12320 | tf_op jit(solution)/shard_map/ppermute | solution.py:573
  18.6 0.4 shard_map.73
  19.0 0.6 %shard_map.74 = (f32[2,128,128]{2,1,0:T(8,128)S(1)}, f32[8,128]{1,0:T(8,128)S(1)}, f32[32,4,128]{2,1,0:T(4,128)S(1)}, f32[2,128,128]{2,1,0:T(8,128)S(1)}) custom-call(f32[4,128,128]{2,1,0:T(8,128)S(1)} %get-tuple-element.36.ctx_ref, f32[7,128,128]{2,1,0:T(8,128)S(1)} %get-tuple-element.41.in_ref, bf16[256,128]{1,0:T(8,128)(2,1)S(1)} %collective-permute-done.4.obs.rest_4_, ...), custom_call_target="tpu_custom_call" | custom-call | tf_op jit(solution)/shard_map/pallas_call | solution.py:625
  19.6 13.2 %all_to_all.10.recv_ref = f32[32,4,128]{2,1,0:T(4,128)S(1)} all-to-all(f32[32,4,128]{2,1,0:T(4,128)S(1)} %get-tuple-element.46), channel_id=1, replica_groups=mesh['light'=4,'strip'=8] {'light','strip'}, dimensions={0} | all-to-all | bytes 131072 | tf_op jit(solution)/shard_map/all_to_all | solution.py:630
  32.8 3.4 %shard_map.75 = (f32[4,128,128]{2,1,0:T(8,128)S(1)}, f32[32,1,128]{2,1,0:T(1,128)S(1)}) custom-call(f32[32,4,128]{2,1,0:T(4,128)S(1)} %all_to_all.10.recv_ref, f32[2,128,128]{2,1,0:T(8,128)S(1)} %get-tuple-element.47.grad_ref, f32[8,128]{1,0:T(8,128)S(1)} %get-tuple-element.48.edge_ref, f32[3,128,128]{2,1,0:T(8,128)S(1)} %get-tuple-element.32.tile_ref, ...), custom_call_target="tpu_custom_call" | custom-call | tf_op jit(solution)/shard_map/pallas_call | solution.py:631
  36.2 0.8 %collective-permute-start.7 = (f32[4,128,128]{2,1,0:T(8,128)S(1)}, f32[4,128,128]{2,1,0:T(8,128)S(1)}, u32[]{:S(2)}, u32[]{:S(2)}) collective-permute-start(f32[4,128,128]{2,1,0:T(8,128)S(1)} %get-tuple-element.57.rest_0_), channel_id=1, source_target_pairs={{0,16},{8,24},{16,0},{24,8},{1,17},{9,25},{17,1},{25,9},{2,18},{10... | collective-permute-start | bytes 786440 | tf_op jit(solution)/shard_map/ppermute | solution.py:573
  37.0 7.6 %collective-permute-done.7.in_ref.rest_2_ = f32[4,128,128]{2,1,0:T(8,128)S(1)} collective-permute-done((f32[4,128,128]{2,1,0:T(8,128)S(1)}, f32[4,128,128]{2,1,0:T(8,128)S(1)}, u32[]{:S(2)}, u32[]{:S(2)}) %collective-permute-start.7) | collective-permute-done | bytes 262176 | tf_op jit(solution)/shard_map/ppermute | solution.py:573
  44.6 0.1 collective-permute-start.8
  44.7 8.8 %all_to_all.11.recv_ref = f32[32,1,128]{2,1,0:T(1,128)S(1)} all-to-all(f32[32,1,128]{2,1,0:T(1,128)S(1)} %get-tuple-element.56), channel_id=1, replica_groups=mesh['light'=4,'strip'=8] {'light','strip'}, dimensions={0} | all-to-all | bytes 32768 | tf_op jit(solution)/shard_map/all_to_all | solution.py:643
  53.5 1.0 %shard_map.77 = (f32[128,512]{1,0:T(8,128)}, f32[128,512]{1,0:T(8,128)}) custom-call(f32[32,1,128]{2,1,0:T(1,128)S(1)} %all_to_all.11.recv_ref, f32[4,128,128]{2,1,0:T(8,128)S(1)} %get-tuple-element.57.rest_0_, f32[4,128,128]{2,1,0:T(8,128)S(1)} %collective-permute-done.6.rest_1_, f32[4,128,128]{2,1,0:T(8,128)S(1)} %collective-permute-done.7.in_ref.rest_2_, ...), custom_call_target="tpu_custom_call" | custom-call | tf_op jit(solution)/shard_map/pallas_call | solution.py:646
  (6 shorter events, 0.0 us)
Async XLA Ops:
  2.4 4.9 %collective-permute-start = (bf16[1072,128]{1,0:T(8,128)(2,1)S(1)}, bf16[1072,128]{1,0:T(8,128)(2,1)S(1)}, u32[]{:S(2)}, u32[]{:S(2)}) collective-permute-start(bf16[1072,128]{1,0:T(8,128)(2,1)S(1)} %get-tuple-element.30), channel_id=1, source_target_pairs={{0,8},{8,0},{16,24},{24,16},{1,9},{9,1},{17,25},{25,17},{2,10},{10... | collective-permute-start | bytes 823304 | tf_op jit(solution)/shard_map/ppermute | solution.py:573
  2.9 12.6 %collective-permute-start.2 = (bf16[1056,128]{1,0:T(8,128)(2,1)S(1)}, bf16[1056,128]{1,0:T(8,128)(2,1)S(1)}, u32[]{:S(2)}, u32[]{:S(2)}) collective-permute-start(bf16[1056,128]{1,0:T(8,128)(2,1)S(1)} %get-tuple-element.38), channel_id=1, source_target_pairs={{0,16},{8,24},{16,0},{24,8},{1,17},{9,25},{17,1},{25,9},{2,18},{10... | collective-permute-start | bytes 811016 | tf_op jit(solution)/shard_map/ppermute | solution.py:573
  5.5 11.3 %collective-permute-start.3 = (bf16[800,128]{1,0:T(8,128)(2,1)S(1)}, bf16[800,128]{1,0:T(8,128)(2,1)S(1)}, u32[]{:S(2)}, u32[]{:S(2)}) collective-permute-start(bf16[800,128]{1,0:T(8,128)(2,1)S(1)} %get-tuple-element.40), channel_id=1, source_target_pairs={{0,24},{8,16},{16,8},{24,0},{1,25},{9,17},{17,9},{25,1},{2,26},{10... | collective-permute-start | bytes 614408 | tf_op jit(solution)/shard_map/ppermute | solution.py:573
  5.5 13.5 %collective-permute-start.4 = (bf16[256,128]{1,0:T(8,128)(2,1)S(1)}, bf16[256,128]{1,0:T(8,128)(2,1)S(1)}, u32[]{:S(2)}, u32[]{:S(2)}) collective-permute-start(bf16[256,128]{1,0:T(8,128)(2,1)S(1)} %get-tuple-element.42), channel_id=1, source_target_pairs={{0,24},{8,16},{16,8},{24,0},{1,25},{9,17},{17,9},{25,1},{2,26},{10... | collective-permute-start | bytes 196616 | tf_op jit(solution)/shard_map/ppermute | solution.py:573
  8.6 4.8 %collective-permute-start.1 = (f32[24,128]{1,0:T(8,128)S(1)}, f32[24,128]{1,0:T(8,128)S(1)}, u32[]{:S(2)}, u32[]{:S(2)}) collective-permute-start(f32[24,128]{1,0:T(8,128)S(1)} %get-tuple-element.34), channel_id=1, source_target_pairs={{0,1},{9,8},{16,17},{25,24},{1,2},{10,9},{17,18},{26,25},{2,3},{11... | collective-permute-start | bytes 36872 | tf_op jit(solution)/shard_map/ppermute | solution.py:608
  13.4 5.2 %collective-permute-start.5 = (f32[24,128]{1,0:T(8,128)S(1)}, f32[24,128]{1,0:T(8,128)S(1)}, u32[]{:S(2)}, u32[]{:S(2)}) collective-permute-start(f32[24,128]{1,0:T(8,128)S(1)} %collective-permute-done.1.strip_ref.direct_ref), channel_id=1, source_target_pairs={{0,16},{8,24},{16,0},{24,8},{1,17},{9,25},{17,1},{25,9},{2,18},{10... | collective-permute-start | bytes 36872 | tf_op jit(solution)/shard_map/ppermute | solution.py:573
  36.2 8.4 %collective-permute-start.7 = (f32[4,128,128]{2,1,0:T(8,128)S(1)}, f32[4,128,128]{2,1,0:T(8,128)S(1)}, u32[]{:S(2)}, u32[]{:S(2)}) collective-permute-start(f32[4,128,128]{2,1,0:T(8,128)S(1)} %get-tuple-element.57.rest_0_), channel_id=1, source_target_pairs={{0,16},{8,24},{16,0},{24,8},{1,17},{9,25},{17,1},{25,9},{2,18},{10... | collective-permute-start | bytes 786440 | tf_op jit(solution)/shard_map/ppermute | solution.py:573
  37.0 16.6 %collective-permute-start.6 = (f32[4,128,128]{2,1,0:T(8,128)S(1)}, f32[4,128,128]{2,1,0:T(8,128)S(1)}, u32[]{:S(2)}, u32[]{:S(2)}) collective-permute-start(f32[4,128,128]{2,1,0:T(8,128)S(1)} %get-tuple-element.57.rest_0_), channel_id=1, source_target_pairs={{0,8},{8,0},{16,24},{24,16},{1,9},{9,1},{17,25},{25,17},{2,10},{10... | collective-permute-start | bytes 786440 | tf_op jit(solution)/shard_map/ppermute | solution.py:573
  44.6 8.9 %collective-permute-start.8 = (f32[4,128,128]{2,1,0:T(8,128)S(1)}, f32[4,128,128]{2,1,0:T(8,128)S(1)}, u32[]{:S(2)}, u32[]{:S(2)}) collective-permute-start(f32[4,128,128]{2,1,0:T(8,128)S(1)} %shard_map.76), channel_id=1, source_target_pairs={{0,8},{8,0},{16,24},{24,16},{1,9},{9,1},{17,25},{25,17},{2,10},{10... | collective-permute-start | bytes 786440 | tf_op jit(solution)/shard_map/ppermute | solution.py:573
